TPU v7x, 256 devices: a whole 4x4x8 slice. The times are simulated.
256 devices in a mesh: row: 16 (over z_hi, x), col: 16 (over z_lo, y, core).
Axes of the slice: x: 4, y: 4, z: 8 (z_hi: 4, z_lo: 2; z = z_hi * 2 + z_lo), core: 2. Of those that a mesh axis runs over, the one named last changes fastest.
Arguments:
- signal: bfloat16 [32768, 2048], P('row', 'col'), may hold values from -40 to 40
- norm_gain: float32 [2048], replicated, may hold values from 0.5 to 2
- qkv_weight: bfloat16 [2048, 6144], P('row', 'col'), may hold values from -4 to 4
- out_weight: bfloat16 [2048, 2048], P('row', 'col'), may hold values from -1 to 1
Outputs:
- layer_out: bfloat16 [32768, 2048], P('row', 'col')
All inputs are finite; a program needn't handle non-finite values.
Results may differ from a plain program's by a relative error of at most 0.006.
Values may be sent and summed in bfloat16 or wider, within the bound.
No kernel may reach another device: no remote copies, remote signals or barrier semaphores. Data moves between devices by JAX's collectives and lax.ppermute only.
A program may use at most 64 MiB of HBM per device.

v0:
```python
import math

import jax
import jax.numpy as jnp
from jax import lax
from jax.experimental import pallas as pl
from jax.experimental.pallas import tpu as pltpu
from jax.sharding import PartitionSpec as P


HS = 128
COLS = 1024
EPSILON = 1e-05
NEGATIVE = -1e30
SCALE2 = math.log2(math.e) / math.sqrt(HS)
TILE = 256
G_COLS = 16
STAT_ROWS = 8

BF16 = jnp.bfloat16
F32 = jnp.float32
NT = (((1,), (1,)), ((), ()))


def _col(z, y, c):
    return (z % 2) * 8 + (y % 4) * 2 + c


def _over_col(x, to):
    pairs = [(_col(z, y, c), to(z, y, c)) for z in range(2) for y in range(4) for c in range(2)]
    return lax.ppermute(x, "col", pairs)


def _over_row(x, to):
    pairs = [(z * 4 + h, to(z, h)) for z in range(4) for h in range(4)]
    return lax.ppermute(x, "row", pairs)


def y_up(x):
    return _over_col(x, lambda z, y, c: _col(z, y + 1, c))


def y_down(x):
    return _over_col(x, lambda z, y, c: _col(z, y + 3, c))


def z_swap(x):
    return _over_col(x, lambda z, y, c: _col(z + 1, y, c))


def core_swap(x):
    return _over_col(x, lambda z, y, c: _col(z, y, 1 - c))


def zh_shift(x, d):
    return _over_row(x, lambda z, h: ((z + d) % 4) * 4 + h)


def x_shift(x, d):
    return _over_row(x, lambda z, h: z * 4 + (h + d) % 4)


def gather_chips(x):
    a = y_up(x)
    b = y_down(x)
    p = z_swap(x)
    left = a[:, :HS]
    fl = y_up(left)
    fr = y_down(b[:, HS:])
    pa = y_up(p)
    pb = y_down(p)
    gl = z_swap(fl)
    gr = z_swap(fr)
    return (x, b, fl, fr, a, p, pb, gl, gr, pa)


def over_z_hi(w):
    return jnp.stack([w] + [zh_shift(w, d) for d in (1, 2, 3)])


def over_x(z):
    return (z, *(x_shift(z, d) for d in (1, 2, 3)))


def _weights_kernel(place, *refs):
    out = refs[-1]
    sides = len(refs) // 4
    width = out.shape[1] // sides
    zl, y, zh, x = place[0], place[1], place[2], place[3]
    for dx in range(4):
        for dz in range(4):
            block = lax.rem(zh + 4 - dz, 4) * 4 + lax.rem(x + 4 - dx, 4)
            chip, half = block // 2, lax.rem(block, 2)
            piece = lax.rem(chip // 4 + zl, 2) * 4 + lax.rem(lax.rem(chip, 4) + 4 - y, 4)
            at = pl.multiple_of(piece * 256 + half * 128, 128)
            for side in range(sides):
                out[pl.ds(at, 128), side * width : (side + 1) * width] = refs[4 * side + dx][dz]


def _qkv_kernel(place, gain_ref, *refs):
    pieces, (w_ref, out_ref, even_ref, odd_ref) = refs[:10], refs[10:]
    zl, y, core = place[0], place[1], place[4]
    gains = []
    for i in range(8):
        j = lax.rem(zl + i // 4, 2) * 4 + lax.rem(y + i, 4)
        gains.append(gain_ref[pl.ds(j, 1), :])
    gain = jnp.concatenate(gains, axis=1)
    wide = 2048
    chunks = []
    lane = 0
    for ref in pieces:
        for k in range(ref.shape[1] // HS):
            chunks.append((ref, k * HS, lane))
            lane += HS

    def rows_of(tile):
        return pl.ds(pl.multiple_of(tile * TILE, TILE), TILE)

    def mean_of(tile):
        total = jnp.zeros((TILE, HS), F32)
        for ref, k, _ in chunks:
            total += ref[rows_of(tile), pl.ds(k, HS)].astype(F32)
        return jnp.sum(total, axis=1, keepdims=True) * (1.0 / wide)

    def rstd_of(tile, mean):
        square = jnp.zeros((TILE, HS), F32)
        for ref, k, _ in chunks:
            v = ref[rows_of(tile), pl.ds(k, HS)].astype(F32) - mean
            square += v * v
        return lax.rsqrt(jnp.sum(square, axis=1, keepdims=True) * (1.0 / wide) + EPSILON)

    def norm(tile, mean, rstd, to_ref):
        for ref, k, at in chunks:
            v = ref[rows_of(tile), pl.ds(k, HS)].astype(F32) - mean
            to_ref[:, pl.ds(at, HS)] = (v * rstd * gain[:, at : at + HS]).astype(BF16)

    def project(tile, from_ref, part):
        lanes = pl.ds(part * HS * 2, HS * 2)
        qkv = jnp.dot(from_ref[...], w_ref[:, lanes], preferred_element_type=F32).astype(BF16)
        blocks = pl.ds(tile * (TILE // 64), TILE // 64)
        for k in range(2):
            n = 2 * part + k
            slot = core if n < 3 else 1 - core
            v = qkv[:, k * HS : (k + 1) * HS].reshape(TILE // 64, 64, HS)
            out_ref[blocks, slot, :, (n % 3) * HS : (n % 3 + 1) * HS] = v

    def both(tile, from_ref, later, to_ref):
        mean = mean_of(later)
        project(tile, from_ref, 0)
        rstd = rstd_of(later, mean)
        project(tile, from_ref, 1)
        norm(later, mean, rstd, to_ref)
        project(tile, from_ref, 2)

    count = COLS // TILE
    mean = mean_of(0)
    norm(0, mean, rstd_of(0, mean), even_ref)

    def step(i, carry):
        both(2 * i, even_ref, 2 * i + 1, odd_ref)
        both(2 * i + 1, odd_ref, jnp.minimum(2 * i + 2, count - 1), even_ref)
        return carry

    lax.fori_loop(0, count // 2, step, 0)


def _out_kernel(place, x_ref, *refs):
    pieces, (w_ref, own_ref, other_ref) = refs[:10], refs[10:]
    core = place[4]

    for tile in range(COLS // TILE):
        at = tile * TILE
        v = jnp.concatenate([ref[pl.ds(at, TILE), :] for ref in pieces], axis=1)
        branch = jnp.dot(v, w_ref[...], preferred_element_type=F32)
        left = x_ref[pl.ds(at, TILE), pl.ds(0, HS)].astype(F32)
        right = x_ref[pl.ds(at, TILE), pl.ds(HS, HS)].astype(F32)
        own = jnp.where(core == 0, left, right) + branch[:, :HS]
        other = jnp.where(core == 0, right, left) + branch[:, HS:]
        own_ref[pl.ds(pl.multiple_of(core * COLS + at, TILE), TILE), :] = own.astype(BF16)
        other_ref[pl.ds(at, TILE), :] = other.astype(BF16)


def _row_kernel(head, qkv_ref, out_ref, lse_ref):
    diagonal = lax.broadcasted_iota(jnp.int32, (TILE, TILE), 0) >= lax.broadcasted_iota(
        jnp.int32, (TILE, TILE), 1
    )
    n = TILE // 64
    lane = lax.broadcasted_iota(jnp.int32, (64, HS), 1)
    packed = jnp.zeros((64, HS), F32)

    def part(lo, hi, k):
        v = qkv_ref[lo * n : hi * n, head, :, k * HS : (k + 1) * HS]
        return v.reshape((hi - lo) * TILE, HS)

    for tile in range(COLS // TILE):
        q = part(tile, tile + 1, 0)
        last = lax.dot_general(q, part(tile, tile + 1, 1), NT, preferred_element_type=F32)
        last = jnp.where(diagonal, last, NEGATIVE)
        top = jnp.max(last, axis=1, keepdims=True)
        if tile:
            before = lax.dot_general(q, part(0, tile, 1), NT, preferred_element_type=F32)
            top = jnp.maximum(top, jnp.max(before, axis=1, keepdims=True))
        w = jnp.exp2((last - top) * SCALE2)
        total = jnp.sum(w, axis=1, keepdims=True)
        acc = jnp.dot(w.astype(BF16), part(tile, tile + 1, 2), preferred_element_type=F32)
        if tile:
            w = jnp.exp2((before - top) * SCALE2)
            total += jnp.sum(w, axis=1, keepdims=True)
            acc += jnp.dot(w.astype(BF16), part(0, tile, 2), preferred_element_type=F32)
        out_ref[tile * TILE : (tile + 1) * TILE, :] = acc / total
        lse = top * SCALE2 + jnp.log2(total)
        for k in range(n):
            here = lane == 2 * (tile * n + k) + head
            packed = jnp.where(here, lse[k * 64 : (k + 1) * 64], packed)
    lse_ref[...] = packed


def _column_kernel(z_ref, out_ref):
    t = 32 * G_COLS
    i = lax.broadcasted_iota(jnp.int32, (t, t), 0)
    j = lax.broadcasted_iota(jnp.int32, (t, t), 1)
    valid = (lax.rem(i, G_COLS) == lax.rem(j, G_COLS)) & (i > j)
    bias = jnp.where(valid, 0.0, NEGATIVE)
    token = lax.broadcasted_iota(jnp.int32, (t, 1), 0)
    lane = lax.broadcasted_iota(jnp.int32, (t, HS), 1) - lax.rem(token, G_COLS)
    dest = lax.broadcasted_iota(jnp.int32, (32 * STAT_ROWS, t), 0)
    source = lax.broadcasted_iota(jnp.int32, (32 * STAT_ROWS, t), 1) // G_COLS
    picks = [(dest == source * STAT_ROWS + m).astype(F32).astype(BF16) for m in range(3)]

    spread = jnp.zeros((t, HS), F32)
    for g in range(64 // G_COLS):
        at = g * G_COLS
        z = z_ref[:, at : at + G_COLS, :].reshape(t, 3 * HS)
        s = lax.dot_general(z[:, :HS], z[:, HS : 2 * HS], NT, preferred_element_type=F32) + bias
        top = jnp.max(s, axis=1, keepdims=True)
        w = jnp.exp2((s - top) * SCALE2)
        total = jnp.sum(w, axis=1, keepdims=True)
        acc = jnp.dot(w.astype(BF16), z[:, 2 * HS :], preferred_element_type=F32)
        out_ref[:, at : at + G_COLS, :] = (acc / total).astype(BF16).reshape(32, G_COLS, HS)
        lse = jnp.where(token >= G_COLS, top * SCALE2 + jnp.log2(total), NEGATIVE)
        spread = jnp.where(lane == at, lse, spread)
    stats = jnp.zeros((32 * STAT_ROWS, HS), F32)
    for pick in picks:
        part = spread.astype(BF16)
        spread = spread - part.astype(F32)
        stats += jnp.dot(pick, part, preferred_element_type=F32)
    out_ref[:, 64 : 64 + STAT_ROWS, :] = stats.astype(BF16).reshape(32, STAT_ROWS, HS)


def _merge_kernel(row0_ref, lse0_ref, row1_ref, lse1_ref, col_ref, out_ref):
    stats = col_ref[:, :, 64:, :].reshape(32 * STAT_ROWS, HS)
    source = lax.broadcasted_iota(jnp.int32, (HS, 32 * STAT_ROWS), 1)
    entry = lax.broadcasted_iota(jnp.int32, (HS, 32 * STAT_ROWS), 0)
    picks = [(source == entry * STAT_ROWS + m).astype(F32).astype(BF16) for m in range(3)]
    parts = [jnp.dot(pick, stats, preferred_element_type=F32) for pick in picks]
    cl = (parts[0] + parts[1] + parts[2]).T[:64]
    rl = lse0_ref[...] + lse1_ref[...]
    top = jnp.maximum(cl, rl)
    rf = jnp.exp2(rl - top)
    cf = jnp.exp2(cl - top)
    share = 1.0 / (rf + cf)
    rf = rf * share
    cf = cf * share
    for block in range(16):
        rows = slice(block * 64, (block + 1) * 64)
        for head, row_ref in enumerate((row0_ref, row1_ref)):
            n = 2 * block + head
            o = rf[:, n : n + 1] * row_ref[rows, :] + cf[:, n : n + 1] * col_ref[block, head, :64, :].astype(F32)
            out_ref[rows, head * HS : (head + 1) * HS] = o.astype(BF16)


def _call(kernel, out, *args, scalars=0, flops=0, scratch=(), mib=24):
    vmem = pl.BlockSpec(memory_space=pltpu.VMEM)
    smem = pl.BlockSpec(memory_space=pltpu.SMEM)
    cost = pl.CostEstimate(flops=flops, transcendentals=0, bytes_accessed=1 << 20) if flops else None
    return pl.pallas_call(
        kernel,
        out_shape=out,
        in_specs=[smem] * scalars + [vmem] * (len(args) - scalars),
        out_specs=jax.tree.map(lambda _: vmem, out),
        cost_estimate=cost,
        scratch_shapes=scratch,
        compiler_params=pltpu.CompilerParams(vmem_limit_bytes=mib << 20),
    )(*args)


CHIP_GROUPS = [[r * 16 + 2 * j + k for r in range(16) for k in range(2)] for j in range(8)]


def exchange_columns(x):
    return lax.all_to_all(
        x, ("row", "col"), split_axis=0, concat_axis=0, axis_index_groups=CHIP_GROUPS, tiled=True
    )


def per_device(signal, norm_gain, qkv_weight, out_weight):
    shape = jax.ShapeDtypeStruct
    r = lax.axis_index("row")
    c = lax.axis_index("col")
    core = lax.rem(c, 2)
    place = jnp.stack([lax.div(c, 8), lax.rem(lax.div(c, 2), 4), lax.div(r, 4), lax.rem(r, 4), core])

    mine = lax.dynamic_slice_in_dim(signal, core * COLS, COLS, 0)
    theirs = core_swap(lax.dynamic_slice_in_dim(signal, (1 - core) * COLS, COLS, 0))
    x = jnp.where(
        core == 0, jnp.concatenate([mine, theirs], axis=1), jnp.concatenate([theirs, mine], axis=1)
    )
    weights = jnp.concatenate([qkv_weight, out_weight], axis=1)
    pieces = gather_chips(x)
    weights = over_z_hi(weights)
    own = over_x(weights[..., : 3 * HS])
    other = (core_swap(t) for t in own)
    w = _call(_weights_kernel, shape((2048, 6 * HS), BF16), place, *own, *other, scalars=1)
    qkv = _call(
        _qkv_kernel,
        shape((16, 2, 64, 3 * HS), BF16),
        place,
        norm_gain.reshape(8, 256),
        *pieces,
        w,
        scalars=1,
        scratch=[pltpu.VMEM((TILE, 2048), BF16)] * 2,
    )
    by_column = exchange_columns(qkv.reshape(32, 64, 3 * HS))
    weights, qkv = lax.optimization_barrier((weights[..., 3 * HS :], qkv))
    w = _call(_weights_kernel, shape((2048, HS), BF16), place, *over_x(weights), scalars=1)
    w = jnp.concatenate([w, core_swap(w)], axis=1)
    row = []
    for head in range(2):
        row += _call(
            lambda *refs, head=head: _row_kernel(head, *refs),
            (shape((COLS, HS), F32), shape((64, HS), F32)),
            qkv,
            flops=1 << 33,
        )
    by_column, w, first = lax.optimization_barrier((by_column, w, tuple(row[:2])))
    col_out = _call(_column_kernel, shape((32, 64 + STAT_ROWS, HS), BF16), by_column)
    col_out = exchange_columns(col_out).reshape(16, 2, 64 + STAT_ROWS, HS)
    att = _call(_merge_kernel, shape((COLS, 2 * HS), BF16), *first, *row[2:], col_out)
    out_own, out_other = _call(
        _out_kernel, (shape((2 * COLS, HS), BF16), shape((COLS, HS), BF16)), place, x, *gather_chips(att), w, scalars=1
    )
    return lax.dynamic_update_slice_in_dim(out_own, core_swap(out_other), (1 - core) * COLS, 0)


def solution(mesh):
    return jax.shard_map(
        per_device,
        mesh=mesh,
        in_specs=(P("row", "col"), P(), P("row", "col"), P("row", "col")),
        out_specs=P("row", "col"),
        check_vma=False,
    )
```

profile of v0, /device:TPU:1, one launch (start us, length us, event | category | flops | bytes accessed | tf_op | source)
XLA Modules:
  0.0 218.9 jit_solution(17859210670055110248)
XLA Ops:
  1.1 3.3 %collective-permute-start = (bf16[1024,128]{1,0:T(8,128)(2,1)S(1)}, bf16[1024,128]{1,0:T(8,128)(2,1)S(1)}, u32[]{:S(2)}, u32[]{:S(2)}) collective-permute-start(bf16[1024,128]{1,0:T(8,128)(2,1)S(1)} %get-tuple-element.30), channel_id=1, source_target_pairs={{0,1},{1,0},{2,3},{3,2},{4,5},{5,4},{6,7},{7,6},{8,9},{9,8},{10,11... | collective-permute-start | bytes 786440 | tf_op jit(solution)/shard_map/ppermute | solution.py:31
  6.0 4.4 %collective-permute-start.12 = (bf16[128,512]{1,0:T(8,128)(2,1)S(1)}, bf16[128,512]{1,0:T(8,128)(2,1)S(1)}, u32[]{:S(2)}, u32[]{:S(2)}) collective-permute-start(bf16[128,512]{1,0:T(8,128)(2,1)S(1)} %constant_dynamic-update-slice_fusion), channel_id=1, source_target_pairs={{0,192},{16,208},{32,224},{48,240},{64,0},{80,16},{96,32},{112,48}... | collective-permute-start | bytes 393224 | tf_op jit(solution)/shard_map/ppermute | solution.py:36
  11.4 2.3 %collective-permute-start.10 = (bf16[128,512]{1,0:T(8,128)(2,1)S(1)}, bf16[128,512]{1,0:T(8,128)(2,1)S(1)}, u32[]{:S(2)}, u32[]{:S(2)}) collective-permute-start(bf16[128,512]{1,0:T(8,128)(2,1)S(1)} %constant_dynamic-update-slice_fusion), channel_id=1, source_target_pairs={{0,64},{16,80},{32,96},{48,112},{64,128},{80,144},{96,160},{112,17... | collective-permute-start | bytes 393224 | tf_op jit(solution)/shard_map/ppermute | solution.py:36
  15.3 7.2 %collective-permute-done.11 = bf16[128,512]{1,0:T(8,128)(2,1)S(1)} collective-permute-done((bf16[128,512]{1,0:T(8,128)(2,1)S(1)}, bf16[128,512]{1,0:T(8,128)(2,1)S(1)}, u32[]{:S(2)}, u32[]{:S(2)}) %collective-permute-start.11) | collective-permute-done | bytes 131104 | tf_op jit(solution)/shard_map/ppermute | solution.py:36
  23.2 2.3 %collective-permute-start.15 = (bf16[4,128,384]{2,1,0:T(8,128)(2,1)S(1)}, bf16[4,128,384]{2,1,0:T(8,128)(2,1)S(1)}, u32[]{:S(2)}, u32[]{:S(2)}) collective-permute-start(bf16[4,128,384]{2,1,0:T(8,128)(2,1)S(1)} %slice.26.refs_0_), channel_id=1, source_target_pairs={{0,48},{16,0},{32,16},{48,32},{64,112},{80,64},{96,80},{112,96},{1... | collective-permute-start | bytes 1179656 | tf_op jit(solution)/shard_map/ppermute | solution.py:36
  25.5 2.7 %collective-permute-start.1 = (bf16[1024,256]{1,0:T(8,128)(2,1)S(1)}, bf16[1024,256]{1,0:T(8,128)(2,1)S(1)}, u32[]{:S(2)}, u32[]{:S(2)}) collective-permute-start(bf16[1024,256]{1,0:T(8,128)(2,1)S(1)} %maximum_select_fusion.refs_0_.x_ref), channel_id=1, source_target_pairs={{0,6},{1,7},{2,0},{3,1},{4,2},{5,3},{6,4},{7,5},{8,14},{9,15},{10,... | collective-permute-start | bytes 1572872 | tf_op jit(solution)/shard_map/ppermute | solution.py:31
  28.7 2.7 %collective-permute-start.5 = (bf16[1024,256]{1,0:T(8,128)(2,1)S(1)}, bf16[1024,256]{1,0:T(8,128)(2,1)S(1)}, u32[]{:S(2)}, u32[]{:S(2)}) collective-permute-start(bf16[1024,256]{1,0:T(8,128)(2,1)S(1)} %maximum_select_fusion.refs_0_.x_ref), channel_id=1, source_target_pairs={{0,8},{1,9},{2,10},{3,11},{4,12},{5,13},{6,14},{7,15},{8,0},{9,1},... | collective-permute-start | bytes 1572872 | tf_op jit(solution)/shard_map/ppermute | solution.py:31
  32.7 10.6 %collective-permute-start.16 = (bf16[4,128,384]{2,1,0:T(8,128)(2,1)S(1)}, bf16[4,128,384]{2,1,0:T(8,128)(2,1)S(1)}, u32[]{:S(2)}, u32[]{:S(2)}) collective-permute-start(bf16[4,128,384]{2,1,0:T(8,128)(2,1)S(1)} %slice.26.refs_0_), channel_id=1, source_target_pairs={{0,1},{1,0},{2,3},{3,2},{4,5},{5,4},{6,7},{7,6},{8,9},{9,8},{10,11... | collective-permute-start | bytes 1179656 | tf_op jit(solution)/shard_map/ppermute | solution.py:31
  43.3 2.1 collective-permute-start.19
  48.9 7.3 %collective-permute-done.13.refs_1_ = bf16[4,128,384]{2,1,0:T(8,128)(2,1)} collective-permute-done((bf16[4,128,384]{2,1,0:T(8,128)(2,1)S(1)}, bf16[4,128,384]{2,1,0:T(8,128)(2,1)}, u32[]{:S(2)}, u32[]{:S(2)}) %collective-permute-start.13) | collective-permute-done | bytes 393248 | tf_op jit(solution)/shard_map/ppermute | solution.py:36
  56.2 2.7 %collective-permute-start.6 = (bf16[1024,256]{1,0:T(8,128)(2,1)S(1)}, bf16[1024,256]{1,0:T(8,128)(2,1)S(1)}, u32[]{:S(2)}, u32[]{:S(2)}) collective-permute-start(bf16[1024,256]{1,0:T(8,128)(2,1)S(1)} %collective-permute-done.5.refs_5_), channel_id=1, source_target_pairs={{0,6},{1,7},{2,0},{3,1},{4,2},{5,3},{6,4},{7,5},{8,14},{9,15},{10,... | collective-permute-start | bytes 1572872 | tf_op jit(solution)/shard_map/ppermute | solution.py:31
  62.1 2.7 %collective-permute-start.7 = (bf16[1024,128]{1,0:T(8,128)(2,1)}, bf16[1024,128]{1,0:T(8,128)(2,1)}, u32[]{:S(2)}, u32[]{:S(2)}) collective-permute-start(bf16[1024,128]{1,0:T(8,128)(2,1)} %collective-permute-done.3.refs_2_), channel_id=1, source_target_pairs={{0,8},{1,9},{2,10},{3,11},{4,12},{5,13},{6,14},{7,15},{8,0},{9,1},... | collective-permute-start | bytes 786440 | tf_op jit(solution)/shard_map/ppermute | solution.py:31
  64.8 10.3 %collective-permute-done.4.refs_3_ = bf16[1024,128]{1,0:T(8,128)(2,1)} collective-permute-done((bf16[1024,128]{1,0:T(8,128)(2,1)S(1)}, bf16[1024,128]{1,0:T(8,128)(2,1)}, u32[]{:S(2)}, u32[]{:S(2)}) %collective-permute-start.4) | collective-permute-done | bytes 262176 | tf_op jit(solution)/shard_map/ppermute | solution.py:31
  75.1 2.7 %collective-permute-start.8 = (bf16[1024,128]{1,0:T(8,128)(2,1)}, bf16[1024,128]{1,0:T(8,128)(2,1)}, u32[]{:S(2)}, u32[]{:S(2)}) collective-permute-start(bf16[1024,128]{1,0:T(8,128)(2,1)} %collective-permute-done.4.refs_3_), channel_id=1, source_target_pairs={{0,8},{1,9},{2,10},{3,11},{4,12},{5,13},{6,14},{7,15},{8,0},{9,1},... | collective-permute-start | bytes 786440 | tf_op jit(solution)/shard_map/ppermute | solution.py:31
  84.5 8.7 %shard_map.47.refs_0_ = bf16[16,2,64,384]{3,2,1,0:T(8,128)(2,1)} custom-call(s32[5]{0:T(128)S(1)} %stack.38.place, f32[8,256]{1,0:T(8,128)S(1)} %reshape.9.gain_ref, bf16[1024,256]{1,0:T(8,128)(2,1)S(1)} %maximum_select_fusion.refs_0_.x_ref, bf16[1024,256]{1,0:T(8,128)(2,1)S(1)} %collective-permute-done.1.refs_1_, ...), custom_call_target="tpu_custom_call" | custom-call | tf_op jit(solution)/shard_map/pallas_call | solution.py:276
  93.2 9.9 %all-to-all-start = ((bf16[32,64,384]{2,1,0:T(8,128)(2,1)}), bf16[32,64,384]{2,1,0:T(8,128)(2,1)S(1)}, u32[]{:S(2)}, u32[]{:S(2)}) async-start(bf16[32,64,384]{2,1,0:T(8,128)(2,1)} %bitcast.9), calls=%async_computation | async-start | bytes 3145728 | tf_op jit(solution)/shard_map/all_to_all | solution.py:291
  103.2 2.6 %collective-permute-start.22 = (bf16[4,128,128]{2,1,0:T(8,128)(2,1)S(1)}, bf16[4,128,128]{2,1,0:T(8,128)(2,1)S(1)}, u32[]{:S(2)}, u32[]{:S(2)}) collective-permute-start(bf16[4,128,128]{2,1,0:T(8,128)(2,1)S(1)} %pad_maximum_fusion.2.refs_0_), channel_id=1, source_target_pairs={{0,48},{16,0},{32,16},{48,32},{64,112},{80,64},{96,80},{112,96},{1... | collective-permute-start | bytes 393224 | tf_op jit(solution)/shard_map/ppermute | solution.py:36
  107.0 7.3 %collective-permute-done.22.refs_3_ = bf16[4,128,128]{2,1,0:T(8,128)(2,1)S(1)} collective-permute-done((bf16[4,128,128]{2,1,0:T(8,128)(2,1)S(1)}, bf16[4,128,128]{2,1,0:T(8,128)(2,1)S(1)}, u32[]{:S(2)}, u32[]{:S(2)}) %collective-permute-start.22) | collective-permute-done | bytes 131104 | tf_op jit(solution)/shard_map/ppermute | solution.py:36
  115.0 3.2 %collective-permute-done.20.refs_1_ = bf16[4,128,128]{2,1,0:T(8,128)(2,1)S(1)} collective-permute-done((bf16[4,128,128]{2,1,0:T(8,128)(2,1)S(1)}, bf16[4,128,128]{2,1,0:T(8,128)(2,1)S(1)}, u32[]{:S(2)}, u32[]{:S(2)}) %collective-permute-start.20) | collective-permute-done | bytes 131104 | tf_op jit(solution)/shard_map/ppermute | solution.py:36
  120.0 3.1 %shard_map.49 = (f32[1024,128]{1,0:T(8,128)S(1)}, f32[64,128]{1,0:T(8,128)S(1)}) custom-call(bf16[16,2,64,384]{3,2,1,0:T(8,128)(2,1)} %shard_map.47.refs_0_), custom_call_target="tpu_custom_call" | custom-call | flops 8589934592 | bytes 1048576 | tf_op jit(solution)/shard_map/pallas_call | solution.py:276
  124.0 18.8 %all-to-all-done.z_ref = bf16[32,64,384]{2,1,0:T(8,128)(2,1)S(1)} async-done(((bf16[32,64,384]{2,1,0:T(8,128)(2,1)}), bf16[32,64,384]{2,1,0:T(8,128)(2,1)S(1)}, u32[]{:S(2)}, u32[]{:S(2)}) %all-to-all-start) | async-done | bytes 1572896 | tf_op jit(solution)/shard_map/all_to_all | solution.py:291
  145.8 6.2 %all-to-all-start.1 = ((bf16[32,72,128]{2,1,0:T(8,128)(2,1)}), bf16[32,72,128]{2,1,0:T(8,128)(2,1)S(1)}, u32[]{:S(2)}, u32[]{:S(2)}) async-start(bf16[32,72,128]{2,1,0:T(8,128)(2,1)} %copy-done), calls=%async_computation.1 | async-start | bytes 1179648 | tf_op jit(solution)/shard_map/all_to_all | solution.py:291
  152.0 3.2 %shard_map.50 = (f32[1024,128]{1,0:T(8,128)S(1)}, f32[64,128]{1,0:T(8,128)S(1)}) custom-call(bf16[16,2,64,384]{3,2,1,0:T(8,128)(2,1)} %shard_map.47.refs_0_), custom_call_target="tpu_custom_call" | custom-call | flops 8589934592 | bytes 1048576 | tf_op jit(solution)/shard_map/pallas_call | solution.py:276
  155.2 15.1 %all-to-all-done.1 = bf16[32,72,128]{2,1,0:T(8,128)(2,1)S(1)} async-done(((bf16[32,72,128]{2,1,0:T(8,128)(2,1)}), bf16[32,72,128]{2,1,0:T(8,128)(2,1)S(1)}, u32[]{:S(2)}, u32[]{:S(2)}) %all-to-all-start.1) | async-done | bytes 589856 | tf_op jit(solution)/shard_map/all_to_all | solution.py:291
  172.2 2.8 %collective-permute-start.24 = (bf16[1024,256]{1,0:T(8,128)(2,1)S(1)}, bf16[1024,256]{1,0:T(8,128)(2,1)S(1)}, u32[]{:S(2)}, u32[]{:S(2)}) collective-permute-start(bf16[1024,256]{1,0:T(8,128)(2,1)S(1)} %shard_map.52.refs_0_), channel_id=1, source_target_pairs={{0,6},{1,7},{2,0},{3,1},{4,2},{5,3},{6,4},{7,5},{8,14},{9,15},{10,... | collective-permute-start | bytes 1572872 | tf_op jit(solution)/shard_map/ppermute | solution.py:31
  175.0 11.9 %collective-permute-done.25.refs_4_ = bf16[1024,256]{1,0:T(8,128)(2,1)S(1)} collective-permute-done((bf16[1024,256]{1,0:T(8,128)(2,1)S(1)}, bf16[1024,256]{1,0:T(8,128)(2,1)S(1)}, u32[]{:S(2)}, u32[]{:S(2)}) %collective-permute-start.25) | collective-permute-done | bytes 524320 | tf_op jit(solution)/shard_map/ppermute | solution.py:31
  187.2 2.7 %collective-permute-start.29 = (bf16[1024,256]{1,0:T(8,128)(2,1)S(1)}, bf16[1024,256]{1,0:T(8,128)(2,1)S(1)}, u32[]{:S(2)}, u32[]{:S(2)}) collective-permute-start(bf16[1024,256]{1,0:T(8,128)(2,1)S(1)} %collective-permute-done.28.refs_5_), channel_id=1, source_target_pairs={{0,6},{1,7},{2,0},{3,1},{4,2},{5,3},{6,4},{7,5},{8,14},{9,15},{10,... | collective-permute-start | bytes 1572872 | tf_op jit(solution)/shard_map/ppermute | solution.py:31
  191.3 4.1 %collective-permute-done.26.refs_2_ = bf16[1024,128]{1,0:T(8,128)(2,1)S(1)} collective-permute-done((bf16[1024,128]{1,0:T(8,128)(2,1)S(1)}, bf16[1024,128]{1,0:T(8,128)(2,1)S(1)}, u32[]{:S(2)}, u32[]{:S(2)}) %collective-permute-start.26) | collective-permute-done | bytes 262176 | tf_op jit(solution)/shard_map/ppermute | solution.py:31
  195.4 10.3 %collective-permute-done.27.refs_3_ = bf16[1024,128]{1,0:T(8,128)(2,1)S(1)} collective-permute-done((bf16[1024,128]{1,0:T(8,128)(2,1)S(1)}, bf16[1024,128]{1,0:T(8,128)(2,1)S(1)}, u32[]{:S(2)}, u32[]{:S(2)}) %collective-permute-start.27) | collective-permute-done | bytes 262176 | tf_op jit(solution)/shard_map/ppermute | solution.py:31
  206.6 5.1 %collective-permute-done.31.refs_8_ = bf16[1024,128]{1,0:T(8,128)(2,1)S(1)} collective-permute-done((bf16[1024,128]{1,0:T(8,128)(2,1)S(1)}, bf16[1024,128]{1,0:T(8,128)(2,1)S(1)}, u32[]{:S(2)}, u32[]{:S(2)}) %collective-permute-start.31) | collective-permute-done | bytes 262176 | tf_op jit(solution)/shard_map/ppermute | solution.py:31
  211.7 2.6 %shard_map.53 = (bf16[2048,128]{1,0:T(8,128)(2,1)}, bf16[1024,128]{1,0:T(8,128)(2,1)S(1)}) custom-call(s32[5]{0:T(128)S(1)} %stack.38.place, bf16[1024,256]{1,0:T(8,128)(2,1)S(1)} %maximum_select_fusion.refs_0_.x_ref, bf16[1024,256]{1,0:T(8,128)(2,1)S(1)} %shard_map.52.refs_0_, bf16[1024,256]{1,0:T(8,128)(2,1)S(1)} %collective-permute-done.24.refs_1_, ...), custom_call_target="tpu_custom_call" | custom-call | tf_op jit(solution)/shard_map/pallas_call | solution.py:276
  214.3 2.7 %collective-permute-start.33 = (bf16[1024,128]{1,0:T(8,128)(2,1)S(1)}, bf16[1024,128]{1,0:T(8,128)(2,1)S(1)}, u32[]{:S(2)}, u32[]{:S(2)}) collective-permute-start(bf16[1024,128]{1,0:T(8,128)(2,1)S(1)} %get-tuple-element.28), channel_id=1, source_target_pairs={{0,1},{1,0},{2,3},{3,2},{4,5},{5,4},{6,7},{7,6},{8,9},{9,8},{10,11... | collective-permute-start | bytes 786440 | tf_op jit(solution)/shard_map/ppermute | solution.py:31
  (107 shorter events, 35.0 us)
Async XLA Ops:
  1.1 12.6 %collective-permute-start = (bf16[1024,128]{1,0:T(8,128)(2,1)S(1)}, bf16[1024,128]{1,0:T(8,128)(2,1)S(1)}, u32[]{:S(2)}, u32[]{:S(2)}) collective-permute-start(bf16[1024,128]{1,0:T(8,128)(2,1)S(1)} %get-tuple-element.30), channel_id=1, source_target_pairs={{0,1},{1,0},{2,3},{3,2},{4,5},{5,4},{6,7},{7,6},{8,9},{9,8},{10,11... | collective-permute-start | bytes 786440 | tf_op jit(solution)/shard_map/ppermute | solution.py:31
  6.0 9.2 %collective-permute-start.12 = (bf16[128,512]{1,0:T(8,128)(2,1)S(1)}, bf16[128,512]{1,0:T(8,128)(2,1)S(1)}, u32[]{:S(2)}, u32[]{:S(2)}) collective-permute-start(bf16[128,512]{1,0:T(8,128)(2,1)S(1)} %constant_dynamic-update-slice_fusion), channel_id=1, source_target_pairs={{0,192},{16,208},{32,224},{48,240},{64,0},{80,16},{96,32},{112,48}... | collective-permute-start | bytes 393224 | tf_op jit(solution)/shard_map/ppermute | solution.py:36
  10.4 12.0 %collective-permute-start.11 = (bf16[128,512]{1,0:T(8,128)(2,1)S(1)}, bf16[128,512]{1,0:T(8,128)(2,1)S(1)}, u32[]{:S(2)}, u32[]{:S(2)}) collective-permute-start(bf16[128,512]{1,0:T(8,128)(2,1)S(1)} %constant_dynamic-update-slice_fusion), channel_id=1, source_target_pairs={{0,128},{16,144},{32,160},{48,176},{64,192},{80,208},{96,224},{112... | collective-permute-start | bytes 393224 | tf_op jit(solution)/shard_map/ppermute | solution.py:36
  11.4 11.0 %collective-permute-start.10 = (bf16[128,512]{1,0:T(8,128)(2,1)S(1)}, bf16[128,512]{1,0:T(8,128)(2,1)S(1)}, u32[]{:S(2)}, u32[]{:S(2)}) collective-permute-start(bf16[128,512]{1,0:T(8,128)(2,1)S(1)} %constant_dynamic-update-slice_fusion), channel_id=1, source_target_pairs={{0,64},{16,80},{32,96},{48,112},{64,128},{80,144},{96,160},{112,17... | collective-permute-start | bytes 393224 | tf_op jit(solution)/shard_map/ppermute | solution.py:36
  13.9 29.4 %collective-permute-start.2 = (bf16[1024,256]{1,0:T(8,128)(2,1)S(1)}, bf16[1024,256]{1,0:T(8,128)(2,1)S(1)}, u32[]{:S(2)}, u32[]{:S(2)}) collective-permute-start(bf16[1024,256]{1,0:T(8,128)(2,1)S(1)} %maximum_select_fusion.refs_0_.x_ref), channel_id=1, source_target_pairs={{0,2},{1,3},{2,4},{3,5},{4,6},{5,7},{6,0},{7,1},{8,10},{9,11},{10,... | collective-permute-start | bytes 1572872 | tf_op jit(solution)/shard_map/ppermute | solution.py:31
  23.2 9.5 %collective-permute-start.15 = (bf16[4,128,384]{2,1,0:T(8,128)(2,1)S(1)}, bf16[4,128,384]{2,1,0:T(8,128)(2,1)S(1)}, u32[]{:S(2)}, u32[]{:S(2)}) collective-permute-start(bf16[4,128,384]{2,1,0:T(8,128)(2,1)S(1)} %slice.26.refs_0_), channel_id=1, source_target_pairs={{0,48},{16,0},{32,16},{48,32},{64,112},{80,64},{96,80},{112,96},{1... | collective-permute-start | bytes 1179656 | tf_op jit(solution)/shard_map/ppermute | solution.py:36
  25.5 19.9 %collective-permute-start.1 = (bf16[1024,256]{1,0:T(8,128)(2,1)S(1)}, bf16[1024,256]{1,0:T(8,128)(2,1)S(1)}, u32[]{:S(2)}, u32[]{:S(2)}) collective-permute-start(bf16[1024,256]{1,0:T(8,128)(2,1)S(1)} %maximum_select_fusion.refs_0_.x_ref), channel_id=1, source_target_pairs={{0,6},{1,7},{2,0},{3,1},{4,2},{5,3},{6,4},{7,5},{8,14},{9,15},{10,... | collective-permute-start | bytes 1572872 | tf_op jit(solution)/shard_map/ppermute | solution.py:31
  28.2 15.1 %collective-permute-start.14 = (bf16[4,128,384]{2,1,0:T(8,128)(2,1)S(1)}, bf16[4,128,384]{2,1,0:T(8,128)(2,1)S(1)}, u32[]{:S(2)}, u32[]{:S(2)}) collective-permute-start(bf16[4,128,384]{2,1,0:T(8,128)(2,1)S(1)} %slice.26.refs_0_), channel_id=1, source_target_pairs={{0,32},{16,48},{32,0},{48,16},{64,96},{80,112},{96,64},{112,80},{1... | collective-permute-start | bytes 1179656 | tf_op jit(solution)/shard_map/ppermute | solution.py:36
  28.7 18.8 %collective-permute-start.5 = (bf16[1024,256]{1,0:T(8,128)(2,1)S(1)}, bf16[1024,256]{1,0:T(8,128)(2,1)S(1)}, u32[]{:S(2)}, u32[]{:S(2)}) collective-permute-start(bf16[1024,256]{1,0:T(8,128)(2,1)S(1)} %maximum_select_fusion.refs_0_.x_ref), channel_id=1, source_target_pairs={{0,8},{1,9},{2,10},{3,11},{4,12},{5,13},{6,14},{7,15},{8,0},{9,1},... | collective-permute-start | bytes 1572872 | tf_op jit(solution)/shard_map/ppermute | solution.py:31
  32.7 12.9 %collective-permute-start.16 = (bf16[4,128,384]{2,1,0:T(8,128)(2,1)S(1)}, bf16[4,128,384]{2,1,0:T(8,128)(2,1)S(1)}, u32[]{:S(2)}, u32[]{:S(2)}) collective-permute-start(bf16[4,128,384]{2,1,0:T(8,128)(2,1)S(1)} %slice.26.refs_0_), channel_id=1, source_target_pairs={{0,1},{1,0},{2,3},{3,2},{4,5},{5,4},{6,7},{7,6},{8,9},{9,8},{10,11... | collective-permute-start | bytes 1179656 | tf_op jit(solution)/shard_map/ppermute | solution.py:31
  43.3 12.9 %collective-permute-start.13 = (bf16[4,128,384]{2,1,0:T(8,128)(2,1)S(1)}, bf16[4,128,384]{2,1,0:T(8,128)(2,1)}, u32[]{:S(2)}, u32[]{:S(2)}) collective-permute-start(bf16[4,128,384]{2,1,0:T(8,128)(2,1)S(1)} %slice.26.refs_0_), channel_id=1, source_target_pairs={{0,16},{16,32},{32,48},{48,0},{64,80},{80,96},{96,112},{112,64},{1... | collective-permute-start | bytes 1179656 | tf_op jit(solution)/shard_map/ppermute | solution.py:36
  43.3 15.6 %collective-permute-start.19 = (bf16[4,128,384]{2,1,0:T(8,128)(2,1)S(1)}, bf16[4,128,384]{2,1,0:T(8,128)(2,1)S(1)}, u32[]{:S(2)}, u32[]{:S(2)}) collective-permute-start(bf16[4,128,384]{2,1,0:T(8,128)(2,1)S(1)} %collective-permute-done.15.refs_3_), channel_id=1, source_target_pairs={{0,1},{1,0},{2,3},{3,2},{4,5},{5,4},{6,7},{7,6},{8,9},{9,8},{10,11... | collective-permute-start | bytes 1179656 | tf_op jit(solution)/shard_map/ppermute | solution.py:31
  45.4 14.7 %collective-permute-start.18 = (bf16[4,128,384]{2,1,0:T(8,128)(2,1)S(1)}, bf16[4,128,384]{2,1,0:T(8,128)(2,1)S(1)}, u32[]{:S(2)}, u32[]{:S(2)}) collective-permute-start(bf16[4,128,384]{2,1,0:T(8,128)(2,1)S(1)} %collective-permute-done.14.refs_2_), channel_id=1, source_target_pairs={{0,1},{1,0},{2,3},{3,2},{4,5},{5,4},{6,7},{7,6},{8,9},{9,8},{10,11... | collective-permute-start | bytes 1179656 | tf_op jit(solution)/shard_map/ppermute | solution.py:31
  46.3 15.8 %collective-permute-start.3 = (bf16[1024,128]{1,0:T(8,128)(2,1)S(1)}, bf16[1024,128]{1,0:T(8,128)(2,1)}, u32[]{:S(2)}, u32[]{:S(2)}) collective-permute-start(bf16[1024,128]{1,0:T(8,128)(2,1)S(1)} %slice.24), channel_id=1, source_target_pairs={{0,2},{1,3},{2,4},{3,5},{4,6},{5,7},{6,0},{7,1},{8,10},{9,11},{10,... | collective-permute-start | bytes 786440 | tf_op jit(solution)/shard_map/ppermute | solution.py:31
  47.6 36.8 %collective-permute-start.9 = (bf16[1024,256]{1,0:T(8,128)(2,1)S(1)}, bf16[1024,256]{1,0:T(8,128)(2,1)S(1)}, u32[]{:S(2)}, u32[]{:S(2)}) collective-permute-start(bf16[1024,256]{1,0:T(8,128)(2,1)S(1)} %collective-permute-done.5.refs_5_), channel_id=1, source_target_pairs={{0,2},{1,3},{2,4},{3,5},{4,6},{5,7},{6,0},{7,1},{8,10},{9,11},{10,... | collective-permute-start | bytes 1572872 | tf_op jit(solution)/shard_map/ppermute | solution.py:31
  56.2 28.3 %collective-permute-start.6 = (bf16[1024,256]{1,0:T(8,128)(2,1)S(1)}, bf16[1024,256]{1,0:T(8,128)(2,1)S(1)}, u32[]{:S(2)}, u32[]{:S(2)}) collective-permute-start(bf16[1024,256]{1,0:T(8,128)(2,1)S(1)} %collective-permute-done.5.refs_5_), channel_id=1, source_target_pairs={{0,6},{1,7},{2,0},{3,1},{4,2},{5,3},{6,4},{7,5},{8,14},{9,15},{10,... | collective-permute-start | bytes 1572872 | tf_op jit(solution)/shard_map/ppermute | solution.py:31
  59.7 15.5 %collective-permute-start.4 = (bf16[1024,128]{1,0:T(8,128)(2,1)S(1)}, bf16[1024,128]{1,0:T(8,128)(2,1)}, u32[]{:S(2)}, u32[]{:S(2)}) collective-permute-start(bf16[1024,128]{1,0:T(8,128)(2,1)S(1)} %slice.25), channel_id=1, source_target_pairs={{0,6},{1,7},{2,0},{3,1},{4,2},{5,3},{6,4},{7,5},{8,14},{9,15},{10,... | collective-permute-start | bytes 786440 | tf_op jit(solution)/shard_map/ppermute | solution.py:31
  60.9 17.0 %collective-permute-start.17 = (bf16[4,128,384]{2,1,0:T(8,128)(2,1)}, bf16[4,128,384]{2,1,0:T(8,128)(2,1)}, u32[]{:S(2)}, u32[]{:S(2)}) collective-permute-start(bf16[4,128,384]{2,1,0:T(8,128)(2,1)} %collective-permute-done.13.refs_1_), channel_id=1, source_target_pairs={{0,1},{1,0},{2,3},{3,2},{4,5},{5,4},{6,7},{7,6},{8,9},{9,8},{10,11... | collective-permute-start | bytes 1179656 | tf_op jit(solution)/shard_map/ppermute | solution.py:31
  62.1 22.3 %collective-permute-start.7 = (bf16[1024,128]{1,0:T(8,128)(2,1)}, bf16[1024,128]{1,0:T(8,128)(2,1)}, u32[]{:S(2)}, u32[]{:S(2)}) collective-permute-start(bf16[1024,128]{1,0:T(8,128)(2,1)} %collective-permute-done.3.refs_2_), channel_id=1, source_target_pairs={{0,8},{1,9},{2,10},{3,11},{4,12},{5,13},{6,14},{7,15},{8,0},{9,1},... | collective-permute-start | bytes 786440 | tf_op jit(solution)/shard_map/ppermute | solution.py:31
  75.1 9.3 %collective-permute-start.8 = (bf16[1024,128]{1,0:T(8,128)(2,1)}, bf16[1024,128]{1,0:T(8,128)(2,1)}, u32[]{:S(2)}, u32[]{:S(2)}) collective-permute-start(bf16[1024,128]{1,0:T(8,128)(2,1)} %collective-permute-done.4.refs_3_), channel_id=1, source_target_pairs={{0,8},{1,9},{2,10},{3,11},{4,12},{5,13},{6,14},{7,15},{8,0},{9,1},... | collective-permute-start | bytes 786440 | tf_op jit(solution)/shard_map/ppermute | solution.py:31
  93.2 49.7 %all-to-all-start = ((bf16[32,64,384]{2,1,0:T(8,128)(2,1)}), bf16[32,64,384]{2,1,0:T(8,128)(2,1)S(1)}, u32[]{:S(2)}, u32[]{:S(2)}) async-start(bf16[32,64,384]{2,1,0:T(8,128)(2,1)} %bitcast.9), calls=%async_computation | async-start | bytes 3145728 | tf_op jit(solution)/shard_map/all_to_all | solution.py:291
  103.2 11.1 %collective-permute-start.22 = (bf16[4,128,128]{2,1,0:T(8,128)(2,1)S(1)}, bf16[4,128,128]{2,1,0:T(8,128)(2,1)S(1)}, u32[]{:S(2)}, u32[]{:S(2)}) collective-permute-start(bf16[4,128,128]{2,1,0:T(8,128)(2,1)S(1)} %pad_maximum_fusion.2.refs_0_), channel_id=1, source_target_pairs={{0,48},{16,0},{32,16},{48,32},{64,112},{80,64},{96,80},{112,96},{1... | collective-permute-start | bytes 393224 | tf_op jit(solution)/shard_map/ppermute | solution.py:36
  105.8 9.2 %collective-permute-start.21 = (bf16[4,128,128]{2,1,0:T(8,128)(2,1)S(1)}, bf16[4,128,128]{2,1,0:T(8,128)(2,1)S(1)}, u32[]{:S(2)}, u32[]{:S(2)}) collective-permute-start(bf16[4,128,128]{2,1,0:T(8,128)(2,1)S(1)} %pad_maximum_fusion.2.refs_0_), channel_id=1, source_target_pairs={{0,32},{16,48},{32,0},{48,16},{64,96},{80,112},{96,64},{112,80},{1... | collective-permute-start | bytes 393224 | tf_op jit(solution)/shard_map/ppermute | solution.py:36
  106.4 11.8 %collective-permute-start.20 = (bf16[4,128,128]{2,1,0:T(8,128)(2,1)S(1)}, bf16[4,128,128]{2,1,0:T(8,128)(2,1)S(1)}, u32[]{:S(2)}, u32[]{:S(2)}) collective-permute-start(bf16[4,128,128]{2,1,0:T(8,128)(2,1)S(1)} %pad_maximum_fusion.2.refs_0_), channel_id=1, source_target_pairs={{0,16},{16,32},{32,48},{48,0},{64,80},{80,96},{96,112},{112,64},{1... | collective-permute-start | bytes 393224 | tf_op jit(solution)/shard_map/ppermute | solution.py:36
  145.8 24.5 %all-to-all-start.1 = ((bf16[32,72,128]{2,1,0:T(8,128)(2,1)}), bf16[32,72,128]{2,1,0:T(8,128)(2,1)S(1)}, u32[]{:S(2)}, u32[]{:S(2)}) async-start(bf16[32,72,128]{2,1,0:T(8,128)(2,1)} %copy-done), calls=%async_computation.1 | async-start | bytes 1179648 | tf_op jit(solution)/shard_map/all_to_all | solution.py:291
  171.2 15.7 %collective-permute-start.25 = (bf16[1024,256]{1,0:T(8,128)(2,1)S(1)}, bf16[1024,256]{1,0:T(8,128)(2,1)S(1)}, u32[]{:S(2)}, u32[]{:S(2)}) collective-permute-start(bf16[1024,256]{1,0:T(8,128)(2,1)S(1)} %shard_map.52.refs_0_), channel_id=1, source_target_pairs={{0,2},{1,3},{2,4},{3,5},{4,6},{5,7},{6,0},{7,1},{8,10},{9,11},{10,... | collective-permute-start | bytes 1572872 | tf_op jit(solution)/shard_map/ppermute | solution.py:31
  172.2 14.9 %collective-permute-start.28 = (bf16[1024,256]{1,0:T(8,128)(2,1)S(1)}, bf16[1024,256]{1,0:T(8,128)(2,1)S(1)}, u32[]{:S(2)}, u32[]{:S(2)}) collective-permute-start(bf16[1024,256]{1,0:T(8,128)(2,1)S(1)} %shard_map.52.refs_0_), channel_id=1, source_target_pairs={{0,8},{1,9},{2,10},{3,11},{4,12},{5,13},{6,14},{7,15},{8,0},{9,1},... | collective-permute-start | bytes 1572872 | tf_op jit(solution)/shard_map/ppermute | solution.py:31
  172.2 17.7 %collective-permute-start.24 = (bf16[1024,256]{1,0:T(8,128)(2,1)S(1)}, bf16[1024,256]{1,0:T(8,128)(2,1)S(1)}, u32[]{:S(2)}, u32[]{:S(2)}) collective-permute-start(bf16[1024,256]{1,0:T(8,128)(2,1)S(1)} %shard_map.52.refs_0_), channel_id=1, source_target_pairs={{0,6},{1,7},{2,0},{3,1},{4,2},{5,3},{6,4},{7,5},{8,14},{9,15},{10,... | collective-permute-start | bytes 1572872 | tf_op jit(solution)/shard_map/ppermute | solution.py:31
  187.1 19.5 %collective-permute-start.32 = (bf16[1024,256]{1,0:T(8,128)(2,1)S(1)}, bf16[1024,256]{1,0:T(8,128)(2,1)S(1)}, u32[]{:S(2)}, u32[]{:S(2)}) collective-permute-start(bf16[1024,256]{1,0:T(8,128)(2,1)S(1)} %collective-permute-done.28.refs_5_), channel_id=1, source_target_pairs={{0,2},{1,3},{2,4},{3,5},{4,6},{5,7},{6,0},{7,1},{8,10},{9,11},{10,... | collective-permute-start | bytes 1572872 | tf_op jit(solution)/shard_map/ppermute | solution.py:31
  187.2 19.5 %collective-permute-start.29 = (bf16[1024,256]{1,0:T(8,128)(2,1)S(1)}, bf16[1024,256]{1,0:T(8,128)(2,1)S(1)}, u32[]{:S(2)}, u32[]{:S(2)}) collective-permute-start(bf16[1024,256]{1,0:T(8,128)(2,1)S(1)} %collective-permute-done.28.refs_5_), channel_id=1, source_target_pairs={{0,6},{1,7},{2,0},{3,1},{4,2},{5,3},{6,4},{7,5},{8,14},{9,15},{10,... | collective-permute-start | bytes 1572872 | tf_op jit(solution)/shard_map/ppermute | solution.py:31
  189.9 15.8 %collective-permute-start.27 = (bf16[1024,128]{1,0:T(8,128)(2,1)S(1)}, bf16[1024,128]{1,0:T(8,128)(2,1)S(1)}, u32[]{:S(2)}, u32[]{:S(2)}) collective-permute-start(bf16[1024,128]{1,0:T(8,128)(2,1)S(1)} %slice.28), channel_id=1, source_target_pairs={{0,6},{1,7},{2,0},{3,1},{4,2},{5,3},{6,4},{7,5},{8,14},{9,15},{10,... | collective-permute-start | bytes 786440 | tf_op jit(solution)/shard_map/ppermute | solution.py:31
  195.4 11.2 %collective-permute-start.30 = (bf16[1024,128]{1,0:T(8,128)(2,1)S(1)}, bf16[1024,128]{1,0:T(8,128)(2,1)S(1)}, u32[]{:S(2)}, u32[]{:S(2)}) collective-permute-start(bf16[1024,128]{1,0:T(8,128)(2,1)S(1)} %collective-permute-done.26.refs_2_), channel_id=1, source_target_pairs={{0,8},{1,9},{2,10},{3,11},{4,12},{5,13},{6,14},{7,15},{8,0},{9,1},... | collective-permute-start | bytes 786440 | tf_op jit(solution)/shard_map/ppermute | solution.py:31
  (26 other events, 231.0 us)
where the time goes:
time: 220 us; the launch traced here: 219 us
  waiting for transfers between devices  105 us (48%)
  starting transfers between devices  77.3 us (35%)
  Pallas kernels  23.1 us (10%)
  local copies, waits for them, and re-layouts  13.1 us (6%)
    ppermute x25, starting transfers between devices, _over_col(): return lax.ppermute(x, 'col', pairs)  46.9 us
    ppermute x25, waiting for transfers between devices, _over_col(): return lax.ppermute(x, 'col', pairs)  43.9 us
    all_to_all x2, waiting for transfers between devices, exchange_columns(): lax.all_to_all(x, ('row', 'col'), split_axis=0, concat_axis=0, axis_index...  33.9 us
    ppermute x9, waiting for transfers between devices, _over_row(): return lax.ppermute(x, 'row', pairs)  27 us
    pallas_call x8, Pallas kernels, _call(): pl.pallas_call(kernel, out_shape=out, in_specs=[smem] * scalars + [vmem]...  23.1 us
    all_to_all x2, starting transfers between devices, exchange_columns(): lax.all_to_all(x, ('row', 'col'), split_axis=0, concat_axis=0, axis_index...  16.1 us
    ppermute x9, starting transfers between devices, _over_row(): return lax.ppermute(x, 'row', pairs)  14.3 us
    unnamed x45, local copies, waits for them, and re-layouts  10.4 us
  transfers between devices with their start and end apart: 36, of which 15 were waited for; matrix products, arithmetic and copies ran while one was open for 1% of the time, Pallas kernels for 4%

commit v1 on v0

--- a/solution.py
+++ b/solution.py
@@ -97,7 +97,42 @@
                 out[pl.ds(at, 128), side * width : (side + 1) * width] = refs[4 * side + dx][dz]
 
 
-def _qkv_kernel(place, gain_ref, *refs):
+def _chunks(refs):
+    return [(ref, k * HS) for ref in refs for k in range(ref.shape[1] // HS)]
+
+
+def _moments(chunks, rows):
+    n = TILE
+    total = jnp.zeros((n, HS), F32)
+    for ref, k in chunks:
+        total += ref[rows, pl.ds(k, HS)].astype(F32)
+    mean = jnp.sum(total, axis=1, keepdims=True) * (1.0 / (len(chunks) * HS))
+    square = jnp.zeros((n, HS), F32)
+    for ref, k in chunks:
+        v = ref[rows, pl.ds(k, HS)].astype(F32) - mean
+        square += v * v
+    return mean, jnp.sum(square, axis=1, keepdims=True)
+
+
+EARLY = (0, 1, 2, 3, 4, 5)
+LATE = (6, 7, 8, 9)
+EARLY_WIDTH = 1280
+LATE_WIDTH = 768
+
+
+def _early_kernel(*refs):
+    chunks = _chunks(refs[:-2])
+    mean_ref, square_ref = refs[-2:]
+
+    def step(tile, carry):
+        rows = pl.ds(pl.multiple_of(tile * TILE, TILE), TILE)
+        mean_ref[rows, :], square_ref[rows, :] = _moments(chunks, rows)
+        return carry
+
+    lax.fori_loop(0, COLS // TILE, step, 0)
+
+
+def _qkv_kernel(place, gain_ref, early_mean_ref, early_square_ref, *refs):
     pieces, (w_ref, out_ref, even_ref, odd_ref) = refs[:10], refs[10:]
     zl, y, core = place[0], place[1], place[4]
     gains = []
@@ -116,18 +151,17 @@
     def rows_of(tile):
         return pl.ds(pl.multiple_of(tile * TILE, TILE), TILE)
 
-    def mean_of(tile):
-        total = jnp.zeros((TILE, HS), F32)
-        for ref, k, _ in chunks:
-            total += ref[rows_of(tile), pl.ds(k, HS)].astype(F32)
-        return jnp.sum(total, axis=1, keepdims=True) * (1.0 / wide)
-
-    def rstd_of(tile, mean):
-        square = jnp.zeros((TILE, HS), F32)
-        for ref, k, _ in chunks:
-            v = ref[rows_of(tile), pl.ds(k, HS)].astype(F32) - mean
-            square += v * v
-        return lax.rsqrt(jnp.sum(square, axis=1, keepdims=True) * (1.0 / wide) + EPSILON)
+    late = _chunks([pieces[i] for i in LATE])
+
+    def moments_of(tile):
+        return _moments(late, rows_of(tile))
+
+    def together(tile, late_mean, late_square):
+        mean = early_mean_ref[rows_of(tile), :]
+        apart = late_mean - mean
+        square = early_square_ref[rows_of(tile), :] + late_square
+        square += apart * apart * (EARLY_WIDTH * LATE_WIDTH / wide)
+        return mean + apart * (LATE_WIDTH / wide), lax.rsqrt(square * (1.0 / wide) + EPSILON)
 
     def norm(tile, mean, rstd, to_ref):
         for ref, k, at in chunks:
@@ -145,16 +179,15 @@
             out_ref[blocks, slot, :, (n % 3) * HS : (n % 3 + 1) * HS] = v
 
     def both(tile, from_ref, later, to_ref):
-        mean = mean_of(later)
+        moments = moments_of(later)
         project(tile, from_ref, 0)
-        rstd = rstd_of(later, mean)
+        mean, rstd = together(later, *moments)
         project(tile, from_ref, 1)
         norm(later, mean, rstd, to_ref)
         project(tile, from_ref, 2)
 
     count = COLS // TILE
-    mean = mean_of(0)
-    norm(0, mean, rstd_of(0, mean), even_ref)
+    norm(0, *together(0, *moments_of(0)), even_ref)
 
     def step(i, carry):
         both(2 * i, even_ref, 2 * i + 1, odd_ref)
@@ -305,17 +338,21 @@
     x = jnp.where(
         core == 0, jnp.concatenate([mine, theirs], axis=1), jnp.concatenate([theirs, mine], axis=1)
     )
-    weights = jnp.concatenate([qkv_weight, out_weight], axis=1)
+    weights = lax.optimization_barrier(jnp.concatenate([qkv_weight, out_weight], axis=1))
     pieces = gather_chips(x)
     weights = over_z_hi(weights)
     own = over_x(weights[..., : 3 * HS])
     other = (core_swap(t) for t in own)
     w = _call(_weights_kernel, shape((2048, 6 * HS), BF16), place, *own, *other, scalars=1)
+    moments = _call(
+        _early_kernel, (shape((COLS, 1), F32), shape((COLS, 1), F32)), *(pieces[i] for i in EARLY), flops=1 << 30
+    )
     qkv = _call(
         _qkv_kernel,
         shape((16, 2, 64, 3 * HS), BF16),
         place,
         norm_gain.reshape(8, 256),
+        *moments,
         *pieces,
         w,
         scalars=1,

time: 220 us -> 219 us (level)
    pallas_call x8 -> x9, Pallas kernels: 23.1 us -> 24.5 us  [_call(): pl.pallas_call(kernel, out_shape=out, in_specs=[smem] * scalars + [vmem]...]
    unnamed x45 -> x44, local copies, waits for them, and re-layouts: 10.4 us -> 8.9 us
  transfers between devices with their start and end apart: 36 -> 36, of which waited for: 15 -> 15; matrix products, arithmetic and copies ran while one was open for 1% -> 1% of each run, Pallas kernels for 4% -> 5%
where the time goes in v1:
time: 219 us
  waiting for transfers between devices  105 us (48%)
  starting transfers between devices  76.2 us (35%)
  Pallas kernels  24.5 us (11%)
  local copies, waits for them, and re-layouts  10.9 us (5%)
    ppermute x25, starting transfers between devices, _over_col(): return lax.ppermute(x, 'col', pairs)  45.6 us
    ppermute x25, waiting for transfers between devices, _over_col(): return lax.ppermute(x, 'col', pairs)  44.3 us
    all_to_all x2, waiting for transfers between devices, exchange_columns(): lax.all_to_all(x, ('row', 'col'), split_axis=0, concat_axis=0, axis_index...  33.6 us
    ppermute x9, waiting for transfers between devices, _over_row(): return lax.ppermute(x, 'row', pairs)  27.6 us
    pallas_call x9, Pallas kernels, _call(): pl.pallas_call(kernel, out_shape=out, in_specs=[smem] * scalars + [vmem]...  24.5 us
    all_to_all x2, starting transfers between devices, exchange_columns(): lax.all_to_all(x, ('row', 'col'), split_axis=0, concat_axis=0, axis_index...  16 us
    ppermute x9, starting transfers between devices, _over_row(): return lax.ppermute(x, 'row', pairs)  14.6 us
    unnamed x44, local copies, waits for them, and re-layouts  8.9 us
  transfers between devices with their start and end apart: 36, of which 15 were waited for; matrix products, arithmetic and copies ran while one was open for 1% of the time, Pallas kernels for 5%

profile of v1, /device:TPU:1, one launch (start us, length us, event | category | flops | bytes accessed | tf_op | source)
XLA Modules:
  0.0 218.6 jit_solution(3500144818749802285)
XLA Ops:
  1.1 3.3 %collective-permute-start = (bf16[1024,128]{1,0:T(8,128)(2,1)S(1)}, bf16[1024,128]{1,0:T(8,128)(2,1)S(1)}, u32[]{:S(2)}, u32[]{:S(2)}) collective-permute-start(bf16[1024,128]{1,0:T(8,128)(2,1)S(1)} %get-tuple-element.34), channel_id=1, source_target_pairs={{0,1},{1,0},{2,3},{3,2},{4,5},{5,4},{6,7},{7,6},{8,9},{9,8},{10,11... | collective-permute-start | bytes 786440 | tf_op jit(solution)/shard_map/ppermute | solution.py:31
  5.3 4.4 %collective-permute-start.12 = (bf16[128,512]{1,0:T(8,128)(2,1)S(1)}, bf16[128,512]{1,0:T(8,128)(2,1)S(1)}, u32[]{:S(2)}, u32[]{:S(2)}) collective-permute-start(bf16[128,512]{1,0:T(8,128)(2,1)S(1)} %pad_maximum_fusion.3), channel_id=1, source_target_pairs={{0,192},{16,208},{32,224},{48,240},{64,0},{80,16},{96,32},{112,48}... | collective-permute-start | bytes 393224 | tf_op jit(solution)/shard_map/ppermute | solution.py:36
  10.7 2.3 %collective-permute-start.10 = (bf16[128,512]{1,0:T(8,128)(2,1)S(1)}, bf16[128,512]{1,0:T(8,128)(2,1)S(1)}, u32[]{:S(2)}, u32[]{:S(2)}) collective-permute-start(bf16[128,512]{1,0:T(8,128)(2,1)S(1)} %pad_maximum_fusion.3), channel_id=1, source_target_pairs={{0,64},{16,80},{32,96},{48,112},{64,128},{80,144},{96,160},{112,17... | collective-permute-start | bytes 393224 | tf_op jit(solution)/shard_map/ppermute | solution.py:36
  16.1 5.7 %collective-permute-done.11 = bf16[128,512]{1,0:T(8,128)(2,1)S(1)} collective-permute-done((bf16[128,512]{1,0:T(8,128)(2,1)S(1)}, bf16[128,512]{1,0:T(8,128)(2,1)S(1)}, u32[]{:S(2)}, u32[]{:S(2)}) %collective-permute-start.11) | collective-permute-done | bytes 131104 | tf_op jit(solution)/shard_map/ppermute | solution.py:36
  21.9 2.4 %collective-permute-start.15 = (bf16[4,128,384]{2,1,0:T(8,128)(2,1)S(1)}, bf16[4,128,384]{2,1,0:T(8,128)(2,1)S(1)}, u32[]{:S(2)}, u32[]{:S(2)}) collective-permute-start(bf16[4,128,384]{2,1,0:T(8,128)(2,1)S(1)} %slice.26.refs_0_), channel_id=1, source_target_pairs={{0,48},{16,0},{32,16},{48,32},{64,112},{80,64},{96,80},{112,96},{1... | collective-permute-start | bytes 1179656 | tf_op jit(solution)/shard_map/ppermute | solution.py:36
  25.0 2.7 %collective-permute-start.5 = (bf16[1024,256]{1,0:T(8,128)(2,1)S(1)}, bf16[1024,256]{1,0:T(8,128)(2,1)S(1)}, u32[]{:S(2)}, u32[]{:S(2)}) collective-permute-start(bf16[1024,256]{1,0:T(8,128)(2,1)S(1)} %maximum_select_fusion.refs_0_.x_ref), channel_id=1, source_target_pairs={{0,8},{1,9},{2,10},{3,11},{4,12},{5,13},{6,14},{7,15},{8,0},{9,1},... | collective-permute-start | bytes 1572872 | tf_op jit(solution)/shard_map/ppermute | solution.py:31
  27.7 3.8 %collective-permute-done.15.refs_3_ = bf16[4,128,384]{2,1,0:T(8,128)(2,1)S(1)} collective-permute-done((bf16[4,128,384]{2,1,0:T(8,128)(2,1)S(1)}, bf16[4,128,384]{2,1,0:T(8,128)(2,1)S(1)}, u32[]{:S(2)}, u32[]{:S(2)}) %collective-permute-start.15) | collective-permute-done | bytes 393248 | tf_op jit(solution)/shard_map/ppermute | solution.py:36
  31.5 10.6 %collective-permute-start.16 = (bf16[4,128,384]{2,1,0:T(8,128)(2,1)S(1)}, bf16[4,128,384]{2,1,0:T(8,128)(2,1)S(1)}, u32[]{:S(2)}, u32[]{:S(2)}) collective-permute-start(bf16[4,128,384]{2,1,0:T(8,128)(2,1)S(1)} %slice.26.refs_0_), channel_id=1, source_target_pairs={{0,1},{1,0},{2,3},{3,2},{4,5},{5,4},{6,7},{7,6},{8,9},{9,8},{10,11... | collective-permute-start | bytes 1179656 | tf_op jit(solution)/shard_map/ppermute | solution.py:31
  47.7 7.3 %collective-permute-done.13.refs_1_ = bf16[4,128,384]{2,1,0:T(8,128)(2,1)} collective-permute-done((bf16[4,128,384]{2,1,0:T(8,128)(2,1)S(1)}, bf16[4,128,384]{2,1,0:T(8,128)(2,1)}, u32[]{:S(2)}, u32[]{:S(2)}) %collective-permute-start.13) | collective-permute-done | bytes 393248 | tf_op jit(solution)/shard_map/ppermute | solution.py:36
  54.9 2.7 %collective-permute-start.6 = (bf16[1024,256]{1,0:T(8,128)(2,1)S(1)}, bf16[1024,256]{1,0:T(8,128)(2,1)S(1)}, u32[]{:S(2)}, u32[]{:S(2)}) collective-permute-start(bf16[1024,256]{1,0:T(8,128)(2,1)S(1)} %collective-permute-done.5.refs_5_), channel_id=1, source_target_pairs={{0,6},{1,7},{2,0},{3,1},{4,2},{5,3},{6,4},{7,5},{8,14},{9,15},{10,... | collective-permute-start | bytes 1572872 | tf_op jit(solution)/shard_map/ppermute | solution.py:31
  60.9 2.7 %collective-permute-start.7 = (bf16[1024,128]{1,0:T(8,128)(2,1)}, bf16[1024,128]{1,0:T(8,128)(2,1)}, u32[]{:S(2)}, u32[]{:S(2)}) collective-permute-start(bf16[1024,128]{1,0:T(8,128)(2,1)} %collective-permute-done.3.refs_2_), channel_id=1, source_target_pairs={{0,8},{1,9},{2,10},{3,11},{4,12},{5,13},{6,14},{7,15},{8,0},{9,1},... | collective-permute-start | bytes 786440 | tf_op jit(solution)/shard_map/ppermute | solution.py:31
  63.6 10.3 %collective-permute-done.4.refs_3_ = bf16[1024,128]{1,0:T(8,128)(2,1)} collective-permute-done((bf16[1024,128]{1,0:T(8,128)(2,1)S(1)}, bf16[1024,128]{1,0:T(8,128)(2,1)}, u32[]{:S(2)}, u32[]{:S(2)}) %collective-permute-start.4) | collective-permute-done | bytes 262176 | tf_op jit(solution)/shard_map/ppermute | solution.py:31
  73.9 2.7 %collective-permute-start.8 = (bf16[1024,128]{1,0:T(8,128)(2,1)}, bf16[1024,128]{1,0:T(8,128)(2,1)}, u32[]{:S(2)}, u32[]{:S(2)}) collective-permute-start(bf16[1024,128]{1,0:T(8,128)(2,1)} %collective-permute-done.4.refs_3_), channel_id=1, source_target_pairs={{0,8},{1,9},{2,10},{3,11},{4,12},{5,13},{6,14},{7,15},{8,0},{9,1},... | collective-permute-start | bytes 786440 | tf_op jit(solution)/shard_map/ppermute | solution.py:31
  83.2 2.4 %shard_map.46 = (f32[1024,1]{1,0:T(8,128)S(1)}, f32[1024,1]{1,0:T(8,128)S(1)}) custom-call(bf16[1024,256]{1,0:T(8,128)(2,1)S(1)} %maximum_select_fusion.refs_0_.x_ref, bf16[1024,256]{1,0:T(8,128)(2,1)S(1)} %collective-permute-done.1.refs_1_, bf16[1024,128]{1,0:T(8,128)(2,1)} %collective-permute-done.3.refs_2_, ...), custom_call_target="tpu_custom_call" | custom-call | flops 1073741824 | bytes 1048576 | tf_op jit(solution)/shard_map/pallas_call | solution.py:309
  85.7 7.8 %shard_map.48.refs_0_ = bf16[16,2,64,384]{3,2,1,0:T(8,128)(2,1)} custom-call(s32[5]{0:T(128)S(1)} %stack.38.place, f32[8,256]{1,0:T(8,128)S(1)} %reshape.9.gain_ref, f32[1024,1]{1,0:T(8,128)S(1)} %get-tuple-element.19.early_mean_ref, f32[1024,1]{1,0:T(8,128)S(1)} %get-tuple-element.20.early_square_ref, ...), custom_call_target="tpu_custom_call" | custom-call | tf_op jit(solution)/shard_map/pallas_call | solution.py:309
  93.5 9.9 %all-to-all-start = ((bf16[32,64,384]{2,1,0:T(8,128)(2,1)}), bf16[32,64,384]{2,1,0:T(8,128)(2,1)S(1)}, u32[]{:S(2)}, u32[]{:S(2)}) async-start(bf16[32,64,384]{2,1,0:T(8,128)(2,1)} %bitcast.9), calls=%async_computation | async-start | bytes 3145728 | tf_op jit(solution)/shard_map/all_to_all | solution.py:324
  103.5 2.6 %collective-permute-start.22 = (bf16[4,128,128]{2,1,0:T(8,128)(2,1)S(1)}, bf16[4,128,128]{2,1,0:T(8,128)(2,1)S(1)}, u32[]{:S(2)}, u32[]{:S(2)}) collective-permute-start(bf16[4,128,128]{2,1,0:T(8,128)(2,1)S(1)} %pad_maximum_fusion.2.refs_0_), channel_id=1, source_target_pairs={{0,48},{16,0},{32,16},{48,32},{64,112},{80,64},{96,80},{112,96},{1... | collective-permute-start | bytes 393224 | tf_op jit(solution)/shard_map/ppermute | solution.py:36
  107.3 6.8 %collective-permute-done.22.refs_3_ = bf16[4,128,128]{2,1,0:T(8,128)(2,1)S(1)} collective-permute-done((bf16[4,128,128]{2,1,0:T(8,128)(2,1)S(1)}, bf16[4,128,128]{2,1,0:T(8,128)(2,1)S(1)}, u32[]{:S(2)}, u32[]{:S(2)}) %collective-permute-start.22) | collective-permute-done | bytes 131104 | tf_op jit(solution)/shard_map/ppermute | solution.py:36
  115.1 3.0 %collective-permute-done.20.refs_1_ = bf16[4,128,128]{2,1,0:T(8,128)(2,1)S(1)} collective-permute-done((bf16[4,128,128]{2,1,0:T(8,128)(2,1)S(1)}, bf16[4,128,128]{2,1,0:T(8,128)(2,1)S(1)}, u32[]{:S(2)}, u32[]{:S(2)}) %collective-permute-start.20) | collective-permute-done | bytes 131104 | tf_op jit(solution)/shard_map/ppermute | solution.py:36
  119.8 3.1 %shard_map.50 = (f32[1024,128]{1,0:T(8,128)S(1)}, f32[64,128]{1,0:T(8,128)S(1)}) custom-call(bf16[16,2,64,384]{3,2,1,0:T(8,128)(2,1)} %shard_map.48.refs_0_), custom_call_target="tpu_custom_call" | custom-call | flops 8589934592 | bytes 1048576 | tf_op jit(solution)/shard_map/pallas_call | solution.py:309
  123.9 19.1 %all-to-all-done.z_ref = bf16[32,64,384]{2,1,0:T(8,128)(2,1)S(1)} async-done(((bf16[32,64,384]{2,1,0:T(8,128)(2,1)}), bf16[32,64,384]{2,1,0:T(8,128)(2,1)S(1)}, u32[]{:S(2)}, u32[]{:S(2)}) %all-to-all-start) | async-done | bytes 1572896 | tf_op jit(solution)/shard_map/all_to_all | solution.py:324
  145.8 6.1 %all-to-all-start.1 = ((bf16[32,72,128]{2,1,0:T(8,128)(2,1)}), bf16[32,72,128]{2,1,0:T(8,128)(2,1)S(1)}, u32[]{:S(2)}, u32[]{:S(2)}) async-start(bf16[32,72,128]{2,1,0:T(8,128)(2,1)} %copy-done), calls=%async_computation.1 | async-start | bytes 1179648 | tf_op jit(solution)/shard_map/all_to_all | solution.py:324
  152.0 3.2 %shard_map.51 = (f32[1024,128]{1,0:T(8,128)S(1)}, f32[64,128]{1,0:T(8,128)S(1)}) custom-call(bf16[16,2,64,384]{3,2,1,0:T(8,128)(2,1)} %shard_map.48.refs_0_), custom_call_target="tpu_custom_call" | custom-call | flops 8589934592 | bytes 1048576 | tf_op jit(solution)/shard_map/pallas_call | solution.py:309
  155.2 14.5 %all-to-all-done.1 = bf16[32,72,128]{2,1,0:T(8,128)(2,1)S(1)} async-done(((bf16[32,72,128]{2,1,0:T(8,128)(2,1)}), bf16[32,72,128]{2,1,0:T(8,128)(2,1)S(1)}, u32[]{:S(2)}, u32[]{:S(2)}) %all-to-all-start.1) | async-done | bytes 589856 | tf_op jit(solution)/shard_map/all_to_all | solution.py:324
  171.6 2.8 %collective-permute-start.24 = (bf16[1024,256]{1,0:T(8,128)(2,1)S(1)}, bf16[1024,256]{1,0:T(8,128)(2,1)S(1)}, u32[]{:S(2)}, u32[]{:S(2)}) collective-permute-start(bf16[1024,256]{1,0:T(8,128)(2,1)S(1)} %shard_map.53.refs_0_), channel_id=1, source_target_pairs={{0,6},{1,7},{2,0},{3,1},{4,2},{5,3},{6,4},{7,5},{8,14},{9,15},{10,... | collective-permute-start | bytes 1572872 | tf_op jit(solution)/shard_map/ppermute | solution.py:31
  174.5 12.1 %collective-permute-done.25.refs_4_ = bf16[1024,256]{1,0:T(8,128)(2,1)S(1)} collective-permute-done((bf16[1024,256]{1,0:T(8,128)(2,1)S(1)}, bf16[1024,256]{1,0:T(8,128)(2,1)S(1)}, u32[]{:S(2)}, u32[]{:S(2)}) %collective-permute-start.25) | collective-permute-done | bytes 524320 | tf_op jit(solution)/shard_map/ppermute | solution.py:31
  186.8 2.7 %collective-permute-start.29 = (bf16[1024,256]{1,0:T(8,128)(2,1)S(1)}, bf16[1024,256]{1,0:T(8,128)(2,1)S(1)}, u32[]{:S(2)}, u32[]{:S(2)}) collective-permute-start(bf16[1024,256]{1,0:T(8,128)(2,1)S(1)} %collective-permute-done.28.refs_5_), channel_id=1, source_target_pairs={{0,6},{1,7},{2,0},{3,1},{4,2},{5,3},{6,4},{7,5},{8,14},{9,15},{10,... | collective-permute-start | bytes 1572872 | tf_op jit(solution)/shard_map/ppermute | solution.py:31
  190.9 4.2 %collective-permute-done.26.refs_2_ = bf16[1024,128]{1,0:T(8,128)(2,1)S(1)} collective-permute-done((bf16[1024,128]{1,0:T(8,128)(2,1)S(1)}, bf16[1024,128]{1,0:T(8,128)(2,1)S(1)}, u32[]{:S(2)}, u32[]{:S(2)}) %collective-permute-start.26) | collective-permute-done | bytes 262176 | tf_op jit(solution)/shard_map/ppermute | solution.py:31
  195.1 10.3 %collective-permute-done.27.refs_3_ = bf16[1024,128]{1,0:T(8,128)(2,1)S(1)} collective-permute-done((bf16[1024,128]{1,0:T(8,128)(2,1)S(1)}, bf16[1024,128]{1,0:T(8,128)(2,1)S(1)}, u32[]{:S(2)}, u32[]{:S(2)}) %collective-permute-start.27) | collective-permute-done | bytes 262176 | tf_op jit(solution)/shard_map/ppermute | solution.py:31
  206.4 5.2 %collective-permute-done.31.refs_8_ = bf16[1024,128]{1,0:T(8,128)(2,1)S(1)} collective-permute-done((bf16[1024,128]{1,0:T(8,128)(2,1)S(1)}, bf16[1024,128]{1,0:T(8,128)(2,1)S(1)}, u32[]{:S(2)}, u32[]{:S(2)}) %collective-permute-start.31) | collective-permute-done | bytes 262176 | tf_op jit(solution)/shard_map/ppermute | solution.py:31
  211.6 2.6 %shard_map.54 = (bf16[2048,128]{1,0:T(8,128)(2,1)}, bf16[1024,128]{1,0:T(8,128)(2,1)S(1)}) custom-call(s32[5]{0:T(128)S(1)} %stack.38.place, bf16[1024,256]{1,0:T(8,128)(2,1)S(1)} %maximum_select_fusion.refs_0_.x_ref, bf16[1024,256]{1,0:T(8,128)(2,1)S(1)} %shard_map.53.refs_0_, bf16[1024,256]{1,0:T(8,128)(2,1)S(1)} %collective-permute-done.24.refs_1_, ...), custom_call_target="tpu_custom_call" | custom-call | tf_op jit(solution)/shard_map/pallas_call | solution.py:309
  214.2 2.6 %collective-permute-start.33 = (bf16[1024,128]{1,0:T(8,128)(2,1)S(1)}, bf16[1024,128]{1,0:T(8,128)(2,1)S(1)}, u32[]{:S(2)}, u32[]{:S(2)}) collective-permute-start(bf16[1024,128]{1,0:T(8,128)(2,1)S(1)} %get-tuple-element.32), channel_id=1, source_target_pairs={{0,1},{1,0},{2,3},{3,2},{4,5},{5,4},{6,7},{7,6},{8,9},{9,8},{10,11... | collective-permute-start | bytes 786440 | tf_op jit(solution)/shard_map/ppermute | solution.py:31
  (107 shorter events, 36.5 us)
Async XLA Ops:
  1.1 11.9 %collective-permute-start = (bf16[1024,128]{1,0:T(8,128)(2,1)S(1)}, bf16[1024,128]{1,0:T(8,128)(2,1)S(1)}, u32[]{:S(2)}, u32[]{:S(2)}) collective-permute-start(bf16[1024,128]{1,0:T(8,128)(2,1)S(1)} %get-tuple-element.34), channel_id=1, source_target_pairs={{0,1},{1,0},{2,3},{3,2},{4,5},{5,4},{6,7},{7,6},{8,9},{9,8},{10,11... | collective-permute-start | bytes 786440 | tf_op jit(solution)/shard_map/ppermute | solution.py:31
  5.3 10.7 %collective-permute-start.12 = (bf16[128,512]{1,0:T(8,128)(2,1)S(1)}, bf16[128,512]{1,0:T(8,128)(2,1)S(1)}, u32[]{:S(2)}, u32[]{:S(2)}) collective-permute-start(bf16[128,512]{1,0:T(8,128)(2,1)S(1)} %pad_maximum_fusion.3), channel_id=1, source_target_pairs={{0,192},{16,208},{32,224},{48,240},{64,0},{80,16},{96,32},{112,48}... | collective-permute-start | bytes 393224 | tf_op jit(solution)/shard_map/ppermute | solution.py:36
  9.7 12.0 %collective-permute-start.11 = (bf16[128,512]{1,0:T(8,128)(2,1)S(1)}, bf16[128,512]{1,0:T(8,128)(2,1)S(1)}, u32[]{:S(2)}, u32[]{:S(2)}) collective-permute-start(bf16[128,512]{1,0:T(8,128)(2,1)S(1)} %pad_maximum_fusion.3), channel_id=1, source_target_pairs={{0,128},{16,144},{32,160},{48,176},{64,192},{80,208},{96,224},{112... | collective-permute-start | bytes 393224 | tf_op jit(solution)/shard_map/ppermute | solution.py:36
  10.7 11.0 %collective-permute-start.10 = (bf16[128,512]{1,0:T(8,128)(2,1)S(1)}, bf16[128,512]{1,0:T(8,128)(2,1)S(1)}, u32[]{:S(2)}, u32[]{:S(2)}) collective-permute-start(bf16[128,512]{1,0:T(8,128)(2,1)S(1)} %pad_maximum_fusion.3), channel_id=1, source_target_pairs={{0,64},{16,80},{32,96},{48,112},{64,128},{80,144},{96,160},{112,17... | collective-permute-start | bytes 393224 | tf_op jit(solution)/shard_map/ppermute | solution.py:36
  13.1 28.9 %collective-permute-start.2 = (bf16[1024,256]{1,0:T(8,128)(2,1)S(1)}, bf16[1024,256]{1,0:T(8,128)(2,1)S(1)}, u32[]{:S(2)}, u32[]{:S(2)}) collective-permute-start(bf16[1024,256]{1,0:T(8,128)(2,1)S(1)} %maximum_select_fusion.refs_0_.x_ref), channel_id=1, source_target_pairs={{0,2},{1,3},{2,4},{3,5},{4,6},{5,7},{6,0},{7,1},{8,10},{9,11},{10,... | collective-permute-start | bytes 1572872 | tf_op jit(solution)/shard_map/ppermute | solution.py:31
  14.5 29.6 %collective-permute-start.1 = (bf16[1024,256]{1,0:T(8,128)(2,1)S(1)}, bf16[1024,256]{1,0:T(8,128)(2,1)S(1)}, u32[]{:S(2)}, u32[]{:S(2)}) collective-permute-start(bf16[1024,256]{1,0:T(8,128)(2,1)S(1)} %maximum_select_fusion.refs_0_.x_ref), channel_id=1, source_target_pairs={{0,6},{1,7},{2,0},{3,1},{4,2},{5,3},{6,4},{7,5},{8,14},{9,15},{10,... | collective-permute-start | bytes 1572872 | tf_op jit(solution)/shard_map/ppermute | solution.py:31
  21.9 9.6 %collective-permute-start.15 = (bf16[4,128,384]{2,1,0:T(8,128)(2,1)S(1)}, bf16[4,128,384]{2,1,0:T(8,128)(2,1)S(1)}, u32[]{:S(2)}, u32[]{:S(2)}) collective-permute-start(bf16[4,128,384]{2,1,0:T(8,128)(2,1)S(1)} %slice.26.refs_0_), channel_id=1, source_target_pairs={{0,48},{16,0},{32,16},{48,32},{64,112},{80,64},{96,80},{112,96},{1... | collective-permute-start | bytes 1179656 | tf_op jit(solution)/shard_map/ppermute | solution.py:36
  24.3 17.8 %collective-permute-start.14 = (bf16[4,128,384]{2,1,0:T(8,128)(2,1)S(1)}, bf16[4,128,384]{2,1,0:T(8,128)(2,1)S(1)}, u32[]{:S(2)}, u32[]{:S(2)}) collective-permute-start(bf16[4,128,384]{2,1,0:T(8,128)(2,1)S(1)} %slice.26.refs_0_), channel_id=1, source_target_pairs={{0,32},{16,48},{32,0},{48,16},{64,96},{80,112},{96,64},{112,80},{1... | collective-permute-start | bytes 1179656 | tf_op jit(solution)/shard_map/ppermute | solution.py:36
  25.0 21.3 %collective-permute-start.5 = (bf16[1024,256]{1,0:T(8,128)(2,1)S(1)}, bf16[1024,256]{1,0:T(8,128)(2,1)S(1)}, u32[]{:S(2)}, u32[]{:S(2)}) collective-permute-start(bf16[1024,256]{1,0:T(8,128)(2,1)S(1)} %maximum_select_fusion.refs_0_.x_ref), channel_id=1, source_target_pairs={{0,8},{1,9},{2,10},{3,11},{4,12},{5,13},{6,14},{7,15},{8,0},{9,1},... | collective-permute-start | bytes 1572872 | tf_op jit(solution)/shard_map/ppermute | solution.py:31
  31.5 12.9 %collective-permute-start.16 = (bf16[4,128,384]{2,1,0:T(8,128)(2,1)S(1)}, bf16[4,128,384]{2,1,0:T(8,128)(2,1)S(1)}, u32[]{:S(2)}, u32[]{:S(2)}) collective-permute-start(bf16[4,128,384]{2,1,0:T(8,128)(2,1)S(1)} %slice.26.refs_0_), channel_id=1, source_target_pairs={{0,1},{1,0},{2,3},{3,2},{4,5},{5,4},{6,7},{7,6},{8,9},{9,8},{10,11... | collective-permute-start | bytes 1179656 | tf_op jit(solution)/shard_map/ppermute | solution.py:31
  42.1 12.9 %collective-permute-start.13 = (bf16[4,128,384]{2,1,0:T(8,128)(2,1)S(1)}, bf16[4,128,384]{2,1,0:T(8,128)(2,1)}, u32[]{:S(2)}, u32[]{:S(2)}) collective-permute-start(bf16[4,128,384]{2,1,0:T(8,128)(2,1)S(1)} %slice.26.refs_0_), channel_id=1, source_target_pairs={{0,16},{16,32},{32,48},{48,0},{64,80},{80,96},{96,112},{112,64},{1... | collective-permute-start | bytes 1179656 | tf_op jit(solution)/shard_map/ppermute | solution.py:36
  42.1 15.6 %collective-permute-start.19 = (bf16[4,128,384]{2,1,0:T(8,128)(2,1)S(1)}, bf16[4,128,384]{2,1,0:T(8,128)(2,1)S(1)}, u32[]{:S(2)}, u32[]{:S(2)}) collective-permute-start(bf16[4,128,384]{2,1,0:T(8,128)(2,1)S(1)} %collective-permute-done.15.refs_3_), channel_id=1, source_target_pairs={{0,1},{1,0},{2,3},{3,2},{4,5},{5,4},{6,7},{7,6},{8,9},{9,8},{10,11... | collective-permute-start | bytes 1179656 | tf_op jit(solution)/shard_map/ppermute | solution.py:31
  44.2 14.7 %collective-permute-start.18 = (bf16[4,128,384]{2,1,0:T(8,128)(2,1)S(1)}, bf16[4,128,384]{2,1,0:T(8,128)(2,1)S(1)}, u32[]{:S(2)}, u32[]{:S(2)}) collective-permute-start(bf16[4,128,384]{2,1,0:T(8,128)(2,1)S(1)} %collective-permute-done.14.refs_2_), channel_id=1, source_target_pairs={{0,1},{1,0},{2,3},{3,2},{4,5},{5,4},{6,7},{7,6},{8,9},{9,8},{10,11... | collective-permute-start | bytes 1179656 | tf_op jit(solution)/shard_map/ppermute | solution.py:31
  45.1 15.8 %collective-permute-start.3 = (bf16[1024,128]{1,0:T(8,128)(2,1)S(1)}, bf16[1024,128]{1,0:T(8,128)(2,1)}, u32[]{:S(2)}, u32[]{:S(2)}) collective-permute-start(bf16[1024,128]{1,0:T(8,128)(2,1)S(1)} %slice.24), channel_id=1, source_target_pairs={{0,2},{1,3},{2,4},{3,5},{4,6},{5,7},{6,0},{7,1},{8,10},{9,11},{10,... | collective-permute-start | bytes 786440 | tf_op jit(solution)/shard_map/ppermute | solution.py:31
  46.4 39.3 %collective-permute-start.9 = (bf16[1024,256]{1,0:T(8,128)(2,1)S(1)}, bf16[1024,256]{1,0:T(8,128)(2,1)S(1)}, u32[]{:S(2)}, u32[]{:S(2)}) collective-permute-start(bf16[1024,256]{1,0:T(8,128)(2,1)S(1)} %collective-permute-done.5.refs_5_), channel_id=1, source_target_pairs={{0,2},{1,3},{2,4},{3,5},{4,6},{5,7},{6,0},{7,1},{8,10},{9,11},{10,... | collective-permute-start | bytes 1572872 | tf_op jit(solution)/shard_map/ppermute | solution.py:31
  54.9 30.7 %collective-permute-start.6 = (bf16[1024,256]{1,0:T(8,128)(2,1)S(1)}, bf16[1024,256]{1,0:T(8,128)(2,1)S(1)}, u32[]{:S(2)}, u32[]{:S(2)}) collective-permute-start(bf16[1024,256]{1,0:T(8,128)(2,1)S(1)} %collective-permute-done.5.refs_5_), channel_id=1, source_target_pairs={{0,6},{1,7},{2,0},{3,1},{4,2},{5,3},{6,4},{7,5},{8,14},{9,15},{10,... | collective-permute-start | bytes 1572872 | tf_op jit(solution)/shard_map/ppermute | solution.py:31
  58.4 15.5 %collective-permute-start.4 = (bf16[1024,128]{1,0:T(8,128)(2,1)S(1)}, bf16[1024,128]{1,0:T(8,128)(2,1)}, u32[]{:S(2)}, u32[]{:S(2)}) collective-permute-start(bf16[1024,128]{1,0:T(8,128)(2,1)S(1)} %slice.25), channel_id=1, source_target_pairs={{0,6},{1,7},{2,0},{3,1},{4,2},{5,3},{6,4},{7,5},{8,14},{9,15},{10,... | collective-permute-start | bytes 786440 | tf_op jit(solution)/shard_map/ppermute | solution.py:31
  59.7 17.0 %collective-permute-start.17 = (bf16[4,128,384]{2,1,0:T(8,128)(2,1)}, bf16[4,128,384]{2,1,0:T(8,128)(2,1)}, u32[]{:S(2)}, u32[]{:S(2)}) collective-permute-start(bf16[4,128,384]{2,1,0:T(8,128)(2,1)} %collective-permute-done.13.refs_1_), channel_id=1, source_target_pairs={{0,1},{1,0},{2,3},{3,2},{4,5},{5,4},{6,7},{7,6},{8,9},{9,8},{10,11... | collective-permute-start | bytes 1179656 | tf_op jit(solution)/shard_map/ppermute | solution.py:31
  60.9 24.7 %collective-permute-start.7 = (bf16[1024,128]{1,0:T(8,128)(2,1)}, bf16[1024,128]{1,0:T(8,128)(2,1)}, u32[]{:S(2)}, u32[]{:S(2)}) collective-permute-start(bf16[1024,128]{1,0:T(8,128)(2,1)} %collective-permute-done.3.refs_2_), channel_id=1, source_target_pairs={{0,8},{1,9},{2,10},{3,11},{4,12},{5,13},{6,14},{7,15},{8,0},{9,1},... | collective-permute-start | bytes 786440 | tf_op jit(solution)/shard_map/ppermute | solution.py:31
  73.9 11.8 %collective-permute-start.8 = (bf16[1024,128]{1,0:T(8,128)(2,1)}, bf16[1024,128]{1,0:T(8,128)(2,1)}, u32[]{:S(2)}, u32[]{:S(2)}) collective-permute-start(bf16[1024,128]{1,0:T(8,128)(2,1)} %collective-permute-done.4.refs_3_), channel_id=1, source_target_pairs={{0,8},{1,9},{2,10},{3,11},{4,12},{5,13},{6,14},{7,15},{8,0},{9,1},... | collective-permute-start | bytes 786440 | tf_op jit(solution)/shard_map/ppermute | solution.py:31
  93.5 49.5 %all-to-all-start = ((bf16[32,64,384]{2,1,0:T(8,128)(2,1)}), bf16[32,64,384]{2,1,0:T(8,128)(2,1)S(1)}, u32[]{:S(2)}, u32[]{:S(2)}) async-start(bf16[32,64,384]{2,1,0:T(8,128)(2,1)} %bitcast.9), calls=%async_computation | async-start | bytes 3145728 | tf_op jit(solution)/shard_map/all_to_all | solution.py:324
  103.5 10.6 %collective-permute-start.22 = (bf16[4,128,128]{2,1,0:T(8,128)(2,1)S(1)}, bf16[4,128,128]{2,1,0:T(8,128)(2,1)S(1)}, u32[]{:S(2)}, u32[]{:S(2)}) collective-permute-start(bf16[4,128,128]{2,1,0:T(8,128)(2,1)S(1)} %pad_maximum_fusion.2.refs_0_), channel_id=1, source_target_pairs={{0,48},{16,0},{32,16},{48,32},{64,112},{80,64},{96,80},{112,96},{1... | collective-permute-start | bytes 393224 | tf_op jit(solution)/shard_map/ppermute | solution.py:36
  106.1 9.0 %collective-permute-start.21 = (bf16[4,128,128]{2,1,0:T(8,128)(2,1)S(1)}, bf16[4,128,128]{2,1,0:T(8,128)(2,1)S(1)}, u32[]{:S(2)}, u32[]{:S(2)}) collective-permute-start(bf16[4,128,128]{2,1,0:T(8,128)(2,1)S(1)} %pad_maximum_fusion.2.refs_0_), channel_id=1, source_target_pairs={{0,32},{16,48},{32,0},{48,16},{64,96},{80,112},{96,64},{112,80},{1... | collective-permute-start | bytes 393224 | tf_op jit(solution)/shard_map/ppermute | solution.py:36
  106.7 11.4 %collective-permute-start.20 = (bf16[4,128,128]{2,1,0:T(8,128)(2,1)S(1)}, bf16[4,128,128]{2,1,0:T(8,128)(2,1)S(1)}, u32[]{:S(2)}, u32[]{:S(2)}) collective-permute-start(bf16[4,128,128]{2,1,0:T(8,128)(2,1)S(1)} %pad_maximum_fusion.2.refs_0_), channel_id=1, source_target_pairs={{0,16},{16,32},{32,48},{48,0},{64,80},{80,96},{96,112},{112,64},{1... | collective-permute-start | bytes 393224 | tf_op jit(solution)/shard_map/ppermute | solution.py:36
  145.8 23.9 %all-to-all-start.1 = ((bf16[32,72,128]{2,1,0:T(8,128)(2,1)}), bf16[32,72,128]{2,1,0:T(8,128)(2,1)S(1)}, u32[]{:S(2)}, u32[]{:S(2)}) async-start(bf16[32,72,128]{2,1,0:T(8,128)(2,1)} %copy-done), calls=%async_computation.1 | async-start | bytes 1179648 | tf_op jit(solution)/shard_map/all_to_all | solution.py:324
  170.7 15.9 %collective-permute-start.25 = (bf16[1024,256]{1,0:T(8,128)(2,1)S(1)}, bf16[1024,256]{1,0:T(8,128)(2,1)S(1)}, u32[]{:S(2)}, u32[]{:S(2)}) collective-permute-start(bf16[1024,256]{1,0:T(8,128)(2,1)S(1)} %shard_map.53.refs_0_), channel_id=1, source_target_pairs={{0,2},{1,3},{2,4},{3,5},{4,6},{5,7},{6,0},{7,1},{8,10},{9,11},{10,... | collective-permute-start | bytes 1572872 | tf_op jit(solution)/shard_map/ppermute | solution.py:31
  171.6 15.0 %collective-permute-start.28 = (bf16[1024,256]{1,0:T(8,128)(2,1)S(1)}, bf16[1024,256]{1,0:T(8,128)(2,1)S(1)}, u32[]{:S(2)}, u32[]{:S(2)}) collective-permute-start(bf16[1024,256]{1,0:T(8,128)(2,1)S(1)} %shard_map.53.refs_0_), channel_id=1, source_target_pairs={{0,8},{1,9},{2,10},{3,11},{4,12},{5,13},{6,14},{7,15},{8,0},{9,1},... | collective-permute-start | bytes 1572872 | tf_op jit(solution)/shard_map/ppermute | solution.py:31
  171.6 17.8 %collective-permute-start.24 = (bf16[1024,256]{1,0:T(8,128)(2,1)S(1)}, bf16[1024,256]{1,0:T(8,128)(2,1)S(1)}, u32[]{:S(2)}, u32[]{:S(2)}) collective-permute-start(bf16[1024,256]{1,0:T(8,128)(2,1)S(1)} %shard_map.53.refs_0_), channel_id=1, source_target_pairs={{0,6},{1,7},{2,0},{3,1},{4,2},{5,3},{6,4},{7,5},{8,14},{9,15},{10,... | collective-permute-start | bytes 1572872 | tf_op jit(solution)/shard_map/ppermute | solution.py:31
  186.7 19.7 %collective-permute-start.32 = (bf16[1024,256]{1,0:T(8,128)(2,1)S(1)}, bf16[1024,256]{1,0:T(8,128)(2,1)S(1)}, u32[]{:S(2)}, u32[]{:S(2)}) collective-permute-start(bf16[1024,256]{1,0:T(8,128)(2,1)S(1)} %collective-permute-done.28.refs_5_), channel_id=1, source_target_pairs={{0,2},{1,3},{2,4},{3,5},{4,6},{5,7},{6,0},{7,1},{8,10},{9,11},{10,... | collective-permute-start | bytes 1572872 | tf_op jit(solution)/shard_map/ppermute | solution.py:31
  186.8 19.6 %collective-permute-start.29 = (bf16[1024,256]{1,0:T(8,128)(2,1)S(1)}, bf16[1024,256]{1,0:T(8,128)(2,1)S(1)}, u32[]{:S(2)}, u32[]{:S(2)}) collective-permute-start(bf16[1024,256]{1,0:T(8,128)(2,1)S(1)} %collective-permute-done.28.refs_5_), channel_id=1, source_target_pairs={{0,6},{1,7},{2,0},{3,1},{4,2},{5,3},{6,4},{7,5},{8,14},{9,15},{10,... | collective-permute-start | bytes 1572872 | tf_op jit(solution)/shard_map/ppermute | solution.py:31
  189.5 16.0 %collective-permute-start.27 = (bf16[1024,128]{1,0:T(8,128)(2,1)S(1)}, bf16[1024,128]{1,0:T(8,128)(2,1)S(1)}, u32[]{:S(2)}, u32[]{:S(2)}) collective-permute-start(bf16[1024,128]{1,0:T(8,128)(2,1)S(1)} %slice.28), channel_id=1, source_target_pairs={{0,6},{1,7},{2,0},{3,1},{4,2},{5,3},{6,4},{7,5},{8,14},{9,15},{10,... | collective-permute-start | bytes 786440 | tf_op jit(solution)/shard_map/ppermute | solution.py:31
  195.1 11.2 %collective-permute-start.30 = (bf16[1024,128]{1,0:T(8,128)(2,1)S(1)}, bf16[1024,128]{1,0:T(8,128)(2,1)S(1)}, u32[]{:S(2)}, u32[]{:S(2)}) collective-permute-start(bf16[1024,128]{1,0:T(8,128)(2,1)S(1)} %collective-permute-done.26.refs_2_), channel_id=1, source_target_pairs={{0,8},{1,9},{2,10},{3,11},{4,12},{5,13},{6,14},{7,15},{8,0},{9,1},... | collective-permute-start | bytes 786440 | tf_op jit(solution)/shard_map/ppermute | solution.py:31
  (26 other events, 233.9 us)

commit v2 on v1

--- a/solution.py
+++ b/solution.py
@@ -121,18 +121,18 @@
 
 
 def _early_kernel(*refs):
-    chunks = _chunks(refs[:-2])
-    mean_ref, square_ref = refs[-2:]
+    chunks = _chunks(refs[:-1])
+    out_ref = refs[-1]
 
     def step(tile, carry):
         rows = pl.ds(pl.multiple_of(tile * TILE, TILE), TILE)
-        mean_ref[rows, :], square_ref[rows, :] = _moments(chunks, rows)
+        out_ref[rows, 0:1], out_ref[rows, 1:2] = _moments(chunks, rows)
         return carry
 
     lax.fori_loop(0, COLS // TILE, step, 0)
 
 
-def _qkv_kernel(place, gain_ref, early_mean_ref, early_square_ref, *refs):
+def _qkv_kernel(place, gain_ref, early_ref, *refs):
     pieces, (w_ref, out_ref, even_ref, odd_ref) = refs[:10], refs[10:]
     zl, y, core = place[0], place[1], place[4]
     gains = []
@@ -157,9 +157,9 @@
         return _moments(late, rows_of(tile))
 
     def together(tile, late_mean, late_square):
-        mean = early_mean_ref[rows_of(tile), :]
+        mean = early_ref[rows_of(tile), 0:1]
         apart = late_mean - mean
-        square = early_square_ref[rows_of(tile), :] + late_square
+        square = early_ref[rows_of(tile), 1:2] + late_square
         square += apart * apart * (EARLY_WIDTH * LATE_WIDTH / wide)
         return mean + apart * (LATE_WIDTH / wide), lax.rsqrt(square * (1.0 / wide) + EPSILON)
 
@@ -344,15 +344,13 @@
     own = over_x(weights[..., : 3 * HS])
     other = (core_swap(t) for t in own)
     w = _call(_weights_kernel, shape((2048, 6 * HS), BF16), place, *own, *other, scalars=1)
-    moments = _call(
-        _early_kernel, (shape((COLS, 1), F32), shape((COLS, 1), F32)), *(pieces[i] for i in EARLY), flops=1 << 30
-    )
+    moments = _call(_early_kernel, shape((COLS, 2), F32), *(pieces[i] for i in EARLY), flops=1 << 30)
     qkv = _call(
         _qkv_kernel,
         shape((16, 2, 64, 3 * HS), BF16),
         place,
         norm_gain.reshape(8, 256),
-        *moments,
+        moments,
         *pieces,
         w,
         scalars=1,

time: 219 us -> 219 us (level)
  no operation moved by 1% of the time
where the time goes in v2:
time: 219 us
  waiting for transfers between devices  105 us (48%)
  starting transfers between devices  76.2 us (35%)
  Pallas kernels  24.7 us (11%)
  local copies, waits for them, and re-layouts  10.9 us (5%)
    ppermute x25, starting transfers between devices, _over_col(): return lax.ppermute(x, 'col', pairs)  45.8 us
    ppermute x25, waiting for transfers between devices, _over_col(): return lax.ppermute(x, 'col', pairs)  44.2 us
    all_to_all x2, waiting for transfers between devices, exchange_columns(): lax.all_to_all(x, ('row', 'col'), split_axis=0, concat_axis=0, axis_index...  33.3 us
    ppermute x9, waiting for transfers between devices, _over_row(): return lax.ppermute(x, 'row', pairs)  27.6 us
    pallas_call x9, Pallas kernels, _call(): pl.pallas_call(kernel, out_shape=out, in_specs=[smem] * scalars + [vmem]...  24.7 us
    all_to_all x2, starting transfers between devices, exchange_columns(): lax.all_to_all(x, ('row', 'col'), split_axis=0, concat_axis=0, axis_index...  15.8 us
    ppermute x9, starting transfers between devices, _over_row(): return lax.ppermute(x, 'row', pairs)  14.6 us
    unnamed x44, local copies, waits for them, and re-layouts  8.9 us
  transfers between devices with their start and end apart: 36, of which 15 were waited for; matrix products, arithmetic and copies ran while one was open for 1% of the time, Pallas kernels for 5%

profile of v2, /device:TPU:1, one launch (start us, length us, event | category | flops | bytes accessed | tf_op | source)
XLA Modules:
  0.0 218.6 jit_solution(16203073715945783253)
XLA Ops:
  1.1 3.3 %collective-permute-start = (bf16[1024,128]{1,0:T(8,128)(2,1)S(1)}, bf16[1024,128]{1,0:T(8,128)(2,1)S(1)}, u32[]{:S(2)}, u32[]{:S(2)}) collective-permute-start(bf16[1024,128]{1,0:T(8,128)(2,1)S(1)} %get-tuple-element.30), channel_id=1, source_target_pairs={{0,1},{1,0},{2,3},{3,2},{4,5},{5,4},{6,7},{7,6},{8,9},{9,8},{10,11... | collective-permute-start | bytes 786440 | tf_op jit(solution)/shard_map/ppermute | solution.py:31
  5.3 4.4 %collective-permute-start.12 = (bf16[128,512]{1,0:T(8,128)(2,1)S(1)}, bf16[128,512]{1,0:T(8,128)(2,1)S(1)}, u32[]{:S(2)}, u32[]{:S(2)}) collective-permute-start(bf16[128,512]{1,0:T(8,128)(2,1)S(1)} %pad_maximum_fusion.3), channel_id=1, source_target_pairs={{0,192},{16,208},{32,224},{48,240},{64,0},{80,16},{96,32},{112,48}... | collective-permute-start | bytes 393224 | tf_op jit(solution)/shard_map/ppermute | solution.py:36
  10.7 2.3 %collective-permute-start.10 = (bf16[128,512]{1,0:T(8,128)(2,1)S(1)}, bf16[128,512]{1,0:T(8,128)(2,1)S(1)}, u32[]{:S(2)}, u32[]{:S(2)}) collective-permute-start(bf16[128,512]{1,0:T(8,128)(2,1)S(1)} %pad_maximum_fusion.3), channel_id=1, source_target_pairs={{0,64},{16,80},{32,96},{48,112},{64,128},{80,144},{96,160},{112,17... | collective-permute-start | bytes 393224 | tf_op jit(solution)/shard_map/ppermute | solution.py:36
  16.1 5.7 %collective-permute-done.11 = bf16[128,512]{1,0:T(8,128)(2,1)S(1)} collective-permute-done((bf16[128,512]{1,0:T(8,128)(2,1)S(1)}, bf16[128,512]{1,0:T(8,128)(2,1)S(1)}, u32[]{:S(2)}, u32[]{:S(2)}) %collective-permute-start.11) | collective-permute-done | bytes 131104 | tf_op jit(solution)/shard_map/ppermute | solution.py:36
  21.9 2.4 %collective-permute-start.15 = (bf16[4,128,384]{2,1,0:T(8,128)(2,1)S(1)}, bf16[4,128,384]{2,1,0:T(8,128)(2,1)S(1)}, u32[]{:S(2)}, u32[]{:S(2)}) collective-permute-start(bf16[4,128,384]{2,1,0:T(8,128)(2,1)S(1)} %slice.26.refs_0_), channel_id=1, source_target_pairs={{0,48},{16,0},{32,16},{48,32},{64,112},{80,64},{96,80},{112,96},{1... | collective-permute-start | bytes 1179656 | tf_op jit(solution)/shard_map/ppermute | solution.py:36
  25.0 2.7 %collective-permute-start.5 = (bf16[1024,256]{1,0:T(8,128)(2,1)S(1)}, bf16[1024,256]{1,0:T(8,128)(2,1)S(1)}, u32[]{:S(2)}, u32[]{:S(2)}) collective-permute-start(bf16[1024,256]{1,0:T(8,128)(2,1)S(1)} %maximum_select_fusion.refs_0_.x_ref), channel_id=1, source_target_pairs={{0,8},{1,9},{2,10},{3,11},{4,12},{5,13},{6,14},{7,15},{8,0},{9,1},... | collective-permute-start | bytes 1572872 | tf_op jit(solution)/shard_map/ppermute | solution.py:31
  27.7 3.8 %collective-permute-done.15.refs_3_ = bf16[4,128,384]{2,1,0:T(8,128)(2,1)S(1)} collective-permute-done((bf16[4,128,384]{2,1,0:T(8,128)(2,1)S(1)}, bf16[4,128,384]{2,1,0:T(8,128)(2,1)S(1)}, u32[]{:S(2)}, u32[]{:S(2)}) %collective-permute-start.15) | collective-permute-done | bytes 393248 | tf_op jit(solution)/shard_map/ppermute | solution.py:36
  31.5 10.6 %collective-permute-start.16 = (bf16[4,128,384]{2,1,0:T(8,128)(2,1)S(1)}, bf16[4,128,384]{2,1,0:T(8,128)(2,1)S(1)}, u32[]{:S(2)}, u32[]{:S(2)}) collective-permute-start(bf16[4,128,384]{2,1,0:T(8,128)(2,1)S(1)} %slice.26.refs_0_), channel_id=1, source_target_pairs={{0,1},{1,0},{2,3},{3,2},{4,5},{5,4},{6,7},{7,6},{8,9},{9,8},{10,11... | collective-permute-start | bytes 1179656 | tf_op jit(solution)/shard_map/ppermute | solution.py:31
  47.7 7.3 %collective-permute-done.13.refs_1_ = bf16[4,128,384]{2,1,0:T(8,128)(2,1)} collective-permute-done((bf16[4,128,384]{2,1,0:T(8,128)(2,1)S(1)}, bf16[4,128,384]{2,1,0:T(8,128)(2,1)}, u32[]{:S(2)}, u32[]{:S(2)}) %collective-permute-start.13) | collective-permute-done | bytes 393248 | tf_op jit(solution)/shard_map/ppermute | solution.py:36
  54.9 2.7 %collective-permute-start.6 = (bf16[1024,256]{1,0:T(8,128)(2,1)S(1)}, bf16[1024,256]{1,0:T(8,128)(2,1)S(1)}, u32[]{:S(2)}, u32[]{:S(2)}) collective-permute-start(bf16[1024,256]{1,0:T(8,128)(2,1)S(1)} %collective-permute-done.5.refs_5_), channel_id=1, source_target_pairs={{0,6},{1,7},{2,0},{3,1},{4,2},{5,3},{6,4},{7,5},{8,14},{9,15},{10,... | collective-permute-start | bytes 1572872 | tf_op jit(solution)/shard_map/ppermute | solution.py:31
  60.9 2.7 %collective-permute-start.7 = (bf16[1024,128]{1,0:T(8,128)(2,1)}, bf16[1024,128]{1,0:T(8,128)(2,1)}, u32[]{:S(2)}, u32[]{:S(2)}) collective-permute-start(bf16[1024,128]{1,0:T(8,128)(2,1)} %collective-permute-done.3.refs_2_), channel_id=1, source_target_pairs={{0,8},{1,9},{2,10},{3,11},{4,12},{5,13},{6,14},{7,15},{8,0},{9,1},... | collective-permute-start | bytes 786440 | tf_op jit(solution)/shard_map/ppermute | solution.py:31
  63.6 10.3 %collective-permute-done.4.refs_3_ = bf16[1024,128]{1,0:T(8,128)(2,1)} collective-permute-done((bf16[1024,128]{1,0:T(8,128)(2,1)S(1)}, bf16[1024,128]{1,0:T(8,128)(2,1)}, u32[]{:S(2)}, u32[]{:S(2)}) %collective-permute-start.4) | collective-permute-done | bytes 262176 | tf_op jit(solution)/shard_map/ppermute | solution.py:31
  73.9 2.7 %collective-permute-start.8 = (bf16[1024,128]{1,0:T(8,128)(2,1)}, bf16[1024,128]{1,0:T(8,128)(2,1)}, u32[]{:S(2)}, u32[]{:S(2)}) collective-permute-start(bf16[1024,128]{1,0:T(8,128)(2,1)} %collective-permute-done.4.refs_3_), channel_id=1, source_target_pairs={{0,8},{1,9},{2,10},{3,11},{4,12},{5,13},{6,14},{7,15},{8,0},{9,1},... | collective-permute-start | bytes 786440 | tf_op jit(solution)/shard_map/ppermute | solution.py:31
  83.2 2.5 %shard_map.46.early_ref = f32[1024,2]{1,0:T(8,128)S(1)} custom-call(bf16[1024,256]{1,0:T(8,128)(2,1)S(1)} %maximum_select_fusion.refs_0_.x_ref, bf16[1024,256]{1,0:T(8,128)(2,1)S(1)} %collective-permute-done.1.refs_1_, bf16[1024,128]{1,0:T(8,128)(2,1)} %collective-permute-done.3.refs_2_, bf16[1024,128]{1,0:T(8,128)(2,1)} %collective-permute-done.4.refs_3_, ...), custom_call_target="tpu_custom_call" | custom-call | flops 1073741824 | bytes 1048576 | tf_op jit(solution)/shard_map/pallas_call | solution.py:309
  85.8 7.9 %shard_map.48.refs_0_ = bf16[16,2,64,384]{3,2,1,0:T(8,128)(2,1)} custom-call(s32[5]{0:T(128)S(1)} %stack.38.place, f32[8,256]{1,0:T(8,128)S(1)} %reshape.9.gain_ref, f32[1024,2]{1,0:T(8,128)S(1)} %shard_map.46.early_ref, bf16[1024,256]{1,0:T(8,128)(2,1)S(1)} %maximum_select_fusion.refs_0_.x_ref, bf16[1024,256]{1,0:T(8,128)(2,1)S(1)} %collective-permute-done.1.refs_1_, ...), custom_call_target="tpu_custom_call" | custom-call | tf_op jit(solution)/shard_map/pallas_call | solution.py:309
  93.7 9.9 %all-to-all-start = ((bf16[32,64,384]{2,1,0:T(8,128)(2,1)}), bf16[32,64,384]{2,1,0:T(8,128)(2,1)S(1)}, u32[]{:S(2)}, u32[]{:S(2)}) async-start(bf16[32,64,384]{2,1,0:T(8,128)(2,1)} %bitcast.9), calls=%async_computation | async-start | bytes 3145728 | tf_op jit(solution)/shard_map/all_to_all | solution.py:324
  103.7 2.6 %collective-permute-start.22 = (bf16[4,128,128]{2,1,0:T(8,128)(2,1)S(1)}, bf16[4,128,128]{2,1,0:T(8,128)(2,1)S(1)}, u32[]{:S(2)}, u32[]{:S(2)}) collective-permute-start(bf16[4,128,128]{2,1,0:T(8,128)(2,1)S(1)} %pad_maximum_fusion.2.refs_0_), channel_id=1, source_target_pairs={{0,48},{16,0},{32,16},{48,32},{64,112},{80,64},{96,80},{112,96},{1... | collective-permute-start | bytes 393224 | tf_op jit(solution)/shard_map/ppermute | solution.py:36
  107.4 6.8 %collective-permute-done.22.refs_3_ = bf16[4,128,128]{2,1,0:T(8,128)(2,1)S(1)} collective-permute-done((bf16[4,128,128]{2,1,0:T(8,128)(2,1)S(1)}, bf16[4,128,128]{2,1,0:T(8,128)(2,1)S(1)}, u32[]{:S(2)}, u32[]{:S(2)}) %collective-permute-start.22) | collective-permute-done | bytes 131104 | tf_op jit(solution)/shard_map/ppermute | solution.py:36
  115.3 3.0 %collective-permute-done.20.refs_1_ = bf16[4,128,128]{2,1,0:T(8,128)(2,1)S(1)} collective-permute-done((bf16[4,128,128]{2,1,0:T(8,128)(2,1)S(1)}, bf16[4,128,128]{2,1,0:T(8,128)(2,1)S(1)}, u32[]{:S(2)}, u32[]{:S(2)}) %collective-permute-start.20) | collective-permute-done | bytes 131104 | tf_op jit(solution)/shard_map/ppermute | solution.py:36
  120.3 3.1 %shard_map.50 = (f32[1024,128]{1,0:T(8,128)S(1)}, f32[64,128]{1,0:T(8,128)S(1)}) custom-call(bf16[16,2,64,384]{3,2,1,0:T(8,128)(2,1)} %shard_map.48.refs_0_), custom_call_target="tpu_custom_call" | custom-call | flops 8589934592 | bytes 1048576 | tf_op jit(solution)/shard_map/pallas_call | solution.py:309
  124.3 18.8 %all-to-all-done.z_ref = bf16[32,64,384]{2,1,0:T(8,128)(2,1)S(1)} async-done(((bf16[32,64,384]{2,1,0:T(8,128)(2,1)}), bf16[32,64,384]{2,1,0:T(8,128)(2,1)S(1)}, u32[]{:S(2)}, u32[]{:S(2)}) %all-to-all-start) | async-done | bytes 1572896 | tf_op jit(solution)/shard_map/all_to_all | solution.py:324
  146.0 5.9 %all-to-all-start.1 = ((bf16[32,72,128]{2,1,0:T(8,128)(2,1)}), bf16[32,72,128]{2,1,0:T(8,128)(2,1)S(1)}, u32[]{:S(2)}, u32[]{:S(2)}) async-start(bf16[32,72,128]{2,1,0:T(8,128)(2,1)} %copy-done), calls=%async_computation.1 | async-start | bytes 1179648 | tf_op jit(solution)/shard_map/all_to_all | solution.py:324
  152.0 3.2 %shard_map.51 = (f32[1024,128]{1,0:T(8,128)S(1)}, f32[64,128]{1,0:T(8,128)S(1)}) custom-call(bf16[16,2,64,384]{3,2,1,0:T(8,128)(2,1)} %shard_map.48.refs_0_), custom_call_target="tpu_custom_call" | custom-call | flops 8589934592 | bytes 1048576 | tf_op jit(solution)/shard_map/pallas_call | solution.py:309
  155.2 14.5 %all-to-all-done.1 = bf16[32,72,128]{2,1,0:T(8,128)(2,1)S(1)} async-done(((bf16[32,72,128]{2,1,0:T(8,128)(2,1)}), bf16[32,72,128]{2,1,0:T(8,128)(2,1)S(1)}, u32[]{:S(2)}, u32[]{:S(2)}) %all-to-all-start.1) | async-done | bytes 589856 | tf_op jit(solution)/shard_map/all_to_all | solution.py:324
  171.6 2.8 %collective-permute-start.24 = (bf16[1024,256]{1,0:T(8,128)(2,1)S(1)}, bf16[1024,256]{1,0:T(8,128)(2,1)S(1)}, u32[]{:S(2)}, u32[]{:S(2)}) collective-permute-start(bf16[1024,256]{1,0:T(8,128)(2,1)S(1)} %shard_map.53.refs_0_), channel_id=1, source_target_pairs={{0,6},{1,7},{2,0},{3,1},{4,2},{5,3},{6,4},{7,5},{8,14},{9,15},{10,... | collective-permute-start | bytes 1572872 | tf_op jit(solution)/shard_map/ppermute | solution.py:31
  174.4 12.1 %collective-permute-done.25.refs_4_ = bf16[1024,256]{1,0:T(8,128)(2,1)S(1)} collective-permute-done((bf16[1024,256]{1,0:T(8,128)(2,1)S(1)}, bf16[1024,256]{1,0:T(8,128)(2,1)S(1)}, u32[]{:S(2)}, u32[]{:S(2)}) %collective-permute-start.25) | collective-permute-done | bytes 524320 | tf_op jit(solution)/shard_map/ppermute | solution.py:31
  186.7 2.7 %collective-permute-start.29 = (bf16[1024,256]{1,0:T(8,128)(2,1)S(1)}, bf16[1024,256]{1,0:T(8,128)(2,1)S(1)}, u32[]{:S(2)}, u32[]{:S(2)}) collective-permute-start(bf16[1024,256]{1,0:T(8,128)(2,1)S(1)} %collective-permute-done.28.refs_5_), channel_id=1, source_target_pairs={{0,6},{1,7},{2,0},{3,1},{4,2},{5,3},{6,4},{7,5},{8,14},{9,15},{10,... | collective-permute-start | bytes 1572872 | tf_op jit(solution)/shard_map/ppermute | solution.py:31
  190.9 4.2 %collective-permute-done.26.refs_2_ = bf16[1024,128]{1,0:T(8,128)(2,1)S(1)} collective-permute-done((bf16[1024,128]{1,0:T(8,128)(2,1)S(1)}, bf16[1024,128]{1,0:T(8,128)(2,1)S(1)}, u32[]{:S(2)}, u32[]{:S(2)}) %collective-permute-start.26) | collective-permute-done | bytes 262176 | tf_op jit(solution)/shard_map/ppermute | solution.py:31
  195.1 10.3 %collective-permute-done.27.refs_3_ = bf16[1024,128]{1,0:T(8,128)(2,1)S(1)} collective-permute-done((bf16[1024,128]{1,0:T(8,128)(2,1)S(1)}, bf16[1024,128]{1,0:T(8,128)(2,1)S(1)}, u32[]{:S(2)}, u32[]{:S(2)}) %collective-permute-start.27) | collective-permute-done | bytes 262176 | tf_op jit(solution)/shard_map/ppermute | solution.py:31
  206.3 5.2 %collective-permute-done.31.refs_8_ = bf16[1024,128]{1,0:T(8,128)(2,1)S(1)} collective-permute-done((bf16[1024,128]{1,0:T(8,128)(2,1)S(1)}, bf16[1024,128]{1,0:T(8,128)(2,1)S(1)}, u32[]{:S(2)}, u32[]{:S(2)}) %collective-permute-start.31) | collective-permute-done | bytes 262176 | tf_op jit(solution)/shard_map/ppermute | solution.py:31
  211.5 2.6 %shard_map.54 = (bf16[2048,128]{1,0:T(8,128)(2,1)}, bf16[1024,128]{1,0:T(8,128)(2,1)S(1)}) custom-call(s32[5]{0:T(128)S(1)} %stack.38.place, bf16[1024,256]{1,0:T(8,128)(2,1)S(1)} %maximum_select_fusion.refs_0_.x_ref, bf16[1024,256]{1,0:T(8,128)(2,1)S(1)} %shard_map.53.refs_0_, bf16[1024,256]{1,0:T(8,128)(2,1)S(1)} %collective-permute-done.24.refs_1_, ...), custom_call_target="tpu_custom_call" | custom-call | tf_op jit(solution)/shard_map/pallas_call | solution.py:309
  214.1 2.6 %collective-permute-start.33 = (bf16[1024,128]{1,0:T(8,128)(2,1)S(1)}, bf16[1024,128]{1,0:T(8,128)(2,1)S(1)}, u32[]{:S(2)}, u32[]{:S(2)}) collective-permute-start(bf16[1024,128]{1,0:T(8,128)(2,1)S(1)} %get-tuple-element.28), channel_id=1, source_target_pairs={{0,1},{1,0},{2,3},{3,2},{4,5},{5,4},{6,7},{7,6},{8,9},{9,8},{10,11... | collective-permute-start | bytes 786440 | tf_op jit(solution)/shard_map/ppermute | solution.py:31
  (107 shorter events, 36.8 us)
Async XLA Ops:
  1.1 11.9 %collective-permute-start = (bf16[1024,128]{1,0:T(8,128)(2,1)S(1)}, bf16[1024,128]{1,0:T(8,128)(2,1)S(1)}, u32[]{:S(2)}, u32[]{:S(2)}) collective-permute-start(bf16[1024,128]{1,0:T(8,128)(2,1)S(1)} %get-tuple-element.30), channel_id=1, source_target_pairs={{0,1},{1,0},{2,3},{3,2},{4,5},{5,4},{6,7},{7,6},{8,9},{9,8},{10,11... | collective-permute-start | bytes 786440 | tf_op jit(solution)/shard_map/ppermute | solution.py:31
  5.3 10.7 %collective-permute-start.12 = (bf16[128,512]{1,0:T(8,128)(2,1)S(1)}, bf16[128,512]{1,0:T(8,128)(2,1)S(1)}, u32[]{:S(2)}, u32[]{:S(2)}) collective-permute-start(bf16[128,512]{1,0:T(8,128)(2,1)S(1)} %pad_maximum_fusion.3), channel_id=1, source_target_pairs={{0,192},{16,208},{32,224},{48,240},{64,0},{80,16},{96,32},{112,48}... | collective-permute-start | bytes 393224 | tf_op jit(solution)/shard_map/ppermute | solution.py:36
  9.7 12.0 %collective-permute-start.11 = (bf16[128,512]{1,0:T(8,128)(2,1)S(1)}, bf16[128,512]{1,0:T(8,128)(2,1)S(1)}, u32[]{:S(2)}, u32[]{:S(2)}) collective-permute-start(bf16[128,512]{1,0:T(8,128)(2,1)S(1)} %pad_maximum_fusion.3), channel_id=1, source_target_pairs={{0,128},{16,144},{32,160},{48,176},{64,192},{80,208},{96,224},{112... | collective-permute-start | bytes 393224 | tf_op jit(solution)/shard_map/ppermute | solution.py:36
  10.7 11.0 %collective-permute-start.10 = (bf16[128,512]{1,0:T(8,128)(2,1)S(1)}, bf16[128,512]{1,0:T(8,128)(2,1)S(1)}, u32[]{:S(2)}, u32[]{:S(2)}) collective-permute-start(bf16[128,512]{1,0:T(8,128)(2,1)S(1)} %pad_maximum_fusion.3), channel_id=1, source_target_pairs={{0,64},{16,80},{32,96},{48,112},{64,128},{80,144},{96,160},{112,17... | collective-permute-start | bytes 393224 | tf_op jit(solution)/shard_map/ppermute | solution.py:36
  13.1 28.9 %collective-permute-start.2 = (bf16[1024,256]{1,0:T(8,128)(2,1)S(1)}, bf16[1024,256]{1,0:T(8,128)(2,1)S(1)}, u32[]{:S(2)}, u32[]{:S(2)}) collective-permute-start(bf16[1024,256]{1,0:T(8,128)(2,1)S(1)} %maximum_select_fusion.refs_0_.x_ref), channel_id=1, source_target_pairs={{0,2},{1,3},{2,4},{3,5},{4,6},{5,7},{6,0},{7,1},{8,10},{9,11},{10,... | collective-permute-start | bytes 1572872 | tf_op jit(solution)/shard_map/ppermute | solution.py:31
  14.5 29.6 %collective-permute-start.1 = (bf16[1024,256]{1,0:T(8,128)(2,1)S(1)}, bf16[1024,256]{1,0:T(8,128)(2,1)S(1)}, u32[]{:S(2)}, u32[]{:S(2)}) collective-permute-start(bf16[1024,256]{1,0:T(8,128)(2,1)S(1)} %maximum_select_fusion.refs_0_.x_ref), channel_id=1, source_target_pairs={{0,6},{1,7},{2,0},{3,1},{4,2},{5,3},{6,4},{7,5},{8,14},{9,15},{10,... | collective-permute-start | bytes 1572872 | tf_op jit(solution)/shard_map/ppermute | solution.py:31
  21.9 9.6 %collective-permute-start.15 = (bf16[4,128,384]{2,1,0:T(8,128)(2,1)S(1)}, bf16[4,128,384]{2,1,0:T(8,128)(2,1)S(1)}, u32[]{:S(2)}, u32[]{:S(2)}) collective-permute-start(bf16[4,128,384]{2,1,0:T(8,128)(2,1)S(1)} %slice.26.refs_0_), channel_id=1, source_target_pairs={{0,48},{16,0},{32,16},{48,32},{64,112},{80,64},{96,80},{112,96},{1... | collective-permute-start | bytes 1179656 | tf_op jit(solution)/shard_map/ppermute | solution.py:36
  24.3 17.8 %collective-permute-start.14 = (bf16[4,128,384]{2,1,0:T(8,128)(2,1)S(1)}, bf16[4,128,384]{2,1,0:T(8,128)(2,1)S(1)}, u32[]{:S(2)}, u32[]{:S(2)}) collective-permute-start(bf16[4,128,384]{2,1,0:T(8,128)(2,1)S(1)} %slice.26.refs_0_), channel_id=1, source_target_pairs={{0,32},{16,48},{32,0},{48,16},{64,96},{80,112},{96,64},{112,80},{1... | collective-permute-start | bytes 1179656 | tf_op jit(solution)/shard_map/ppermute | solution.py:36
  25.0 21.3 %collective-permute-start.5 = (bf16[1024,256]{1,0:T(8,128)(2,1)S(1)}, bf16[1024,256]{1,0:T(8,128)(2,1)S(1)}, u32[]{:S(2)}, u32[]{:S(2)}) collective-permute-start(bf16[1024,256]{1,0:T(8,128)(2,1)S(1)} %maximum_select_fusion.refs_0_.x_ref), channel_id=1, source_target_pairs={{0,8},{1,9},{2,10},{3,11},{4,12},{5,13},{6,14},{7,15},{8,0},{9,1},... | collective-permute-start | bytes 1572872 | tf_op jit(solution)/shard_map/ppermute | solution.py:31
  31.5 12.9 %collective-permute-start.16 = (bf16[4,128,384]{2,1,0:T(8,128)(2,1)S(1)}, bf16[4,128,384]{2,1,0:T(8,128)(2,1)S(1)}, u32[]{:S(2)}, u32[]{:S(2)}) collective-permute-start(bf16[4,128,384]{2,1,0:T(8,128)(2,1)S(1)} %slice.26.refs_0_), channel_id=1, source_target_pairs={{0,1},{1,0},{2,3},{3,2},{4,5},{5,4},{6,7},{7,6},{8,9},{9,8},{10,11... | collective-permute-start | bytes 1179656 | tf_op jit(solution)/shard_map/ppermute | solution.py:31
  42.1 12.9 %collective-permute-start.13 = (bf16[4,128,384]{2,1,0:T(8,128)(2,1)S(1)}, bf16[4,128,384]{2,1,0:T(8,128)(2,1)}, u32[]{:S(2)}, u32[]{:S(2)}) collective-permute-start(bf16[4,128,384]{2,1,0:T(8,128)(2,1)S(1)} %slice.26.refs_0_), channel_id=1, source_target_pairs={{0,16},{16,32},{32,48},{48,0},{64,80},{80,96},{96,112},{112,64},{1... | collective-permute-start | bytes 1179656 | tf_op jit(solution)/shard_map/ppermute | solution.py:36
  42.1 15.6 %collective-permute-start.19 = (bf16[4,128,384]{2,1,0:T(8,128)(2,1)S(1)}, bf16[4,128,384]{2,1,0:T(8,128)(2,1)S(1)}, u32[]{:S(2)}, u32[]{:S(2)}) collective-permute-start(bf16[4,128,384]{2,1,0:T(8,128)(2,1)S(1)} %collective-permute-done.15.refs_3_), channel_id=1, source_target_pairs={{0,1},{1,0},{2,3},{3,2},{4,5},{5,4},{6,7},{7,6},{8,9},{9,8},{10,11... | collective-permute-start | bytes 1179656 | tf_op jit(solution)/shard_map/ppermute | solution.py:31
  44.2 14.7 %collective-permute-start.18 = (bf16[4,128,384]{2,1,0:T(8,128)(2,1)S(1)}, bf16[4,128,384]{2,1,0:T(8,128)(2,1)S(1)}, u32[]{:S(2)}, u32[]{:S(2)}) collective-permute-start(bf16[4,128,384]{2,1,0:T(8,128)(2,1)S(1)} %collective-permute-done.14.refs_2_), channel_id=1, source_target_pairs={{0,1},{1,0},{2,3},{3,2},{4,5},{5,4},{6,7},{7,6},{8,9},{9,8},{10,11... | collective-permute-start | bytes 1179656 | tf_op jit(solution)/shard_map/ppermute | solution.py:31
  45.1 15.8 %collective-permute-start.3 = (bf16[1024,128]{1,0:T(8,128)(2,1)S(1)}, bf16[1024,128]{1,0:T(8,128)(2,1)}, u32[]{:S(2)}, u32[]{:S(2)}) collective-permute-start(bf16[1024,128]{1,0:T(8,128)(2,1)S(1)} %slice.24), channel_id=1, source_target_pairs={{0,2},{1,3},{2,4},{3,5},{4,6},{5,7},{6,0},{7,1},{8,10},{9,11},{10,... | collective-permute-start | bytes 786440 | tf_op jit(solution)/shard_map/ppermute | solution.py:31
  46.4 39.4 %collective-permute-start.9 = (bf16[1024,256]{1,0:T(8,128)(2,1)S(1)}, bf16[1024,256]{1,0:T(8,128)(2,1)S(1)}, u32[]{:S(2)}, u32[]{:S(2)}) collective-permute-start(bf16[1024,256]{1,0:T(8,128)(2,1)S(1)} %collective-permute-done.5.refs_5_), channel_id=1, source_target_pairs={{0,2},{1,3},{2,4},{3,5},{4,6},{5,7},{6,0},{7,1},{8,10},{9,11},{10,... | collective-permute-start | bytes 1572872 | tf_op jit(solution)/shard_map/ppermute | solution.py:31
  54.9 30.8 %collective-permute-start.6 = (bf16[1024,256]{1,0:T(8,128)(2,1)S(1)}, bf16[1024,256]{1,0:T(8,128)(2,1)S(1)}, u32[]{:S(2)}, u32[]{:S(2)}) collective-permute-start(bf16[1024,256]{1,0:T(8,128)(2,1)S(1)} %collective-permute-done.5.refs_5_), channel_id=1, source_target_pairs={{0,6},{1,7},{2,0},{3,1},{4,2},{5,3},{6,4},{7,5},{8,14},{9,15},{10,... | collective-permute-start | bytes 1572872 | tf_op jit(solution)/shard_map/ppermute | solution.py:31
  58.4 15.5 %collective-permute-start.4 = (bf16[1024,128]{1,0:T(8,128)(2,1)S(1)}, bf16[1024,128]{1,0:T(8,128)(2,1)}, u32[]{:S(2)}, u32[]{:S(2)}) collective-permute-start(bf16[1024,128]{1,0:T(8,128)(2,1)S(1)} %slice.25), channel_id=1, source_target_pairs={{0,6},{1,7},{2,0},{3,1},{4,2},{5,3},{6,4},{7,5},{8,14},{9,15},{10,... | collective-permute-start | bytes 786440 | tf_op jit(solution)/shard_map/ppermute | solution.py:31
  59.7 17.0 %collective-permute-start.17 = (bf16[4,128,384]{2,1,0:T(8,128)(2,1)}, bf16[4,128,384]{2,1,0:T(8,128)(2,1)}, u32[]{:S(2)}, u32[]{:S(2)}) collective-permute-start(bf16[4,128,384]{2,1,0:T(8,128)(2,1)} %collective-permute-done.13.refs_1_), channel_id=1, source_target_pairs={{0,1},{1,0},{2,3},{3,2},{4,5},{5,4},{6,7},{7,6},{8,9},{9,8},{10,11... | collective-permute-start | bytes 1179656 | tf_op jit(solution)/shard_map/ppermute | solution.py:31
  60.9 24.8 %collective-permute-start.7 = (bf16[1024,128]{1,0:T(8,128)(2,1)}, bf16[1024,128]{1,0:T(8,128)(2,1)}, u32[]{:S(2)}, u32[]{:S(2)}) collective-permute-start(bf16[1024,128]{1,0:T(8,128)(2,1)} %collective-permute-done.3.refs_2_), channel_id=1, source_target_pairs={{0,8},{1,9},{2,10},{3,11},{4,12},{5,13},{6,14},{7,15},{8,0},{9,1},... | collective-permute-start | bytes 786440 | tf_op jit(solution)/shard_map/ppermute | solution.py:31
  73.9 11.9 %collective-permute-start.8 = (bf16[1024,128]{1,0:T(8,128)(2,1)}, bf16[1024,128]{1,0:T(8,128)(2,1)}, u32[]{:S(2)}, u32[]{:S(2)}) collective-permute-start(bf16[1024,128]{1,0:T(8,128)(2,1)} %collective-permute-done.4.refs_3_), channel_id=1, source_target_pairs={{0,8},{1,9},{2,10},{3,11},{4,12},{5,13},{6,14},{7,15},{8,0},{9,1},... | collective-permute-start | bytes 786440 | tf_op jit(solution)/shard_map/ppermute | solution.py:31
  93.7 49.5 %all-to-all-start = ((bf16[32,64,384]{2,1,0:T(8,128)(2,1)}), bf16[32,64,384]{2,1,0:T(8,128)(2,1)S(1)}, u32[]{:S(2)}, u32[]{:S(2)}) async-start(bf16[32,64,384]{2,1,0:T(8,128)(2,1)} %bitcast.9), calls=%async_computation | async-start | bytes 3145728 | tf_op jit(solution)/shard_map/all_to_all | solution.py:324
  103.7 10.6 %collective-permute-start.22 = (bf16[4,128,128]{2,1,0:T(8,128)(2,1)S(1)}, bf16[4,128,128]{2,1,0:T(8,128)(2,1)S(1)}, u32[]{:S(2)}, u32[]{:S(2)}) collective-permute-start(bf16[4,128,128]{2,1,0:T(8,128)(2,1)S(1)} %pad_maximum_fusion.2.refs_0_), channel_id=1, source_target_pairs={{0,48},{16,0},{32,16},{48,32},{64,112},{80,64},{96,80},{112,96},{1... | collective-permute-start | bytes 393224 | tf_op jit(solution)/shard_map/ppermute | solution.py:36
  106.3 9.0 %collective-permute-start.21 = (bf16[4,128,128]{2,1,0:T(8,128)(2,1)S(1)}, bf16[4,128,128]{2,1,0:T(8,128)(2,1)S(1)}, u32[]{:S(2)}, u32[]{:S(2)}) collective-permute-start(bf16[4,128,128]{2,1,0:T(8,128)(2,1)S(1)} %pad_maximum_fusion.2.refs_0_), channel_id=1, source_target_pairs={{0,32},{16,48},{32,0},{48,16},{64,96},{80,112},{96,64},{112,80},{1... | collective-permute-start | bytes 393224 | tf_op jit(solution)/shard_map/ppermute | solution.py:36
  106.9 11.5 %collective-permute-start.20 = (bf16[4,128,128]{2,1,0:T(8,128)(2,1)S(1)}, bf16[4,128,128]{2,1,0:T(8,128)(2,1)S(1)}, u32[]{:S(2)}, u32[]{:S(2)}) collective-permute-start(bf16[4,128,128]{2,1,0:T(8,128)(2,1)S(1)} %pad_maximum_fusion.2.refs_0_), channel_id=1, source_target_pairs={{0,16},{16,32},{32,48},{48,0},{64,80},{80,96},{96,112},{112,64},{1... | collective-permute-start | bytes 393224 | tf_op jit(solution)/shard_map/ppermute | solution.py:36
  146.0 23.6 %all-to-all-start.1 = ((bf16[32,72,128]{2,1,0:T(8,128)(2,1)}), bf16[32,72,128]{2,1,0:T(8,128)(2,1)S(1)}, u32[]{:S(2)}, u32[]{:S(2)}) async-start(bf16[32,72,128]{2,1,0:T(8,128)(2,1)} %copy-done), calls=%async_computation.1 | async-start | bytes 1179648 | tf_op jit(solution)/shard_map/all_to_all | solution.py:324
  170.7 15.9 %collective-permute-start.25 = (bf16[1024,256]{1,0:T(8,128)(2,1)S(1)}, bf16[1024,256]{1,0:T(8,128)(2,1)S(1)}, u32[]{:S(2)}, u32[]{:S(2)}) collective-permute-start(bf16[1024,256]{1,0:T(8,128)(2,1)S(1)} %shard_map.53.refs_0_), channel_id=1, source_target_pairs={{0,2},{1,3},{2,4},{3,5},{4,6},{5,7},{6,0},{7,1},{8,10},{9,11},{10,... | collective-permute-start | bytes 1572872 | tf_op jit(solution)/shard_map/ppermute | solution.py:31
  171.6 15.0 %collective-permute-start.28 = (bf16[1024,256]{1,0:T(8,128)(2,1)S(1)}, bf16[1024,256]{1,0:T(8,128)(2,1)S(1)}, u32[]{:S(2)}, u32[]{:S(2)}) collective-permute-start(bf16[1024,256]{1,0:T(8,128)(2,1)S(1)} %shard_map.53.refs_0_), channel_id=1, source_target_pairs={{0,8},{1,9},{2,10},{3,11},{4,12},{5,13},{6,14},{7,15},{8,0},{9,1},... | collective-permute-start | bytes 1572872 | tf_op jit(solution)/shard_map/ppermute | solution.py:31
  171.6 17.8 %collective-permute-start.24 = (bf16[1024,256]{1,0:T(8,128)(2,1)S(1)}, bf16[1024,256]{1,0:T(8,128)(2,1)S(1)}, u32[]{:S(2)}, u32[]{:S(2)}) collective-permute-start(bf16[1024,256]{1,0:T(8,128)(2,1)S(1)} %shard_map.53.refs_0_), channel_id=1, source_target_pairs={{0,6},{1,7},{2,0},{3,1},{4,2},{5,3},{6,4},{7,5},{8,14},{9,15},{10,... | collective-permute-start | bytes 1572872 | tf_op jit(solution)/shard_map/ppermute | solution.py:31
  186.7 19.7 %collective-permute-start.32 = (bf16[1024,256]{1,0:T(8,128)(2,1)S(1)}, bf16[1024,256]{1,0:T(8,128)(2,1)S(1)}, u32[]{:S(2)}, u32[]{:S(2)}) collective-permute-start(bf16[1024,256]{1,0:T(8,128)(2,1)S(1)} %collective-permute-done.28.refs_5_), channel_id=1, source_target_pairs={{0,2},{1,3},{2,4},{3,5},{4,6},{5,7},{6,0},{7,1},{8,10},{9,11},{10,... | collective-permute-start | bytes 1572872 | tf_op jit(solution)/shard_map/ppermute | solution.py:31
  186.7 19.6 %collective-permute-start.29 = (bf16[1024,256]{1,0:T(8,128)(2,1)S(1)}, bf16[1024,256]{1,0:T(8,128)(2,1)S(1)}, u32[]{:S(2)}, u32[]{:S(2)}) collective-permute-start(bf16[1024,256]{1,0:T(8,128)(2,1)S(1)} %collective-permute-done.28.refs_5_), channel_id=1, source_target_pairs={{0,6},{1,7},{2,0},{3,1},{4,2},{5,3},{6,4},{7,5},{8,14},{9,15},{10,... | collective-permute-start | bytes 1572872 | tf_op jit(solution)/shard_map/ppermute | solution.py:31
  189.4 16.0 %collective-permute-start.27 = (bf16[1024,128]{1,0:T(8,128)(2,1)S(1)}, bf16[1024,128]{1,0:T(8,128)(2,1)S(1)}, u32[]{:S(2)}, u32[]{:S(2)}) collective-permute-start(bf16[1024,128]{1,0:T(8,128)(2,1)S(1)} %slice.28), channel_id=1, source_target_pairs={{0,6},{1,7},{2,0},{3,1},{4,2},{5,3},{6,4},{7,5},{8,14},{9,15},{10,... | collective-permute-start | bytes 786440 | tf_op jit(solution)/shard_map/ppermute | solution.py:31
  195.1 11.2 %collective-permute-start.30 = (bf16[1024,128]{1,0:T(8,128)(2,1)S(1)}, bf16[1024,128]{1,0:T(8,128)(2,1)S(1)}, u32[]{:S(2)}, u32[]{:S(2)}) collective-permute-start(bf16[1024,128]{1,0:T(8,128)(2,1)S(1)} %collective-permute-done.26.refs_2_), channel_id=1, source_target_pairs={{0,8},{1,9},{2,10},{3,11},{4,12},{5,13},{6,14},{7,15},{8,0},{9,1},... | collective-permute-start | bytes 786440 | tf_op jit(solution)/shard_map/ppermute | solution.py:31
  (26 other events, 234.1 us)

commit v3 on v2

--- a/solution.py
+++ b/solution.py
@@ -186,15 +186,13 @@
         norm(later, mean, rstd, to_ref)
         project(tile, from_ref, 2)
 
+    slots = (even_ref, odd_ref)
     count = COLS // TILE
     norm(0, *together(0, *moments_of(0)), even_ref)
-
-    def step(i, carry):
-        both(2 * i, even_ref, 2 * i + 1, odd_ref)
-        both(2 * i + 1, odd_ref, jnp.minimum(2 * i + 2, count - 1), even_ref)
-        return carry
-
-    lax.fori_loop(0, count // 2, step, 0)
+    for tile in range(count - 1):
+        both(tile, slots[tile % 2], tile + 1, slots[(tile + 1) % 2])
+    for part in range(3):
+        project(count - 1, slots[(count - 1) % 2], part)
 
 
 def _out_kernel(place, x_ref, *refs):
@@ -213,39 +211,41 @@
         other_ref[pl.ds(at, TILE), :] = other.astype(BF16)
 
 
-def _row_kernel(head, qkv_ref, out_ref, lse_ref):
+def _row_kernel(qkv_ref, out_ref, lse_ref):
     diagonal = lax.broadcasted_iota(jnp.int32, (TILE, TILE), 0) >= lax.broadcasted_iota(
         jnp.int32, (TILE, TILE), 1
     )
     n = TILE // 64
     lane = lax.broadcasted_iota(jnp.int32, (64, HS), 1)
-    packed = jnp.zeros((64, HS), F32)
-
-    def part(lo, hi, k):
-        v = qkv_ref[lo * n : hi * n, head, :, k * HS : (k + 1) * HS]
-        return v.reshape((hi - lo) * TILE, HS)
-
-    for tile in range(COLS // TILE):
-        q = part(tile, tile + 1, 0)
-        last = lax.dot_general(q, part(tile, tile + 1, 1), NT, preferred_element_type=F32)
-        last = jnp.where(diagonal, last, NEGATIVE)
-        top = jnp.max(last, axis=1, keepdims=True)
-        if tile:
-            before = lax.dot_general(q, part(0, tile, 1), NT, preferred_element_type=F32)
-            top = jnp.maximum(top, jnp.max(before, axis=1, keepdims=True))
-        w = jnp.exp2((last - top) * SCALE2)
-        total = jnp.sum(w, axis=1, keepdims=True)
-        acc = jnp.dot(w.astype(BF16), part(tile, tile + 1, 2), preferred_element_type=F32)
-        if tile:
-            w = jnp.exp2((before - top) * SCALE2)
-            total += jnp.sum(w, axis=1, keepdims=True)
-            acc += jnp.dot(w.astype(BF16), part(0, tile, 2), preferred_element_type=F32)
-        out_ref[tile * TILE : (tile + 1) * TILE, :] = acc / total
-        lse = top * SCALE2 + jnp.log2(total)
-        for k in range(n):
-            here = lane == 2 * (tile * n + k) + head
-            packed = jnp.where(here, lse[k * 64 : (k + 1) * 64], packed)
-    lse_ref[...] = packed
+
+    def attend(head, packed):
+        def part(lo, hi, k):
+            v = qkv_ref[lo * n : hi * n, head, :, k * HS : (k + 1) * HS]
+            return v.reshape((hi - lo) * TILE, HS)
+
+        for tile in range(COLS // TILE):
+            q = part(tile, tile + 1, 0)
+            last = lax.dot_general(q, part(tile, tile + 1, 1), NT, preferred_element_type=F32)
+            last = jnp.where(diagonal, last, NEGATIVE)
+            top = jnp.max(last, axis=1, keepdims=True)
+            if tile:
+                before = lax.dot_general(q, part(0, tile, 1), NT, preferred_element_type=F32)
+                top = jnp.maximum(top, jnp.max(before, axis=1, keepdims=True))
+            w = jnp.exp2((last - top) * SCALE2)
+            total = jnp.sum(w, axis=1, keepdims=True)
+            acc = jnp.dot(w.astype(BF16), part(tile, tile + 1, 2), preferred_element_type=F32)
+            if tile:
+                w = jnp.exp2((before - top) * SCALE2)
+                total += jnp.sum(w, axis=1, keepdims=True)
+                acc += jnp.dot(w.astype(BF16), part(0, tile, 2), preferred_element_type=F32)
+            out_ref[head, tile * TILE : (tile + 1) * TILE, :] = acc / total
+            lse = top * SCALE2 + jnp.log2(total)
+            for k in range(n):
+                here = lane == 2 * (tile * n + k) + head
+                packed = jnp.where(here, lse[k * 64 : (k + 1) * 64], packed)
+        return packed
+
+    lse_ref[...] = lax.fori_loop(0, 2, attend, jnp.zeros((64, HS), F32))
 
 
 def _column_kernel(z_ref, out_ref):
@@ -280,14 +280,14 @@
     out_ref[:, 64 : 64 + STAT_ROWS, :] = stats.astype(BF16).reshape(32, STAT_ROWS, HS)
 
 
-def _merge_kernel(row0_ref, lse0_ref, row1_ref, lse1_ref, col_ref, out_ref):
+def _merge_kernel(row_ref, lse_ref, col_ref, out_ref):
     stats = col_ref[:, :, 64:, :].reshape(32 * STAT_ROWS, HS)
     source = lax.broadcasted_iota(jnp.int32, (HS, 32 * STAT_ROWS), 1)
     entry = lax.broadcasted_iota(jnp.int32, (HS, 32 * STAT_ROWS), 0)
     picks = [(source == entry * STAT_ROWS + m).astype(F32).astype(BF16) for m in range(3)]
     parts = [jnp.dot(pick, stats, preferred_element_type=F32) for pick in picks]
     cl = (parts[0] + parts[1] + parts[2]).T[:64]
-    rl = lse0_ref[...] + lse1_ref[...]
+    rl = lse_ref[...]
     top = jnp.maximum(cl, rl)
     rf = jnp.exp2(rl - top)
     cf = jnp.exp2(cl - top)
@@ -296,9 +296,9 @@
     cf = cf * share
     for block in range(16):
         rows = slice(block * 64, (block + 1) * 64)
-        for head, row_ref in enumerate((row0_ref, row1_ref)):
+        for head in range(2):
             n = 2 * block + head
-            o = rf[:, n : n + 1] * row_ref[rows, :] + cf[:, n : n + 1] * col_ref[block, head, :64, :].astype(F32)
+            o = rf[:, n : n + 1] * row_ref[head, rows, :] + cf[:, n : n + 1] * col_ref[block, head, :64, :].astype(F32)
             out_ref[rows, head * HS : (head + 1) * HS] = o.astype(BF16)
 
 
@@ -358,20 +358,15 @@
     )
     by_column = exchange_columns(qkv.reshape(32, 64, 3 * HS))
     weights, qkv = lax.optimization_barrier((weights[..., 3 * HS :], qkv))
-    w = _call(_weights_kernel, shape((2048, HS), BF16), place, *over_x(weights), scalars=1)
-    w = jnp.concatenate([w, core_swap(w)], axis=1)
-    row = []
-    for head in range(2):
-        row += _call(
-            lambda *refs, head=head: _row_kernel(head, *refs),
-            (shape((COLS, HS), F32), shape((64, HS), F32)),
-            qkv,
-            flops=1 << 33,
-        )
-    by_column, w, first = lax.optimization_barrier((by_column, w, tuple(row[:2])))
+    weights = over_x(weights)
+    w = _call(_weights_kernel, shape((2048, HS), BF16), place, *weights, scalars=1, flops=1 << 31)
+    swapped = core_swap(w)
+    w = jnp.concatenate([w, swapped], axis=1)
+    row = _call(_row_kernel, (shape((2, COLS, HS), F32), shape((64, HS), F32)), qkv, flops=1 << 33)
+    by_column, w = lax.optimization_barrier((by_column, w))
     col_out = _call(_column_kernel, shape((32, 64 + STAT_ROWS, HS), BF16), by_column)
     col_out = exchange_columns(col_out).reshape(16, 2, 64 + STAT_ROWS, HS)
-    att = _call(_merge_kernel, shape((COLS, 2 * HS), BF16), *first, *row[2:], col_out)
+    att = _call(_merge_kernel, shape((COLS, 2 * HS), BF16), *row, col_out)
     out_own, out_other = _call(
         _out_kernel, (shape((2 * COLS, HS), BF16), shape((COLS, HS), BF16)), place, x, *gather_chips(att), w, scalars=1
     )

time: 219 us -> 218 us (level)
  waiting for transfers between devices: 105 us -> 108 us
  Pallas kernels: 24.7 us -> 22.1 us
    pallas_call x9 -> x8, Pallas kernels: 24.7 us -> 22.1 us  [_call(): pl.pallas_call(kernel, out_shape=out, in_specs=[smem] * scalars + [vmem]...]
    unnamed x44 -> x40, local copies, waits for them, and re-layouts: 8.9 us -> 8.09 us
  transfers between devices with their start and end apart: 36 -> 36, of which waited for: 15 -> 16; matrix products, arithmetic and copies ran while one was open for 1% -> 1% of each run, Pallas kernels for 5% -> 4%
where the time goes in v3:
time: 218 us
  waiting for transfers between devices  108 us (50%)
  starting transfers between devices  76.3 us (35%)
  Pallas kernels  22.1 us (10%)
  local copies, waits for them, and re-layouts  10 us (5%)
    ppermute x25, waiting for transfers between devices, _over_col(): return lax.ppermute(x, 'col', pairs)  45.8 us
    ppermute x25, starting transfers between devices, _over_col(): return lax.ppermute(x, 'col', pairs)  45.6 us
    all_to_all x2, waiting for transfers between devices, exchange_columns(): lax.all_to_all(x, ('row', 'col'), split_axis=0, concat_axis=0, axis_index...  34.2 us
    ppermute x9, waiting for transfers between devices, _over_row(): return lax.ppermute(x, 'row', pairs)  27.5 us
    pallas_call x8, Pallas kernels, _call(): pl.pallas_call(kernel, out_shape=out, in_specs=[smem] * scalars + [vmem]...  22.1 us
    all_to_all x2, starting transfers between devices, exchange_columns(): lax.all_to_all(x, ('row', 'col'), split_axis=0, concat_axis=0, axis_index...  16.1 us
    ppermute x9, starting transfers between devices, _over_row(): return lax.ppermute(x, 'row', pairs)  14.7 us
    unnamed x40, local copies, waits for them, and re-layouts  8.09 us
  transfers between devices with their start and end apart: 36, of which 16 were waited for; matrix products, arithmetic and copies ran while one was open for 1% of the time, Pallas kernels for 4%

profile of v3, /device:TPU:1, one launch (start us, length us, event | category | flops | bytes accessed | tf_op | source)
XLA Modules:
  0.0 217.6 jit_solution(2483445187187999412)
XLA Ops:
  1.1 3.3 %collective-permute-start = (bf16[1024,128]{1,0:T(8,128)(2,1)S(1)}, bf16[1024,128]{1,0:T(8,128)(2,1)S(1)}, u32[]{:S(2)}, u32[]{:S(2)}) collective-permute-start(bf16[1024,128]{1,0:T(8,128)(2,1)S(1)} %get-tuple-element.22), channel_id=1, source_target_pairs={{0,1},{1,0},{2,3},{3,2},{4,5},{5,4},{6,7},{7,6},{8,9},{9,8},{10,11... | collective-permute-start | bytes 786440 | tf_op jit(solution)/shard_map/ppermute | solution.py:31
  5.3 4.4 %collective-permute-start.3 = (bf16[128,512]{1,0:T(8,128)(2,1)S(1)}, bf16[128,512]{1,0:T(8,128)(2,1)S(1)}, u32[]{:S(2)}, u32[]{:S(2)}) collective-permute-start(bf16[128,512]{1,0:T(8,128)(2,1)S(1)} %pad_maximum_fusion.5), channel_id=1, source_target_pairs={{0,192},{16,208},{32,224},{48,240},{64,0},{80,16},{96,32},{112,48}... | collective-permute-start | bytes 393224 | tf_op jit(solution)/shard_map/ppermute | solution.py:36
  10.7 2.3 %collective-permute-start.1 = (bf16[128,512]{1,0:T(8,128)(2,1)S(1)}, bf16[128,512]{1,0:T(8,128)(2,1)S(1)}, u32[]{:S(2)}, u32[]{:S(2)}) collective-permute-start(bf16[128,512]{1,0:T(8,128)(2,1)S(1)} %pad_maximum_fusion.5), channel_id=1, source_target_pairs={{0,64},{16,80},{32,96},{48,112},{64,128},{80,144},{96,160},{112,17... | collective-permute-start | bytes 393224 | tf_op jit(solution)/shard_map/ppermute | solution.py:36
  16.1 5.7 %collective-permute-done.2 = bf16[128,512]{1,0:T(8,128)(2,1)S(1)} collective-permute-done((bf16[128,512]{1,0:T(8,128)(2,1)S(1)}, bf16[128,512]{1,0:T(8,128)(2,1)S(1)}, u32[]{:S(2)}, u32[]{:S(2)}) %collective-permute-start.2) | collective-permute-done | bytes 131104 | tf_op jit(solution)/shard_map/ppermute | solution.py:36
  21.8 2.4 %collective-permute-start.15 = (bf16[4,128,384]{2,1,0:T(8,128)(2,1)S(1)}, bf16[4,128,384]{2,1,0:T(8,128)(2,1)S(1)}, u32[]{:S(2)}, u32[]{:S(2)}) collective-permute-start(bf16[4,128,384]{2,1,0:T(8,128)(2,1)S(1)} %pad_maximum_fusion.1.refs_0_), channel_id=1, source_target_pairs={{0,48},{16,0},{32,16},{48,32},{64,112},{80,64},{96,80},{112,96},{1... | collective-permute-start | bytes 1179656 | tf_op jit(solution)/shard_map/ppermute | solution.py:36
  25.0 2.6 %collective-permute-start.8 = (bf16[1024,256]{1,0:T(8,128)(2,1)S(1)}, bf16[1024,256]{1,0:T(8,128)(2,1)S(1)}, u32[]{:S(2)}, u32[]{:S(2)}) collective-permute-start(bf16[1024,256]{1,0:T(8,128)(2,1)S(1)} %maximum_select_fusion.refs_0_.x_ref), channel_id=1, source_target_pairs={{0,8},{1,9},{2,10},{3,11},{4,12},{5,13},{6,14},{7,15},{8,0},{9,1},... | collective-permute-start | bytes 1572872 | tf_op jit(solution)/shard_map/ppermute | solution.py:31
  27.7 3.7 %collective-permute-done.15.refs_3_ = bf16[4,128,384]{2,1,0:T(8,128)(2,1)S(1)} collective-permute-done((bf16[4,128,384]{2,1,0:T(8,128)(2,1)S(1)}, bf16[4,128,384]{2,1,0:T(8,128)(2,1)S(1)}, u32[]{:S(2)}, u32[]{:S(2)}) %collective-permute-start.15) | collective-permute-done | bytes 393248 | tf_op jit(solution)/shard_map/ppermute | solution.py:36
  31.4 10.6 %collective-permute-start.16 = (bf16[4,128,384]{2,1,0:T(8,128)(2,1)S(1)}, bf16[4,128,384]{2,1,0:T(8,128)(2,1)S(1)}, u32[]{:S(2)}, u32[]{:S(2)}) collective-permute-start(bf16[4,128,384]{2,1,0:T(8,128)(2,1)S(1)} %pad_maximum_fusion.1.refs_0_), channel_id=1, source_target_pairs={{0,1},{1,0},{2,3},{3,2},{4,5},{5,4},{6,7},{7,6},{8,9},{9,8},{10,11... | collective-permute-start | bytes 1179656 | tf_op jit(solution)/shard_map/ppermute | solution.py:31
  42.0 2.1 collective-permute-start.19
  47.6 7.3 %collective-permute-done.13.refs_1_ = bf16[4,128,384]{2,1,0:T(8,128)(2,1)} collective-permute-done((bf16[4,128,384]{2,1,0:T(8,128)(2,1)S(1)}, bf16[4,128,384]{2,1,0:T(8,128)(2,1)}, u32[]{:S(2)}, u32[]{:S(2)}) %collective-permute-start.13) | collective-permute-done | bytes 393248 | tf_op jit(solution)/shard_map/ppermute | solution.py:36
  54.8 2.7 %collective-permute-start.9 = (bf16[1024,256]{1,0:T(8,128)(2,1)S(1)}, bf16[1024,256]{1,0:T(8,128)(2,1)S(1)}, u32[]{:S(2)}, u32[]{:S(2)}) collective-permute-start(bf16[1024,256]{1,0:T(8,128)(2,1)S(1)} %collective-permute-done.8.refs_5_), channel_id=1, source_target_pairs={{0,6},{1,7},{2,0},{3,1},{4,2},{5,3},{6,4},{7,5},{8,14},{9,15},{10,... | collective-permute-start | bytes 1572872 | tf_op jit(solution)/shard_map/ppermute | solution.py:31
  60.8 2.7 %collective-permute-start.10 = (bf16[1024,128]{1,0:T(8,128)(2,1)}, bf16[1024,128]{1,0:T(8,128)(2,1)}, u32[]{:S(2)}, u32[]{:S(2)}) collective-permute-start(bf16[1024,128]{1,0:T(8,128)(2,1)} %collective-permute-done.6.refs_2_), channel_id=1, source_target_pairs={{0,8},{1,9},{2,10},{3,11},{4,12},{5,13},{6,14},{7,15},{8,0},{9,1},... | collective-permute-start | bytes 786440 | tf_op jit(solution)/shard_map/ppermute | solution.py:31
  63.5 10.3 %collective-permute-done.7.refs_3_ = bf16[1024,128]{1,0:T(8,128)(2,1)} collective-permute-done((bf16[1024,128]{1,0:T(8,128)(2,1)S(1)}, bf16[1024,128]{1,0:T(8,128)(2,1)}, u32[]{:S(2)}, u32[]{:S(2)}) %collective-permute-start.7) | collective-permute-done | bytes 262176 | tf_op jit(solution)/shard_map/ppermute | solution.py:31
  73.8 2.7 %collective-permute-start.11 = (bf16[1024,128]{1,0:T(8,128)(2,1)}, bf16[1024,128]{1,0:T(8,128)(2,1)}, u32[]{:S(2)}, u32[]{:S(2)}) collective-permute-start(bf16[1024,128]{1,0:T(8,128)(2,1)} %collective-permute-done.7.refs_3_), channel_id=1, source_target_pairs={{0,8},{1,9},{2,10},{3,11},{4,12},{5,13},{6,14},{7,15},{8,0},{9,1},... | collective-permute-start | bytes 786440 | tf_op jit(solution)/shard_map/ppermute | solution.py:31
  83.2 2.5 %shard_map.46.early_ref = f32[1024,2]{1,0:T(8,128)S(1)} custom-call(bf16[1024,256]{1,0:T(8,128)(2,1)S(1)} %maximum_select_fusion.refs_0_.x_ref, bf16[1024,256]{1,0:T(8,128)(2,1)S(1)} %collective-permute-done.4.refs_1_, bf16[1024,128]{1,0:T(8,128)(2,1)} %collective-permute-done.6.refs_2_, bf16[1024,128]{1,0:T(8,128)(2,1)} %collective-permute-done.7.refs_3_, ...), custom_call_target="tpu_custom_call" | custom-call | flops 1073741824 | bytes 1048576 | tf_op jit(solution)/shard_map/pallas_call | solution.py:309
  85.7 6.7 %shard_map.48.qkv_ref = bf16[16,2,64,384]{3,2,1,0:T(8,128)(2,1)} custom-call(s32[5]{0:T(128)S(1)} %stack.38.place, f32[8,256]{1,0:T(8,128)S(1)} %reshape.9.gain_ref, f32[1024,2]{1,0:T(8,128)S(1)} %shard_map.46.early_ref, bf16[1024,256]{1,0:T(8,128)(2,1)S(1)} %maximum_select_fusion.refs_0_.x_ref, bf16[1024,256]{1,0:T(8,128)(2,1)S(1)} %collective-permute-done.4.refs_1_, ...), custom_call_target="tpu_custom_call" | custom-call | tf_op jit(solution)/shard_map/pallas_call | solution.py:309
  92.4 9.9 %all-to-all-start = ((bf16[32,64,384]{2,1,0:T(8,128)(2,1)}), bf16[32,64,384]{2,1,0:T(8,128)(2,1)S(1)}, u32[]{:S(2)}, u32[]{:S(2)}) async-start(bf16[32,64,384]{2,1,0:T(8,128)(2,1)} %bitcast.9), calls=%async_computation | async-start | bytes 3145728 | tf_op jit(solution)/shard_map/all_to_all | solution.py:324
  102.4 2.6 %collective-permute-start.22 = (bf16[4,128,128]{2,1,0:T(8,128)(2,1)S(1)}, bf16[4,128,128]{2,1,0:T(8,128)(2,1)S(1)}, u32[]{:S(2)}, u32[]{:S(2)}) collective-permute-start(bf16[4,128,128]{2,1,0:T(8,128)(2,1)S(1)} %pad_maximum_fusion.4.refs_0_), channel_id=1, source_target_pairs={{0,48},{16,0},{32,16},{48,32},{64,112},{80,64},{96,80},{112,96},{1... | collective-permute-start | bytes 393224 | tf_op jit(solution)/shard_map/ppermute | solution.py:36
  106.2 6.8 %collective-permute-done.22.refs_3_ = bf16[4,128,128]{2,1,0:T(8,128)(2,1)S(1)} collective-permute-done((bf16[4,128,128]{2,1,0:T(8,128)(2,1)S(1)}, bf16[4,128,128]{2,1,0:T(8,128)(2,1)S(1)}, u32[]{:S(2)}, u32[]{:S(2)}) %collective-permute-start.22) | collective-permute-done | bytes 131104 | tf_op jit(solution)/shard_map/ppermute | solution.py:36
  114.1 3.0 %collective-permute-done.20.refs_1_ = bf16[4,128,128]{2,1,0:T(8,128)(2,1)S(1)} collective-permute-done((bf16[4,128,128]{2,1,0:T(8,128)(2,1)S(1)}, bf16[4,128,128]{2,1,0:T(8,128)(2,1)S(1)}, u32[]{:S(2)}, u32[]{:S(2)}) %collective-permute-start.20) | collective-permute-done | bytes 131104 | tf_op jit(solution)/shard_map/ppermute | solution.py:36
  120.4 21.4 %all-to-all-done.z_ref = bf16[32,64,384]{2,1,0:T(8,128)(2,1)S(1)} async-done(((bf16[32,64,384]{2,1,0:T(8,128)(2,1)}), bf16[32,64,384]{2,1,0:T(8,128)(2,1)S(1)}, u32[]{:S(2)}, u32[]{:S(2)}) %all-to-all-start) | async-done | bytes 1572896 | tf_op jit(solution)/shard_map/all_to_all | solution.py:324
  144.8 6.2 %all-to-all-start.1 = ((bf16[32,72,128]{2,1,0:T(8,128)(2,1)}), bf16[32,72,128]{2,1,0:T(8,128)(2,1)S(1)}, u32[]{:S(2)}, u32[]{:S(2)}) async-start(bf16[32,72,128]{2,1,0:T(8,128)(2,1)} %copy-done), calls=%async_computation.1 | async-start | bytes 1179648 | tf_op jit(solution)/shard_map/all_to_all | solution.py:324
  151.0 4.9 %shard_map.49 = (f32[2,1024,128]{2,1,0:T(8,128)S(1)}, f32[64,128]{1,0:T(8,128)S(1)}) custom-call(bf16[16,2,64,384]{3,2,1,0:T(8,128)(2,1)} %shard_map.48.qkv_ref), custom_call_target="tpu_custom_call" | custom-call | flops 8589934592 | bytes 1048576 | tf_op jit(solution)/shard_map/pallas_call | solution.py:309
  155.9 12.8 %all-to-all-done.1 = bf16[32,72,128]{2,1,0:T(8,128)(2,1)S(1)} async-done(((bf16[32,72,128]{2,1,0:T(8,128)(2,1)}), bf16[32,72,128]{2,1,0:T(8,128)(2,1)S(1)}, u32[]{:S(2)}, u32[]{:S(2)}) %all-to-all-start.1) | async-done | bytes 589856 | tf_op jit(solution)/shard_map/all_to_all | solution.py:324
  170.6 2.8 %collective-permute-start.24 = (bf16[1024,256]{1,0:T(8,128)(2,1)S(1)}, bf16[1024,256]{1,0:T(8,128)(2,1)S(1)}, u32[]{:S(2)}, u32[]{:S(2)}) collective-permute-start(bf16[1024,256]{1,0:T(8,128)(2,1)S(1)} %shard_map.52.refs_0_), channel_id=1, source_target_pairs={{0,6},{1,7},{2,0},{3,1},{4,2},{5,3},{6,4},{7,5},{8,14},{9,15},{10,... | collective-permute-start | bytes 1572872 | tf_op jit(solution)/shard_map/ppermute | solution.py:31
  173.4 12.1 %collective-permute-done.25.refs_4_ = bf16[1024,256]{1,0:T(8,128)(2,1)S(1)} collective-permute-done((bf16[1024,256]{1,0:T(8,128)(2,1)S(1)}, bf16[1024,256]{1,0:T(8,128)(2,1)S(1)}, u32[]{:S(2)}, u32[]{:S(2)}) %collective-permute-start.25) | collective-permute-done | bytes 524320 | tf_op jit(solution)/shard_map/ppermute | solution.py:31
  185.7 2.7 %collective-permute-start.29 = (bf16[1024,256]{1,0:T(8,128)(2,1)S(1)}, bf16[1024,256]{1,0:T(8,128)(2,1)S(1)}, u32[]{:S(2)}, u32[]{:S(2)}) collective-permute-start(bf16[1024,256]{1,0:T(8,128)(2,1)S(1)} %collective-permute-done.28.refs_5_), channel_id=1, source_target_pairs={{0,6},{1,7},{2,0},{3,1},{4,2},{5,3},{6,4},{7,5},{8,14},{9,15},{10,... | collective-permute-start | bytes 1572872 | tf_op jit(solution)/shard_map/ppermute | solution.py:31
  189.9 4.2 %collective-permute-done.26.refs_2_ = bf16[1024,128]{1,0:T(8,128)(2,1)S(1)} collective-permute-done((bf16[1024,128]{1,0:T(8,128)(2,1)S(1)}, bf16[1024,128]{1,0:T(8,128)(2,1)S(1)}, u32[]{:S(2)}, u32[]{:S(2)}) %collective-permute-start.26) | collective-permute-done | bytes 262176 | tf_op jit(solution)/shard_map/ppermute | solution.py:31
  194.1 10.3 %collective-permute-done.27.refs_3_ = bf16[1024,128]{1,0:T(8,128)(2,1)S(1)} collective-permute-done((bf16[1024,128]{1,0:T(8,128)(2,1)S(1)}, bf16[1024,128]{1,0:T(8,128)(2,1)S(1)}, u32[]{:S(2)}, u32[]{:S(2)}) %collective-permute-start.27) | collective-permute-done | bytes 262176 | tf_op jit(solution)/shard_map/ppermute | solution.py:31
  205.3 5.2 %collective-permute-done.31.refs_8_ = bf16[1024,128]{1,0:T(8,128)(2,1)S(1)} collective-permute-done((bf16[1024,128]{1,0:T(8,128)(2,1)S(1)}, bf16[1024,128]{1,0:T(8,128)(2,1)S(1)}, u32[]{:S(2)}, u32[]{:S(2)}) %collective-permute-start.31) | collective-permute-done | bytes 262176 | tf_op jit(solution)/shard_map/ppermute | solution.py:31
  210.5 2.6 %shard_map.53 = (bf16[2048,128]{1,0:T(8,128)(2,1)}, bf16[1024,128]{1,0:T(8,128)(2,1)S(1)}) custom-call(s32[5]{0:T(128)S(1)} %stack.38.place, bf16[1024,256]{1,0:T(8,128)(2,1)S(1)} %maximum_select_fusion.refs_0_.x_ref, bf16[1024,256]{1,0:T(8,128)(2,1)S(1)} %shard_map.52.refs_0_, bf16[1024,256]{1,0:T(8,128)(2,1)S(1)} %collective-permute-done.24.refs_1_, ...), custom_call_target="tpu_custom_call" | custom-call | tf_op jit(solution)/shard_map/pallas_call | solution.py:309
  213.1 2.6 %collective-permute-start.33 = (bf16[1024,128]{1,0:T(8,128)(2,1)S(1)}, bf16[1024,128]{1,0:T(8,128)(2,1)S(1)}, u32[]{:S(2)}, u32[]{:S(2)}) collective-permute-start(bf16[1024,128]{1,0:T(8,128)(2,1)S(1)} %get-tuple-element.20), channel_id=1, source_target_pairs={{0,1},{1,0},{2,3},{3,2},{4,5},{5,4},{6,7},{7,6},{8,9},{9,8},{10,11... | collective-permute-start | bytes 786440 | tf_op jit(solution)/shard_map/ppermute | solution.py:31
  (101 shorter events, 35.2 us)
Async XLA Ops:
  1.1 11.9 %collective-permute-start = (bf16[1024,128]{1,0:T(8,128)(2,1)S(1)}, bf16[1024,128]{1,0:T(8,128)(2,1)S(1)}, u32[]{:S(2)}, u32[]{:S(2)}) collective-permute-start(bf16[1024,128]{1,0:T(8,128)(2,1)S(1)} %get-tuple-element.22), channel_id=1, source_target_pairs={{0,1},{1,0},{2,3},{3,2},{4,5},{5,4},{6,7},{7,6},{8,9},{9,8},{10,11... | collective-permute-start | bytes 786440 | tf_op jit(solution)/shard_map/ppermute | solution.py:31
  5.3 10.7 %collective-permute-start.3 = (bf16[128,512]{1,0:T(8,128)(2,1)S(1)}, bf16[128,512]{1,0:T(8,128)(2,1)S(1)}, u32[]{:S(2)}, u32[]{:S(2)}) collective-permute-start(bf16[128,512]{1,0:T(8,128)(2,1)S(1)} %pad_maximum_fusion.5), channel_id=1, source_target_pairs={{0,192},{16,208},{32,224},{48,240},{64,0},{80,16},{96,32},{112,48}... | collective-permute-start | bytes 393224 | tf_op jit(solution)/shard_map/ppermute | solution.py:36
  9.7 12.0 %collective-permute-start.2 = (bf16[128,512]{1,0:T(8,128)(2,1)S(1)}, bf16[128,512]{1,0:T(8,128)(2,1)S(1)}, u32[]{:S(2)}, u32[]{:S(2)}) collective-permute-start(bf16[128,512]{1,0:T(8,128)(2,1)S(1)} %pad_maximum_fusion.5), channel_id=1, source_target_pairs={{0,128},{16,144},{32,160},{48,176},{64,192},{80,208},{96,224},{112... | collective-permute-start | bytes 393224 | tf_op jit(solution)/shard_map/ppermute | solution.py:36
  10.7 11.0 %collective-permute-start.1 = (bf16[128,512]{1,0:T(8,128)(2,1)S(1)}, bf16[128,512]{1,0:T(8,128)(2,1)S(1)}, u32[]{:S(2)}, u32[]{:S(2)}) collective-permute-start(bf16[128,512]{1,0:T(8,128)(2,1)S(1)} %pad_maximum_fusion.5), channel_id=1, source_target_pairs={{0,64},{16,80},{32,96},{48,112},{64,128},{80,144},{96,160},{112,17... | collective-permute-start | bytes 393224 | tf_op jit(solution)/shard_map/ppermute | solution.py:36
  13.2 28.8 %collective-permute-start.5 = (bf16[1024,256]{1,0:T(8,128)(2,1)S(1)}, bf16[1024,256]{1,0:T(8,128)(2,1)S(1)}, u32[]{:S(2)}, u32[]{:S(2)}) collective-permute-start(bf16[1024,256]{1,0:T(8,128)(2,1)S(1)} %maximum_select_fusion.refs_0_.x_ref), channel_id=1, source_target_pairs={{0,2},{1,3},{2,4},{3,5},{4,6},{5,7},{6,0},{7,1},{8,10},{9,11},{10,... | collective-permute-start | bytes 1572872 | tf_op jit(solution)/shard_map/ppermute | solution.py:31
  14.5 29.6 %collective-permute-start.4 = (bf16[1024,256]{1,0:T(8,128)(2,1)S(1)}, bf16[1024,256]{1,0:T(8,128)(2,1)S(1)}, u32[]{:S(2)}, u32[]{:S(2)}) collective-permute-start(bf16[1024,256]{1,0:T(8,128)(2,1)S(1)} %maximum_select_fusion.refs_0_.x_ref), channel_id=1, source_target_pairs={{0,6},{1,7},{2,0},{3,1},{4,2},{5,3},{6,4},{7,5},{8,14},{9,15},{10,... | collective-permute-start | bytes 1572872 | tf_op jit(solution)/shard_map/ppermute | solution.py:31
  21.8 9.6 %collective-permute-start.15 = (bf16[4,128,384]{2,1,0:T(8,128)(2,1)S(1)}, bf16[4,128,384]{2,1,0:T(8,128)(2,1)S(1)}, u32[]{:S(2)}, u32[]{:S(2)}) collective-permute-start(bf16[4,128,384]{2,1,0:T(8,128)(2,1)S(1)} %pad_maximum_fusion.1.refs_0_), channel_id=1, source_target_pairs={{0,48},{16,0},{32,16},{48,32},{64,112},{80,64},{96,80},{112,96},{1... | collective-permute-start | bytes 1179656 | tf_op jit(solution)/shard_map/ppermute | solution.py:36
  24.2 17.8 %collective-permute-start.14 = (bf16[4,128,384]{2,1,0:T(8,128)(2,1)S(1)}, bf16[4,128,384]{2,1,0:T(8,128)(2,1)S(1)}, u32[]{:S(2)}, u32[]{:S(2)}) collective-permute-start(bf16[4,128,384]{2,1,0:T(8,128)(2,1)S(1)} %pad_maximum_fusion.1.refs_0_), channel_id=1, source_target_pairs={{0,32},{16,48},{32,0},{48,16},{64,96},{80,112},{96,64},{112,80},{1... | collective-permute-start | bytes 1179656 | tf_op jit(solution)/shard_map/ppermute | solution.py:36
  25.0 21.2 %collective-permute-start.8 = (bf16[1024,256]{1,0:T(8,128)(2,1)S(1)}, bf16[1024,256]{1,0:T(8,128)(2,1)S(1)}, u32[]{:S(2)}, u32[]{:S(2)}) collective-permute-start(bf16[1024,256]{1,0:T(8,128)(2,1)S(1)} %maximum_select_fusion.refs_0_.x_ref), channel_id=1, source_target_pairs={{0,8},{1,9},{2,10},{3,11},{4,12},{5,13},{6,14},{7,15},{8,0},{9,1},... | collective-permute-start | bytes 1572872 | tf_op jit(solution)/shard_map/ppermute | solution.py:31
  31.4 12.9 %collective-permute-start.16 = (bf16[4,128,384]{2,1,0:T(8,128)(2,1)S(1)}, bf16[4,128,384]{2,1,0:T(8,128)(2,1)S(1)}, u32[]{:S(2)}, u32[]{:S(2)}) collective-permute-start(bf16[4,128,384]{2,1,0:T(8,128)(2,1)S(1)} %pad_maximum_fusion.1.refs_0_), channel_id=1, source_target_pairs={{0,1},{1,0},{2,3},{3,2},{4,5},{5,4},{6,7},{7,6},{8,9},{9,8},{10,11... | collective-permute-start | bytes 1179656 | tf_op jit(solution)/shard_map/ppermute | solution.py:31
  42.0 12.9 %collective-permute-start.13 = (bf16[4,128,384]{2,1,0:T(8,128)(2,1)S(1)}, bf16[4,128,384]{2,1,0:T(8,128)(2,1)}, u32[]{:S(2)}, u32[]{:S(2)}) collective-permute-start(bf16[4,128,384]{2,1,0:T(8,128)(2,1)S(1)} %pad_maximum_fusion.1.refs_0_), channel_id=1, source_target_pairs={{0,16},{16,32},{32,48},{48,0},{64,80},{80,96},{96,112},{112,64},{1... | collective-permute-start | bytes 1179656 | tf_op jit(solution)/shard_map/ppermute | solution.py:36
  42.0 15.6 %collective-permute-start.19 = (bf16[4,128,384]{2,1,0:T(8,128)(2,1)S(1)}, bf16[4,128,384]{2,1,0:T(8,128)(2,1)S(1)}, u32[]{:S(2)}, u32[]{:S(2)}) collective-permute-start(bf16[4,128,384]{2,1,0:T(8,128)(2,1)S(1)} %collective-permute-done.15.refs_3_), channel_id=1, source_target_pairs={{0,1},{1,0},{2,3},{3,2},{4,5},{5,4},{6,7},{7,6},{8,9},{9,8},{10,11... | collective-permute-start | bytes 1179656 | tf_op jit(solution)/shard_map/ppermute | solution.py:31
  44.1 14.7 %collective-permute-start.18 = (bf16[4,128,384]{2,1,0:T(8,128)(2,1)S(1)}, bf16[4,128,384]{2,1,0:T(8,128)(2,1)S(1)}, u32[]{:S(2)}, u32[]{:S(2)}) collective-permute-start(bf16[4,128,384]{2,1,0:T(8,128)(2,1)S(1)} %collective-permute-done.14.refs_2_), channel_id=1, source_target_pairs={{0,1},{1,0},{2,3},{3,2},{4,5},{5,4},{6,7},{7,6},{8,9},{9,8},{10,11... | collective-permute-start | bytes 1179656 | tf_op jit(solution)/shard_map/ppermute | solution.py:31
  45.0 15.8 %collective-permute-start.6 = (bf16[1024,128]{1,0:T(8,128)(2,1)S(1)}, bf16[1024,128]{1,0:T(8,128)(2,1)}, u32[]{:S(2)}, u32[]{:S(2)}) collective-permute-start(bf16[1024,128]{1,0:T(8,128)(2,1)S(1)} %slice.24), channel_id=1, source_target_pairs={{0,2},{1,3},{2,4},{3,5},{4,6},{5,7},{6,0},{7,1},{8,10},{9,11},{10,... | collective-permute-start | bytes 786440 | tf_op jit(solution)/shard_map/ppermute | solution.py:31
  46.3 39.4 %collective-permute-start.12 = (bf16[1024,256]{1,0:T(8,128)(2,1)S(1)}, bf16[1024,256]{1,0:T(8,128)(2,1)S(1)}, u32[]{:S(2)}, u32[]{:S(2)}) collective-permute-start(bf16[1024,256]{1,0:T(8,128)(2,1)S(1)} %collective-permute-done.8.refs_5_), channel_id=1, source_target_pairs={{0,2},{1,3},{2,4},{3,5},{4,6},{5,7},{6,0},{7,1},{8,10},{9,11},{10,... | collective-permute-start | bytes 1572872 | tf_op jit(solution)/shard_map/ppermute | solution.py:31
  54.8 30.8 %collective-permute-start.9 = (bf16[1024,256]{1,0:T(8,128)(2,1)S(1)}, bf16[1024,256]{1,0:T(8,128)(2,1)S(1)}, u32[]{:S(2)}, u32[]{:S(2)}) collective-permute-start(bf16[1024,256]{1,0:T(8,128)(2,1)S(1)} %collective-permute-done.8.refs_5_), channel_id=1, source_target_pairs={{0,6},{1,7},{2,0},{3,1},{4,2},{5,3},{6,4},{7,5},{8,14},{9,15},{10,... | collective-permute-start | bytes 1572872 | tf_op jit(solution)/shard_map/ppermute | solution.py:31
  58.3 15.5 %collective-permute-start.7 = (bf16[1024,128]{1,0:T(8,128)(2,1)S(1)}, bf16[1024,128]{1,0:T(8,128)(2,1)}, u32[]{:S(2)}, u32[]{:S(2)}) collective-permute-start(bf16[1024,128]{1,0:T(8,128)(2,1)S(1)} %slice.25), channel_id=1, source_target_pairs={{0,6},{1,7},{2,0},{3,1},{4,2},{5,3},{6,4},{7,5},{8,14},{9,15},{10,... | collective-permute-start | bytes 786440 | tf_op jit(solution)/shard_map/ppermute | solution.py:31
  59.6 17.0 %collective-permute-start.17 = (bf16[4,128,384]{2,1,0:T(8,128)(2,1)}, bf16[4,128,384]{2,1,0:T(8,128)(2,1)}, u32[]{:S(2)}, u32[]{:S(2)}) collective-permute-start(bf16[4,128,384]{2,1,0:T(8,128)(2,1)} %collective-permute-done.13.refs_1_), channel_id=1, source_target_pairs={{0,1},{1,0},{2,3},{3,2},{4,5},{5,4},{6,7},{7,6},{8,9},{9,8},{10,11... | collective-permute-start | bytes 1179656 | tf_op jit(solution)/shard_map/ppermute | solution.py:31
  60.8 24.9 %collective-permute-start.10 = (bf16[1024,128]{1,0:T(8,128)(2,1)}, bf16[1024,128]{1,0:T(8,128)(2,1)}, u32[]{:S(2)}, u32[]{:S(2)}) collective-permute-start(bf16[1024,128]{1,0:T(8,128)(2,1)} %collective-permute-done.6.refs_2_), channel_id=1, source_target_pairs={{0,8},{1,9},{2,10},{3,11},{4,12},{5,13},{6,14},{7,15},{8,0},{9,1},... | collective-permute-start | bytes 786440 | tf_op jit(solution)/shard_map/ppermute | solution.py:31
  73.8 11.9 %collective-permute-start.11 = (bf16[1024,128]{1,0:T(8,128)(2,1)}, bf16[1024,128]{1,0:T(8,128)(2,1)}, u32[]{:S(2)}, u32[]{:S(2)}) collective-permute-start(bf16[1024,128]{1,0:T(8,128)(2,1)} %collective-permute-done.7.refs_3_), channel_id=1, source_target_pairs={{0,8},{1,9},{2,10},{3,11},{4,12},{5,13},{6,14},{7,15},{8,0},{9,1},... | collective-permute-start | bytes 786440 | tf_op jit(solution)/shard_map/ppermute | solution.py:31
  92.4 49.5 %all-to-all-start = ((bf16[32,64,384]{2,1,0:T(8,128)(2,1)}), bf16[32,64,384]{2,1,0:T(8,128)(2,1)S(1)}, u32[]{:S(2)}, u32[]{:S(2)}) async-start(bf16[32,64,384]{2,1,0:T(8,128)(2,1)} %bitcast.9), calls=%async_computation | async-start | bytes 3145728 | tf_op jit(solution)/shard_map/all_to_all | solution.py:324
  102.4 10.6 %collective-permute-start.22 = (bf16[4,128,128]{2,1,0:T(8,128)(2,1)S(1)}, bf16[4,128,128]{2,1,0:T(8,128)(2,1)S(1)}, u32[]{:S(2)}, u32[]{:S(2)}) collective-permute-start(bf16[4,128,128]{2,1,0:T(8,128)(2,1)S(1)} %pad_maximum_fusion.4.refs_0_), channel_id=1, source_target_pairs={{0,48},{16,0},{32,16},{48,32},{64,112},{80,64},{96,80},{112,96},{1... | collective-permute-start | bytes 393224 | tf_op jit(solution)/shard_map/ppermute | solution.py:36
  105.0 9.0 %collective-permute-start.21 = (bf16[4,128,128]{2,1,0:T(8,128)(2,1)S(1)}, bf16[4,128,128]{2,1,0:T(8,128)(2,1)S(1)}, u32[]{:S(2)}, u32[]{:S(2)}) collective-permute-start(bf16[4,128,128]{2,1,0:T(8,128)(2,1)S(1)} %pad_maximum_fusion.4.refs_0_), channel_id=1, source_target_pairs={{0,32},{16,48},{32,0},{48,16},{64,96},{80,112},{96,64},{112,80},{1... | collective-permute-start | bytes 393224 | tf_op jit(solution)/shard_map/ppermute | solution.py:36
  105.6 11.4 %collective-permute-start.20 = (bf16[4,128,128]{2,1,0:T(8,128)(2,1)S(1)}, bf16[4,128,128]{2,1,0:T(8,128)(2,1)S(1)}, u32[]{:S(2)}, u32[]{:S(2)}) collective-permute-start(bf16[4,128,128]{2,1,0:T(8,128)(2,1)S(1)} %pad_maximum_fusion.4.refs_0_), channel_id=1, source_target_pairs={{0,16},{16,32},{32,48},{48,0},{64,80},{80,96},{96,112},{112,64},{1... | collective-permute-start | bytes 393224 | tf_op jit(solution)/shard_map/ppermute | solution.py:36
  144.8 23.9 %all-to-all-start.1 = ((bf16[32,72,128]{2,1,0:T(8,128)(2,1)}), bf16[32,72,128]{2,1,0:T(8,128)(2,1)S(1)}, u32[]{:S(2)}, u32[]{:S(2)}) async-start(bf16[32,72,128]{2,1,0:T(8,128)(2,1)} %copy-done), calls=%async_computation.1 | async-start | bytes 1179648 | tf_op jit(solution)/shard_map/all_to_all | solution.py:324
  169.6 15.9 %collective-permute-start.25 = (bf16[1024,256]{1,0:T(8,128)(2,1)S(1)}, bf16[1024,256]{1,0:T(8,128)(2,1)S(1)}, u32[]{:S(2)}, u32[]{:S(2)}) collective-permute-start(bf16[1024,256]{1,0:T(8,128)(2,1)S(1)} %shard_map.52.refs_0_), channel_id=1, source_target_pairs={{0,2},{1,3},{2,4},{3,5},{4,6},{5,7},{6,0},{7,1},{8,10},{9,11},{10,... | collective-permute-start | bytes 1572872 | tf_op jit(solution)/shard_map/ppermute | solution.py:31
  170.6 15.1 %collective-permute-start.28 = (bf16[1024,256]{1,0:T(8,128)(2,1)S(1)}, bf16[1024,256]{1,0:T(8,128)(2,1)S(1)}, u32[]{:S(2)}, u32[]{:S(2)}) collective-permute-start(bf16[1024,256]{1,0:T(8,128)(2,1)S(1)} %shard_map.52.refs_0_), channel_id=1, source_target_pairs={{0,8},{1,9},{2,10},{3,11},{4,12},{5,13},{6,14},{7,15},{8,0},{9,1},... | collective-permute-start | bytes 1572872 | tf_op jit(solution)/shard_map/ppermute | solution.py:31
  170.6 17.8 %collective-permute-start.24 = (bf16[1024,256]{1,0:T(8,128)(2,1)S(1)}, bf16[1024,256]{1,0:T(8,128)(2,1)S(1)}, u32[]{:S(2)}, u32[]{:S(2)}) collective-permute-start(bf16[1024,256]{1,0:T(8,128)(2,1)S(1)} %shard_map.52.refs_0_), channel_id=1, source_target_pairs={{0,6},{1,7},{2,0},{3,1},{4,2},{5,3},{6,4},{7,5},{8,14},{9,15},{10,... | collective-permute-start | bytes 1572872 | tf_op jit(solution)/shard_map/ppermute | solution.py:31
  185.6 19.7 %collective-permute-start.32 = (bf16[1024,256]{1,0:T(8,128)(2,1)S(1)}, bf16[1024,256]{1,0:T(8,128)(2,1)S(1)}, u32[]{:S(2)}, u32[]{:S(2)}) collective-permute-start(bf16[1024,256]{1,0:T(8,128)(2,1)S(1)} %collective-permute-done.28.refs_5_), channel_id=1, source_target_pairs={{0,2},{1,3},{2,4},{3,5},{4,6},{5,7},{6,0},{7,1},{8,10},{9,11},{10,... | collective-permute-start | bytes 1572872 | tf_op jit(solution)/shard_map/ppermute | solution.py:31
  185.7 19.6 %collective-permute-start.29 = (bf16[1024,256]{1,0:T(8,128)(2,1)S(1)}, bf16[1024,256]{1,0:T(8,128)(2,1)S(1)}, u32[]{:S(2)}, u32[]{:S(2)}) collective-permute-start(bf16[1024,256]{1,0:T(8,128)(2,1)S(1)} %collective-permute-done.28.refs_5_), channel_id=1, source_target_pairs={{0,6},{1,7},{2,0},{3,1},{4,2},{5,3},{6,4},{7,5},{8,14},{9,15},{10,... | collective-permute-start | bytes 1572872 | tf_op jit(solution)/shard_map/ppermute | solution.py:31
  188.4 16.0 %collective-permute-start.27 = (bf16[1024,128]{1,0:T(8,128)(2,1)S(1)}, bf16[1024,128]{1,0:T(8,128)(2,1)S(1)}, u32[]{:S(2)}, u32[]{:S(2)}) collective-permute-start(bf16[1024,128]{1,0:T(8,128)(2,1)S(1)} %slice.27), channel_id=1, source_target_pairs={{0,6},{1,7},{2,0},{3,1},{4,2},{5,3},{6,4},{7,5},{8,14},{9,15},{10,... | collective-permute-start | bytes 786440 | tf_op jit(solution)/shard_map/ppermute | solution.py:31
  194.1 11.2 %collective-permute-start.30 = (bf16[1024,128]{1,0:T(8,128)(2,1)S(1)}, bf16[1024,128]{1,0:T(8,128)(2,1)S(1)}, u32[]{:S(2)}, u32[]{:S(2)}) collective-permute-start(bf16[1024,128]{1,0:T(8,128)(2,1)S(1)} %collective-permute-done.26.refs_2_), channel_id=1, source_target_pairs={{0,8},{1,9},{2,10},{3,11},{4,12},{5,13},{6,14},{7,15},{8,0},{9,1},... | collective-permute-start | bytes 786440 | tf_op jit(solution)/shard_map/ppermute | solution.py:31
  (24 other events, 216.2 us)

commit v4 on v3

--- a/solution.py
+++ b/solution.py
@@ -60,18 +60,22 @@
     return _over_row(x, lambda z, h: z * 4 + (h + d) % 4)
 
 
-def gather_chips(x):
-    a = y_up(x)
+def gather_chips(x, halves=None):
+    if halves is None:
+        a = (y_up(x),)
+        left = a[0][:, :HS]
+    else:
+        a = (y_up(halves[0]), y_up(halves[1]))
+        left = a[0]
     b = y_down(x)
     p = z_swap(x)
-    left = a[:, :HS]
     fl = y_up(left)
     fr = y_down(b[:, HS:])
     pa = y_up(p)
     pb = y_down(p)
     gl = z_swap(fl)
     gr = z_swap(fr)
-    return (x, b, fl, fr, a, p, pb, gl, gr, pa)
+    return (x, b, fl, fr, *a, p, pb, gl, gr, pa)
 
 
 def over_z_hi(w):
@@ -196,7 +200,7 @@
 
 
 def _out_kernel(place, x_ref, *refs):
-    pieces, (w_ref, own_ref, other_ref) = refs[:10], refs[10:]
+    pieces, (w_ref, own_ref, other_ref) = refs[:-3], refs[-3:]
     core = place[4]
 
     for tile in range(COLS // TILE):
@@ -280,7 +284,7 @@
     out_ref[:, 64 : 64 + STAT_ROWS, :] = stats.astype(BF16).reshape(32, STAT_ROWS, HS)
 
 
-def _merge_kernel(row_ref, lse_ref, col_ref, out_ref):
+def _merge_kernel(row_ref, lse_ref, col_ref, out_ref, left_ref, right_ref):
     stats = col_ref[:, :, 64:, :].reshape(32 * STAT_ROWS, HS)
     source = lax.broadcasted_iota(jnp.int32, (HS, 32 * STAT_ROWS), 1)
     entry = lax.broadcasted_iota(jnp.int32, (HS, 32 * STAT_ROWS), 0)
@@ -299,7 +303,9 @@
         for head in range(2):
             n = 2 * block + head
             o = rf[:, n : n + 1] * row_ref[head, rows, :] + cf[:, n : n + 1] * col_ref[block, head, :64, :].astype(F32)
-            out_ref[rows, head * HS : (head + 1) * HS] = o.astype(BF16)
+            o = o.astype(BF16)
+            out_ref[rows, head * HS : (head + 1) * HS] = o
+            (left_ref, right_ref)[head][rows, :] = o
 
 
 def _call(kernel, out, *args, scalars=0, flops=0, scratch=(), mib=24):
@@ -366,9 +372,16 @@
     by_column, w = lax.optimization_barrier((by_column, w))
     col_out = _call(_column_kernel, shape((32, 64 + STAT_ROWS, HS), BF16), by_column)
     col_out = exchange_columns(col_out).reshape(16, 2, 64 + STAT_ROWS, HS)
-    att = _call(_merge_kernel, shape((COLS, 2 * HS), BF16), *row, col_out)
+    one = shape((COLS, HS), BF16)
+    att, *halves = _call(_merge_kernel, (shape((COLS, 2 * HS), BF16), one, one), *row, col_out)
     out_own, out_other = _call(
-        _out_kernel, (shape((2 * COLS, HS), BF16), shape((COLS, HS), BF16)), place, x, *gather_chips(att), w, scalars=1
+        _out_kernel,
+        (shape((2 * COLS, HS), BF16), shape((COLS, HS), BF16)),
+        place,
+        x,
+        *gather_chips(att, halves),
+        w,
+        scalars=1,
     )
     return lax.dynamic_update_slice_in_dim(out_own, core_swap(out_other), (1 - core) * COLS, 0)
 

time: 218 us -> 214 us (0.982)
  waiting for transfers between devices: 108 us -> 102 us
    ppermute x25 -> x26, waiting for transfers between devices: 45.8 us -> 40.6 us  [_over_col(): return lax.ppermute(x, 'col', pairs)]
    ppermute x25 -> x26, starting transfers between devices: 45.6 us -> 46.8 us  [_over_col(): return lax.ppermute(x, 'col', pairs)]
  transfers between devices with their start and end apart: 36 -> 37, of which waited for: 16 -> 15; matrix products, arithmetic and copies ran while one was open for 1% -> 1% of each run, Pallas kernels for 4% -> 5%
where the time goes in v4:
time: 214 us
  waiting for transfers between devices  102 us (48%)
  starting transfers between devices  77.6 us (36%)
  Pallas kernels  22.1 us (10%)
  local copies, waits for them, and re-layouts  10 us (5%)
    ppermute x26, starting transfers between devices, _over_col(): return lax.ppermute(x, 'col', pairs)  46.8 us
    ppermute x26, waiting for transfers between devices, _over_col(): return lax.ppermute(x, 'col', pairs)  40.6 us
    all_to_all x2, waiting for transfers between devices, exchange_columns(): lax.all_to_all(x, ('row', 'col'), split_axis=0, concat_axis=0, axis_index...  34.2 us
    ppermute x9, waiting for transfers between devices, _over_row(): return lax.ppermute(x, 'row', pairs)  27.5 us
    pallas_call x8, Pallas kernels, _call(): pl.pallas_call(kernel, out_shape=out, in_specs=[smem] * scalars + [vmem]...  22.1 us
    all_to_all x2, starting transfers between devices, exchange_columns(): lax.all_to_all(x, ('row', 'col'), split_axis=0, concat_axis=0, axis_index...  16 us
    ppermute x9, starting transfers between devices, _over_row(): return lax.ppermute(x, 'row', pairs)  14.7 us
    unnamed x40, local copies, waits for them, and re-layouts  8.08 us
  transfers between devices with their start and end apart: 37, of which 15 were waited for; matrix products, arithmetic and copies ran while one was open for 1% of the time, Pallas kernels for 5%

profile of v4, /device:TPU:1, one launch (start us, length us, event | category | flops | bytes accessed | tf_op | source)
XLA Modules:
  0.0 213.6 jit_solution(6945310696080285695)
XLA Ops:
  1.1 3.3 %collective-permute-start = (bf16[1024,128]{1,0:T(8,128)(2,1)S(1)}, bf16[1024,128]{1,0:T(8,128)(2,1)S(1)}, u32[]{:S(2)}, u32[]{:S(2)}) collective-permute-start(bf16[1024,128]{1,0:T(8,128)(2,1)S(1)} %get-tuple-element.28), channel_id=1, source_target_pairs={{0,1},{1,0},{2,3},{3,2},{4,5},{5,4},{6,7},{7,6},{8,9},{9,8},{10,11... | collective-permute-start | bytes 786440 | tf_op jit(solution)/shard_map/ppermute | solution.py:31
  5.3 4.4 %collective-permute-start.3 = (bf16[128,512]{1,0:T(8,128)(2,1)S(1)}, bf16[128,512]{1,0:T(8,128)(2,1)S(1)}, u32[]{:S(2)}, u32[]{:S(2)}) collective-permute-start(bf16[128,512]{1,0:T(8,128)(2,1)S(1)} %pad_maximum_fusion.5), channel_id=1, source_target_pairs={{0,192},{16,208},{32,224},{48,240},{64,0},{80,16},{96,32},{112,48}... | collective-permute-start | bytes 393224 | tf_op jit(solution)/shard_map/ppermute | solution.py:36
  10.7 2.3 %collective-permute-start.1 = (bf16[128,512]{1,0:T(8,128)(2,1)S(1)}, bf16[128,512]{1,0:T(8,128)(2,1)S(1)}, u32[]{:S(2)}, u32[]{:S(2)}) collective-permute-start(bf16[128,512]{1,0:T(8,128)(2,1)S(1)} %pad_maximum_fusion.5), channel_id=1, source_target_pairs={{0,64},{16,80},{32,96},{48,112},{64,128},{80,144},{96,160},{112,17... | collective-permute-start | bytes 393224 | tf_op jit(solution)/shard_map/ppermute | solution.py:36
  16.1 5.7 %collective-permute-done.2 = bf16[128,512]{1,0:T(8,128)(2,1)S(1)} collective-permute-done((bf16[128,512]{1,0:T(8,128)(2,1)S(1)}, bf16[128,512]{1,0:T(8,128)(2,1)S(1)}, u32[]{:S(2)}, u32[]{:S(2)}) %collective-permute-start.2) | collective-permute-done | bytes 131104 | tf_op jit(solution)/shard_map/ppermute | solution.py:36
  21.8 2.4 %collective-permute-start.15 = (bf16[4,128,384]{2,1,0:T(8,128)(2,1)S(1)}, bf16[4,128,384]{2,1,0:T(8,128)(2,1)S(1)}, u32[]{:S(2)}, u32[]{:S(2)}) collective-permute-start(bf16[4,128,384]{2,1,0:T(8,128)(2,1)S(1)} %pad_maximum_fusion.1.refs_0_), channel_id=1, source_target_pairs={{0,48},{16,0},{32,16},{48,32},{64,112},{80,64},{96,80},{112,96},{1... | collective-permute-start | bytes 1179656 | tf_op jit(solution)/shard_map/ppermute | solution.py:36
  25.0 2.7 %collective-permute-start.8 = (bf16[1024,256]{1,0:T(8,128)(2,1)S(1)}, bf16[1024,256]{1,0:T(8,128)(2,1)S(1)}, u32[]{:S(2)}, u32[]{:S(2)}) collective-permute-start(bf16[1024,256]{1,0:T(8,128)(2,1)S(1)} %maximum_select_fusion.refs_0_.x_ref), channel_id=1, source_target_pairs={{0,8},{1,9},{2,10},{3,11},{4,12},{5,13},{6,14},{7,15},{8,0},{9,1},... | collective-permute-start | bytes 1572872 | tf_op jit(solution)/shard_map/ppermute | solution.py:31
  27.7 3.7 %collective-permute-done.15.refs_3_ = bf16[4,128,384]{2,1,0:T(8,128)(2,1)S(1)} collective-permute-done((bf16[4,128,384]{2,1,0:T(8,128)(2,1)S(1)}, bf16[4,128,384]{2,1,0:T(8,128)(2,1)S(1)}, u32[]{:S(2)}, u32[]{:S(2)}) %collective-permute-start.15) | collective-permute-done | bytes 393248 | tf_op jit(solution)/shard_map/ppermute | solution.py:36
  31.4 10.6 %collective-permute-start.16 = (bf16[4,128,384]{2,1,0:T(8,128)(2,1)S(1)}, bf16[4,128,384]{2,1,0:T(8,128)(2,1)S(1)}, u32[]{:S(2)}, u32[]{:S(2)}) collective-permute-start(bf16[4,128,384]{2,1,0:T(8,128)(2,1)S(1)} %pad_maximum_fusion.1.refs_0_), channel_id=1, source_target_pairs={{0,1},{1,0},{2,3},{3,2},{4,5},{5,4},{6,7},{7,6},{8,9},{9,8},{10,11... | collective-permute-start | bytes 1179656 | tf_op jit(solution)/shard_map/ppermute | solution.py:31
  42.0 2.1 collective-permute-start.19
  47.6 7.3 %collective-permute-done.13.refs_1_ = bf16[4,128,384]{2,1,0:T(8,128)(2,1)} collective-permute-done((bf16[4,128,384]{2,1,0:T(8,128)(2,1)S(1)}, bf16[4,128,384]{2,1,0:T(8,128)(2,1)}, u32[]{:S(2)}, u32[]{:S(2)}) %collective-permute-start.13) | collective-permute-done | bytes 393248 | tf_op jit(solution)/shard_map/ppermute | solution.py:36
  54.8 2.7 %collective-permute-start.9 = (bf16[1024,256]{1,0:T(8,128)(2,1)S(1)}, bf16[1024,256]{1,0:T(8,128)(2,1)S(1)}, u32[]{:S(2)}, u32[]{:S(2)}) collective-permute-start(bf16[1024,256]{1,0:T(8,128)(2,1)S(1)} %collective-permute-done.8.refs_5_), channel_id=1, source_target_pairs={{0,6},{1,7},{2,0},{3,1},{4,2},{5,3},{6,4},{7,5},{8,14},{9,15},{10,... | collective-permute-start | bytes 1572872 | tf_op jit(solution)/shard_map/ppermute | solution.py:31
  60.8 2.7 %collective-permute-start.10 = (bf16[1024,128]{1,0:T(8,128)(2,1)}, bf16[1024,128]{1,0:T(8,128)(2,1)}, u32[]{:S(2)}, u32[]{:S(2)}) collective-permute-start(bf16[1024,128]{1,0:T(8,128)(2,1)} %collective-permute-done.6.refs_2_), channel_id=1, source_target_pairs={{0,8},{1,9},{2,10},{3,11},{4,12},{5,13},{6,14},{7,15},{8,0},{9,1},... | collective-permute-start | bytes 786440 | tf_op jit(solution)/shard_map/ppermute | solution.py:31
  63.5 10.3 %collective-permute-done.7.refs_3_ = bf16[1024,128]{1,0:T(8,128)(2,1)} collective-permute-done((bf16[1024,128]{1,0:T(8,128)(2,1)S(1)}, bf16[1024,128]{1,0:T(8,128)(2,1)}, u32[]{:S(2)}, u32[]{:S(2)}) %collective-permute-start.7) | collective-permute-done | bytes 262176 | tf_op jit(solution)/shard_map/ppermute | solution.py:31
  73.8 2.7 %collective-permute-start.11 = (bf16[1024,128]{1,0:T(8,128)(2,1)}, bf16[1024,128]{1,0:T(8,128)(2,1)}, u32[]{:S(2)}, u32[]{:S(2)}) collective-permute-start(bf16[1024,128]{1,0:T(8,128)(2,1)} %collective-permute-done.7.refs_3_), channel_id=1, source_target_pairs={{0,8},{1,9},{2,10},{3,11},{4,12},{5,13},{6,14},{7,15},{8,0},{9,1},... | collective-permute-start | bytes 786440 | tf_op jit(solution)/shard_map/ppermute | solution.py:31
  83.2 2.5 %shard_map.46.early_ref = f32[1024,2]{1,0:T(8,128)S(1)} custom-call(bf16[1024,256]{1,0:T(8,128)(2,1)S(1)} %maximum_select_fusion.refs_0_.x_ref, bf16[1024,256]{1,0:T(8,128)(2,1)S(1)} %collective-permute-done.4.refs_1_, bf16[1024,128]{1,0:T(8,128)(2,1)} %collective-permute-done.6.refs_2_, bf16[1024,128]{1,0:T(8,128)(2,1)} %collective-permute-done.7.refs_3_, ...), custom_call_target="tpu_custom_call" | custom-call | flops 1073741824 | bytes 1048576 | tf_op jit(solution)/shard_map/pallas_call | solution.py:315
  85.7 6.7 %shard_map.48.qkv_ref = bf16[16,2,64,384]{3,2,1,0:T(8,128)(2,1)} custom-call(s32[5]{0:T(128)S(1)} %stack.38.place, f32[8,256]{1,0:T(8,128)S(1)} %reshape.9.gain_ref, f32[1024,2]{1,0:T(8,128)S(1)} %shard_map.46.early_ref, bf16[1024,256]{1,0:T(8,128)(2,1)S(1)} %maximum_select_fusion.refs_0_.x_ref, bf16[1024,256]{1,0:T(8,128)(2,1)S(1)} %collective-permute-done.4.refs_1_, ...), custom_call_target="tpu_custom_call" | custom-call | tf_op jit(solution)/shard_map/pallas_call | solution.py:315
  92.4 9.9 %all-to-all-start = ((bf16[32,64,384]{2,1,0:T(8,128)(2,1)}), bf16[32,64,384]{2,1,0:T(8,128)(2,1)S(1)}, u32[]{:S(2)}, u32[]{:S(2)}) async-start(bf16[32,64,384]{2,1,0:T(8,128)(2,1)} %bitcast.9), calls=%async_computation | async-start | bytes 3145728 | tf_op jit(solution)/shard_map/all_to_all | solution.py:330
  102.4 2.6 %collective-permute-start.22 = (bf16[4,128,128]{2,1,0:T(8,128)(2,1)S(1)}, bf16[4,128,128]{2,1,0:T(8,128)(2,1)S(1)}, u32[]{:S(2)}, u32[]{:S(2)}) collective-permute-start(bf16[4,128,128]{2,1,0:T(8,128)(2,1)S(1)} %pad_maximum_fusion.4.refs_0_), channel_id=1, source_target_pairs={{0,48},{16,0},{32,16},{48,32},{64,112},{80,64},{96,80},{112,96},{1... | collective-permute-start | bytes 393224 | tf_op jit(solution)/shard_map/ppermute | solution.py:36
  106.2 6.8 %collective-permute-done.22.refs_3_ = bf16[4,128,128]{2,1,0:T(8,128)(2,1)S(1)} collective-permute-done((bf16[4,128,128]{2,1,0:T(8,128)(2,1)S(1)}, bf16[4,128,128]{2,1,0:T(8,128)(2,1)S(1)}, u32[]{:S(2)}, u32[]{:S(2)}) %collective-permute-start.22) | collective-permute-done | bytes 131104 | tf_op jit(solution)/shard_map/ppermute | solution.py:36
  114.1 3.0 %collective-permute-done.20.refs_1_ = bf16[4,128,128]{2,1,0:T(8,128)(2,1)S(1)} collective-permute-done((bf16[4,128,128]{2,1,0:T(8,128)(2,1)S(1)}, bf16[4,128,128]{2,1,0:T(8,128)(2,1)S(1)}, u32[]{:S(2)}, u32[]{:S(2)}) %collective-permute-start.20) | collective-permute-done | bytes 131104 | tf_op jit(solution)/shard_map/ppermute | solution.py:36
  120.4 21.4 %all-to-all-done.z_ref = bf16[32,64,384]{2,1,0:T(8,128)(2,1)S(1)} async-done(((bf16[32,64,384]{2,1,0:T(8,128)(2,1)}), bf16[32,64,384]{2,1,0:T(8,128)(2,1)S(1)}, u32[]{:S(2)}, u32[]{:S(2)}) %all-to-all-start) | async-done | bytes 1572896 | tf_op jit(solution)/shard_map/all_to_all | solution.py:330
  141.9 2.1 shard_map.51
  144.8 6.2 %all-to-all-start.1 = ((bf16[32,72,128]{2,1,0:T(8,128)(2,1)}), bf16[32,72,128]{2,1,0:T(8,128)(2,1)S(1)}, u32[]{:S(2)}, u32[]{:S(2)}) async-start(bf16[32,72,128]{2,1,0:T(8,128)(2,1)} %copy-done), calls=%async_computation.1 | async-start | bytes 1179648 | tf_op jit(solution)/shard_map/all_to_all | solution.py:330
  150.9 4.9 %shard_map.49 = (f32[2,1024,128]{2,1,0:T(8,128)S(1)}, f32[64,128]{1,0:T(8,128)S(1)}) custom-call(bf16[16,2,64,384]{3,2,1,0:T(8,128)(2,1)} %shard_map.48.qkv_ref), custom_call_target="tpu_custom_call" | custom-call | flops 8589934592 | bytes 1048576 | tf_op jit(solution)/shard_map/pallas_call | solution.py:315
  155.9 12.8 %all-to-all-done.1 = bf16[32,72,128]{2,1,0:T(8,128)(2,1)S(1)} async-done(((bf16[32,72,128]{2,1,0:T(8,128)(2,1)}), bf16[32,72,128]{2,1,0:T(8,128)(2,1)S(1)}, u32[]{:S(2)}, u32[]{:S(2)}) %all-to-all-start.1) | async-done | bytes 589856 | tf_op jit(solution)/shard_map/all_to_all | solution.py:330
  169.6 3.6 %collective-permute-start.24 = (bf16[1024,256]{1,0:T(8,128)(2,1)S(1)}, bf16[1024,256]{1,0:T(8,128)(2,1)S(1)}, u32[]{:S(2)}, u32[]{:S(2)}) collective-permute-start(bf16[1024,256]{1,0:T(8,128)(2,1)S(1)} %get-tuple-element.21.refs_0_), channel_id=1, source_target_pairs={{0,6},{1,7},{2,0},{3,1},{4,2},{5,3},{6,4},{7,5},{8,14},{9,15},{10,... | collective-permute-start | bytes 1572872 | tf_op jit(solution)/shard_map/ppermute | solution.py:31
  173.2 8.8 %collective-permute-done.25.refs_4_ = bf16[1024,128]{1,0:T(8,128)(2,1)S(1)} collective-permute-done((bf16[1024,128]{1,0:T(8,128)(2,1)S(1)}, bf16[1024,128]{1,0:T(8,128)(2,1)S(1)}, u32[]{:S(2)}, u32[]{:S(2)}) %collective-permute-start.25) | collective-permute-done | bytes 262176 | tf_op jit(solution)/shard_map/ppermute | solution.py:31
  182.0 2.5 %collective-permute-done.24.refs_1_ = bf16[1024,256]{1,0:T(8,128)(2,1)S(1)} collective-permute-done((bf16[1024,256]{1,0:T(8,128)(2,1)S(1)}, bf16[1024,256]{1,0:T(8,128)(2,1)S(1)}, u32[]{:S(2)}, u32[]{:S(2)}) %collective-permute-start.24) | collective-permute-done | bytes 524320 | tf_op jit(solution)/shard_map/ppermute | solution.py:31
  184.5 3.5 %collective-permute-start.27 = (bf16[1024,128]{1,0:T(8,128)(2,1)S(1)}, bf16[1024,128]{1,0:T(8,128)(2,1)S(1)}, u32[]{:S(2)}, u32[]{:S(2)}) collective-permute-start(bf16[1024,128]{1,0:T(8,128)(2,1)S(1)} %slice.22), channel_id=1, source_target_pairs={{0,6},{1,7},{2,0},{3,1},{4,2},{5,3},{6,4},{7,5},{8,14},{9,15},{10,... | collective-permute-start | bytes 786440 | tf_op jit(solution)/shard_map/ppermute | solution.py:31
  188.0 2.7 %collective-permute-start.30 = (bf16[1024,256]{1,0:T(8,128)(2,1)S(1)}, bf16[1024,256]{1,0:T(8,128)(2,1)S(1)}, u32[]{:S(2)}, u32[]{:S(2)}) collective-permute-start(bf16[1024,256]{1,0:T(8,128)(2,1)S(1)} %collective-permute-done.29.refs_6_), channel_id=1, source_target_pairs={{0,6},{1,7},{2,0},{3,1},{4,2},{5,3},{6,4},{7,5},{8,14},{9,15},{10,... | collective-permute-start | bytes 1572872 | tf_op jit(solution)/shard_map/ppermute | solution.py:31
  192.8 14.4 %collective-permute-done.28.refs_5_ = bf16[1024,128]{1,0:T(8,128)(2,1)S(1)} collective-permute-done((bf16[1024,128]{1,0:T(8,128)(2,1)S(1)}, bf16[1024,128]{1,0:T(8,128)(2,1)S(1)}, u32[]{:S(2)}, u32[]{:S(2)}) %collective-permute-start.28) | collective-permute-done | bytes 262176 | tf_op jit(solution)/shard_map/ppermute | solution.py:31
  207.1 2.6 %shard_map.53 = (bf16[2048,128]{1,0:T(8,128)(2,1)}, bf16[1024,128]{1,0:T(8,128)(2,1)S(1)}) custom-call(s32[5]{0:T(128)S(1)} %stack.38.place, bf16[1024,256]{1,0:T(8,128)(2,1)S(1)} %maximum_select_fusion.refs_0_.x_ref, bf16[1024,256]{1,0:T(8,128)(2,1)S(1)} %get-tuple-element.21.refs_0_, bf16[1024,256]{1,0:T(8,128)(2,1)S(1)} %collective-permute-done.24.refs_1_, ...), custom_call_target="tpu_custom_call" | custom-call | tf_op jit(solution)/shard_map/pallas_call | solution.py:315
  (102 shorter events, 33.8 us)
Async XLA Ops:
  1.1 11.9 %collective-permute-start = (bf16[1024,128]{1,0:T(8,128)(2,1)S(1)}, bf16[1024,128]{1,0:T(8,128)(2,1)S(1)}, u32[]{:S(2)}, u32[]{:S(2)}) collective-permute-start(bf16[1024,128]{1,0:T(8,128)(2,1)S(1)} %get-tuple-element.28), channel_id=1, source_target_pairs={{0,1},{1,0},{2,3},{3,2},{4,5},{5,4},{6,7},{7,6},{8,9},{9,8},{10,11... | collective-permute-start | bytes 786440 | tf_op jit(solution)/shard_map/ppermute | solution.py:31
  5.3 10.7 %collective-permute-start.3 = (bf16[128,512]{1,0:T(8,128)(2,1)S(1)}, bf16[128,512]{1,0:T(8,128)(2,1)S(1)}, u32[]{:S(2)}, u32[]{:S(2)}) collective-permute-start(bf16[128,512]{1,0:T(8,128)(2,1)S(1)} %pad_maximum_fusion.5), channel_id=1, source_target_pairs={{0,192},{16,208},{32,224},{48,240},{64,0},{80,16},{96,32},{112,48}... | collective-permute-start | bytes 393224 | tf_op jit(solution)/shard_map/ppermute | solution.py:36
  9.7 12.0 %collective-permute-start.2 = (bf16[128,512]{1,0:T(8,128)(2,1)S(1)}, bf16[128,512]{1,0:T(8,128)(2,1)S(1)}, u32[]{:S(2)}, u32[]{:S(2)}) collective-permute-start(bf16[128,512]{1,0:T(8,128)(2,1)S(1)} %pad_maximum_fusion.5), channel_id=1, source_target_pairs={{0,128},{16,144},{32,160},{48,176},{64,192},{80,208},{96,224},{112... | collective-permute-start | bytes 393224 | tf_op jit(solution)/shard_map/ppermute | solution.py:36
  10.7 11.0 %collective-permute-start.1 = (bf16[128,512]{1,0:T(8,128)(2,1)S(1)}, bf16[128,512]{1,0:T(8,128)(2,1)S(1)}, u32[]{:S(2)}, u32[]{:S(2)}) collective-permute-start(bf16[128,512]{1,0:T(8,128)(2,1)S(1)} %pad_maximum_fusion.5), channel_id=1, source_target_pairs={{0,64},{16,80},{32,96},{48,112},{64,128},{80,144},{96,160},{112,17... | collective-permute-start | bytes 393224 | tf_op jit(solution)/shard_map/ppermute | solution.py:36
  13.2 28.8 %collective-permute-start.5 = (bf16[1024,256]{1,0:T(8,128)(2,1)S(1)}, bf16[1024,256]{1,0:T(8,128)(2,1)S(1)}, u32[]{:S(2)}, u32[]{:S(2)}) collective-permute-start(bf16[1024,256]{1,0:T(8,128)(2,1)S(1)} %maximum_select_fusion.refs_0_.x_ref), channel_id=1, source_target_pairs={{0,2},{1,3},{2,4},{3,5},{4,6},{5,7},{6,0},{7,1},{8,10},{9,11},{10,... | collective-permute-start | bytes 1572872 | tf_op jit(solution)/shard_map/ppermute | solution.py:31
  14.5 29.6 %collective-permute-start.4 = (bf16[1024,256]{1,0:T(8,128)(2,1)S(1)}, bf16[1024,256]{1,0:T(8,128)(2,1)S(1)}, u32[]{:S(2)}, u32[]{:S(2)}) collective-permute-start(bf16[1024,256]{1,0:T(8,128)(2,1)S(1)} %maximum_select_fusion.refs_0_.x_ref), channel_id=1, source_target_pairs={{0,6},{1,7},{2,0},{3,1},{4,2},{5,3},{6,4},{7,5},{8,14},{9,15},{10,... | collective-permute-start | bytes 1572872 | tf_op jit(solution)/shard_map/ppermute | solution.py:31
  21.8 9.6 %collective-permute-start.15 = (bf16[4,128,384]{2,1,0:T(8,128)(2,1)S(1)}, bf16[4,128,384]{2,1,0:T(8,128)(2,1)S(1)}, u32[]{:S(2)}, u32[]{:S(2)}) collective-permute-start(bf16[4,128,384]{2,1,0:T(8,128)(2,1)S(1)} %pad_maximum_fusion.1.refs_0_), channel_id=1, source_target_pairs={{0,48},{16,0},{32,16},{48,32},{64,112},{80,64},{96,80},{112,96},{1... | collective-permute-start | bytes 1179656 | tf_op jit(solution)/shard_map/ppermute | solution.py:36
  24.2 17.8 %collective-permute-start.14 = (bf16[4,128,384]{2,1,0:T(8,128)(2,1)S(1)}, bf16[4,128,384]{2,1,0:T(8,128)(2,1)S(1)}, u32[]{:S(2)}, u32[]{:S(2)}) collective-permute-start(bf16[4,128,384]{2,1,0:T(8,128)(2,1)S(1)} %pad_maximum_fusion.1.refs_0_), channel_id=1, source_target_pairs={{0,32},{16,48},{32,0},{48,16},{64,96},{80,112},{96,64},{112,80},{1... | collective-permute-start | bytes 1179656 | tf_op jit(solution)/shard_map/ppermute | solution.py:36
  25.0 21.3 %collective-permute-start.8 = (bf16[1024,256]{1,0:T(8,128)(2,1)S(1)}, bf16[1024,256]{1,0:T(8,128)(2,1)S(1)}, u32[]{:S(2)}, u32[]{:S(2)}) collective-permute-start(bf16[1024,256]{1,0:T(8,128)(2,1)S(1)} %maximum_select_fusion.refs_0_.x_ref), channel_id=1, source_target_pairs={{0,8},{1,9},{2,10},{3,11},{4,12},{5,13},{6,14},{7,15},{8,0},{9,1},... | collective-permute-start | bytes 1572872 | tf_op jit(solution)/shard_map/ppermute | solution.py:31
  31.4 12.9 %collective-permute-start.16 = (bf16[4,128,384]{2,1,0:T(8,128)(2,1)S(1)}, bf16[4,128,384]{2,1,0:T(8,128)(2,1)S(1)}, u32[]{:S(2)}, u32[]{:S(2)}) collective-permute-start(bf16[4,128,384]{2,1,0:T(8,128)(2,1)S(1)} %pad_maximum_fusion.1.refs_0_), channel_id=1, source_target_pairs={{0,1},{1,0},{2,3},{3,2},{4,5},{5,4},{6,7},{7,6},{8,9},{9,8},{10,11... | collective-permute-start | bytes 1179656 | tf_op jit(solution)/shard_map/ppermute | solution.py:31
  42.0 12.9 %collective-permute-start.13 = (bf16[4,128,384]{2,1,0:T(8,128)(2,1)S(1)}, bf16[4,128,384]{2,1,0:T(8,128)(2,1)}, u32[]{:S(2)}, u32[]{:S(2)}) collective-permute-start(bf16[4,128,384]{2,1,0:T(8,128)(2,1)S(1)} %pad_maximum_fusion.1.refs_0_), channel_id=1, source_target_pairs={{0,16},{16,32},{32,48},{48,0},{64,80},{80,96},{96,112},{112,64},{1... | collective-permute-start | bytes 1179656 | tf_op jit(solution)/shard_map/ppermute | solution.py:36
  42.0 15.6 %collective-permute-start.19 = (bf16[4,128,384]{2,1,0:T(8,128)(2,1)S(1)}, bf16[4,128,384]{2,1,0:T(8,128)(2,1)S(1)}, u32[]{:S(2)}, u32[]{:S(2)}) collective-permute-start(bf16[4,128,384]{2,1,0:T(8,128)(2,1)S(1)} %collective-permute-done.15.refs_3_), channel_id=1, source_target_pairs={{0,1},{1,0},{2,3},{3,2},{4,5},{5,4},{6,7},{7,6},{8,9},{9,8},{10,11... | collective-permute-start | bytes 1179656 | tf_op jit(solution)/shard_map/ppermute | solution.py:31
  44.1 14.7 %collective-permute-start.18 = (bf16[4,128,384]{2,1,0:T(8,128)(2,1)S(1)}, bf16[4,128,384]{2,1,0:T(8,128)(2,1)S(1)}, u32[]{:S(2)}, u32[]{:S(2)}) collective-permute-start(bf16[4,128,384]{2,1,0:T(8,128)(2,1)S(1)} %collective-permute-done.14.refs_2_), channel_id=1, source_target_pairs={{0,1},{1,0},{2,3},{3,2},{4,5},{5,4},{6,7},{7,6},{8,9},{9,8},{10,11... | collective-permute-start | bytes 1179656 | tf_op jit(solution)/shard_map/ppermute | solution.py:31
  45.0 15.8 %collective-permute-start.6 = (bf16[1024,128]{1,0:T(8,128)(2,1)S(1)}, bf16[1024,128]{1,0:T(8,128)(2,1)}, u32[]{:S(2)}, u32[]{:S(2)}) collective-permute-start(bf16[1024,128]{1,0:T(8,128)(2,1)S(1)} %slice.20), channel_id=1, source_target_pairs={{0,2},{1,3},{2,4},{3,5},{4,6},{5,7},{6,0},{7,1},{8,10},{9,11},{10,... | collective-permute-start | bytes 786440 | tf_op jit(solution)/shard_map/ppermute | solution.py:31
  46.3 39.4 %collective-permute-start.12 = (bf16[1024,256]{1,0:T(8,128)(2,1)S(1)}, bf16[1024,256]{1,0:T(8,128)(2,1)S(1)}, u32[]{:S(2)}, u32[]{:S(2)}) collective-permute-start(bf16[1024,256]{1,0:T(8,128)(2,1)S(1)} %collective-permute-done.8.refs_5_), channel_id=1, source_target_pairs={{0,2},{1,3},{2,4},{3,5},{4,6},{5,7},{6,0},{7,1},{8,10},{9,11},{10,... | collective-permute-start | bytes 1572872 | tf_op jit(solution)/shard_map/ppermute | solution.py:31
  54.8 30.8 %collective-permute-start.9 = (bf16[1024,256]{1,0:T(8,128)(2,1)S(1)}, bf16[1024,256]{1,0:T(8,128)(2,1)S(1)}, u32[]{:S(2)}, u32[]{:S(2)}) collective-permute-start(bf16[1024,256]{1,0:T(8,128)(2,1)S(1)} %collective-permute-done.8.refs_5_), channel_id=1, source_target_pairs={{0,6},{1,7},{2,0},{3,1},{4,2},{5,3},{6,4},{7,5},{8,14},{9,15},{10,... | collective-permute-start | bytes 1572872 | tf_op jit(solution)/shard_map/ppermute | solution.py:31
  58.3 15.5 %collective-permute-start.7 = (bf16[1024,128]{1,0:T(8,128)(2,1)S(1)}, bf16[1024,128]{1,0:T(8,128)(2,1)}, u32[]{:S(2)}, u32[]{:S(2)}) collective-permute-start(bf16[1024,128]{1,0:T(8,128)(2,1)S(1)} %slice.21), channel_id=1, source_target_pairs={{0,6},{1,7},{2,0},{3,1},{4,2},{5,3},{6,4},{7,5},{8,14},{9,15},{10,... | collective-permute-start | bytes 786440 | tf_op jit(solution)/shard_map/ppermute | solution.py:31
  59.6 17.0 %collective-permute-start.17 = (bf16[4,128,384]{2,1,0:T(8,128)(2,1)}, bf16[4,128,384]{2,1,0:T(8,128)(2,1)}, u32[]{:S(2)}, u32[]{:S(2)}) collective-permute-start(bf16[4,128,384]{2,1,0:T(8,128)(2,1)} %collective-permute-done.13.refs_1_), channel_id=1, source_target_pairs={{0,1},{1,0},{2,3},{3,2},{4,5},{5,4},{6,7},{7,6},{8,9},{9,8},{10,11... | collective-permute-start | bytes 1179656 | tf_op jit(solution)/shard_map/ppermute | solution.py:31
  60.8 24.9 %collective-permute-start.10 = (bf16[1024,128]{1,0:T(8,128)(2,1)}, bf16[1024,128]{1,0:T(8,128)(2,1)}, u32[]{:S(2)}, u32[]{:S(2)}) collective-permute-start(bf16[1024,128]{1,0:T(8,128)(2,1)} %collective-permute-done.6.refs_2_), channel_id=1, source_target_pairs={{0,8},{1,9},{2,10},{3,11},{4,12},{5,13},{6,14},{7,15},{8,0},{9,1},... | collective-permute-start | bytes 786440 | tf_op jit(solution)/shard_map/ppermute | solution.py:31
  73.8 11.9 %collective-permute-start.11 = (bf16[1024,128]{1,0:T(8,128)(2,1)}, bf16[1024,128]{1,0:T(8,128)(2,1)}, u32[]{:S(2)}, u32[]{:S(2)}) collective-permute-start(bf16[1024,128]{1,0:T(8,128)(2,1)} %collective-permute-done.7.refs_3_), channel_id=1, source_target_pairs={{0,8},{1,9},{2,10},{3,11},{4,12},{5,13},{6,14},{7,15},{8,0},{9,1},... | collective-permute-start | bytes 786440 | tf_op jit(solution)/shard_map/ppermute | solution.py:31
  92.4 49.5 %all-to-all-start = ((bf16[32,64,384]{2,1,0:T(8,128)(2,1)}), bf16[32,64,384]{2,1,0:T(8,128)(2,1)S(1)}, u32[]{:S(2)}, u32[]{:S(2)}) async-start(bf16[32,64,384]{2,1,0:T(8,128)(2,1)} %bitcast.9), calls=%async_computation | async-start | bytes 3145728 | tf_op jit(solution)/shard_map/all_to_all | solution.py:330
  102.4 10.6 %collective-permute-start.22 = (bf16[4,128,128]{2,1,0:T(8,128)(2,1)S(1)}, bf16[4,128,128]{2,1,0:T(8,128)(2,1)S(1)}, u32[]{:S(2)}, u32[]{:S(2)}) collective-permute-start(bf16[4,128,128]{2,1,0:T(8,128)(2,1)S(1)} %pad_maximum_fusion.4.refs_0_), channel_id=1, source_target_pairs={{0,48},{16,0},{32,16},{48,32},{64,112},{80,64},{96,80},{112,96},{1... | collective-permute-start | bytes 393224 | tf_op jit(solution)/shard_map/ppermute | solution.py:36
  105.0 9.0 %collective-permute-start.21 = (bf16[4,128,128]{2,1,0:T(8,128)(2,1)S(1)}, bf16[4,128,128]{2,1,0:T(8,128)(2,1)S(1)}, u32[]{:S(2)}, u32[]{:S(2)}) collective-permute-start(bf16[4,128,128]{2,1,0:T(8,128)(2,1)S(1)} %pad_maximum_fusion.4.refs_0_), channel_id=1, source_target_pairs={{0,32},{16,48},{32,0},{48,16},{64,96},{80,112},{96,64},{112,80},{1... | collective-permute-start | bytes 393224 | tf_op jit(solution)/shard_map/ppermute | solution.py:36
  105.6 11.4 %collective-permute-start.20 = (bf16[4,128,128]{2,1,0:T(8,128)(2,1)S(1)}, bf16[4,128,128]{2,1,0:T(8,128)(2,1)S(1)}, u32[]{:S(2)}, u32[]{:S(2)}) collective-permute-start(bf16[4,128,128]{2,1,0:T(8,128)(2,1)S(1)} %pad_maximum_fusion.4.refs_0_), channel_id=1, source_target_pairs={{0,16},{16,32},{32,48},{48,0},{64,80},{80,96},{96,112},{112,64},{1... | collective-permute-start | bytes 393224 | tf_op jit(solution)/shard_map/ppermute | solution.py:36
  144.8 23.9 %all-to-all-start.1 = ((bf16[32,72,128]{2,1,0:T(8,128)(2,1)}), bf16[32,72,128]{2,1,0:T(8,128)(2,1)S(1)}, u32[]{:S(2)}, u32[]{:S(2)}) async-start(bf16[32,72,128]{2,1,0:T(8,128)(2,1)} %copy-done), calls=%async_computation.1 | async-start | bytes 1179648 | tf_op jit(solution)/shard_map/all_to_all | solution.py:330
  169.6 14.8 %collective-permute-start.24 = (bf16[1024,256]{1,0:T(8,128)(2,1)S(1)}, bf16[1024,256]{1,0:T(8,128)(2,1)S(1)}, u32[]{:S(2)}, u32[]{:S(2)}) collective-permute-start(bf16[1024,256]{1,0:T(8,128)(2,1)S(1)} %get-tuple-element.21.refs_0_), channel_id=1, source_target_pairs={{0,6},{1,7},{2,0},{3,1},{4,2},{5,3},{6,4},{7,5},{8,14},{9,15},{10,... | collective-permute-start | bytes 1572872 | tf_op jit(solution)/shard_map/ppermute | solution.py:31
  173.2 14.8 %collective-permute-start.29 = (bf16[1024,256]{1,0:T(8,128)(2,1)S(1)}, bf16[1024,256]{1,0:T(8,128)(2,1)S(1)}, u32[]{:S(2)}, u32[]{:S(2)}) collective-permute-start(bf16[1024,256]{1,0:T(8,128)(2,1)S(1)} %get-tuple-element.21.refs_0_), channel_id=1, source_target_pairs={{0,8},{1,9},{2,10},{3,11},{4,12},{5,13},{6,14},{7,15},{8,0},{9,1},... | collective-permute-start | bytes 1572872 | tf_op jit(solution)/shard_map/ppermute | solution.py:31
  188.0 19.2 %collective-permute-start.33 = (bf16[1024,256]{1,0:T(8,128)(2,1)S(1)}, bf16[1024,256]{1,0:T(8,128)(2,1)S(1)}, u32[]{:S(2)}, u32[]{:S(2)}) collective-permute-start(bf16[1024,256]{1,0:T(8,128)(2,1)S(1)} %collective-permute-done.29.refs_6_), channel_id=1, source_target_pairs={{0,2},{1,3},{2,4},{3,5},{4,6},{5,7},{6,0},{7,1},{8,10},{9,11},{10,... | collective-permute-start | bytes 1572872 | tf_op jit(solution)/shard_map/ppermute | solution.py:31
  188.0 19.2 %collective-permute-start.30 = (bf16[1024,256]{1,0:T(8,128)(2,1)S(1)}, bf16[1024,256]{1,0:T(8,128)(2,1)S(1)}, u32[]{:S(2)}, u32[]{:S(2)}) collective-permute-start(bf16[1024,256]{1,0:T(8,128)(2,1)S(1)} %collective-permute-done.29.refs_6_), channel_id=1, source_target_pairs={{0,6},{1,7},{2,0},{3,1},{4,2},{5,3},{6,4},{7,5},{8,14},{9,15},{10,... | collective-permute-start | bytes 1572872 | tf_op jit(solution)/shard_map/ppermute | solution.py:31
  190.6 16.5 %collective-permute-start.28 = (bf16[1024,128]{1,0:T(8,128)(2,1)S(1)}, bf16[1024,128]{1,0:T(8,128)(2,1)S(1)}, u32[]{:S(2)}, u32[]{:S(2)}) collective-permute-start(bf16[1024,128]{1,0:T(8,128)(2,1)S(1)} %get-tuple-element.23), channel_id=1, source_target_pairs={{0,2},{1,3},{2,4},{3,5},{4,6},{5,7},{6,0},{7,1},{8,10},{9,11},{10,... | collective-permute-start | bytes 786440 | tf_op jit(solution)/shard_map/ppermute | solution.py:31
  190.7 16.5 %collective-permute-start.31 = (bf16[1024,128]{1,0:T(8,128)(2,1)S(1)}, bf16[1024,128]{1,0:T(8,128)(2,1)S(1)}, u32[]{:S(2)}, u32[]{:S(2)}) collective-permute-start(bf16[1024,128]{1,0:T(8,128)(2,1)S(1)} %collective-permute-done.26.refs_2_), channel_id=1, source_target_pairs={{0,8},{1,9},{2,10},{3,11},{4,12},{5,13},{6,14},{7,15},{8,0},{9,1},... | collective-permute-start | bytes 786440 | tf_op jit(solution)/shard_map/ppermute | solution.py:31
  192.7 14.4 %collective-permute-start.32 = (bf16[1024,128]{1,0:T(8,128)(2,1)S(1)}, bf16[1024,128]{1,0:T(8,128)(2,1)S(1)}, u32[]{:S(2)}, u32[]{:S(2)}) collective-permute-start(bf16[1024,128]{1,0:T(8,128)(2,1)S(1)} %collective-permute-done.27.refs_3_), channel_id=1, source_target_pairs={{0,8},{1,9},{2,10},{3,11},{4,12},{5,13},{6,14},{7,15},{8,0},{9,1},... | collective-permute-start | bytes 786440 | tf_op jit(solution)/shard_map/ppermute | solution.py:31
  (25 other events, 226.6 us)
